TPU v7x, 256 devices: a whole 4x4x8 slice. The times are simulated.
256 devices in a mesh: src: 32 (over z, y), tgt: 8 (over x, core).
Axes of the slice: x: 4, y: 4, z: 8, core: 2. Of those that a mesh axis runs over, the one named last changes fastest.
Arguments:
- source: bfloat16 [32768, 300], P('src'), may hold values from -70 to 70
- target: bfloat16 [16384, 300], P('tgt'), may hold values from -11 to 11
- start_map: float32 [300, 300], replicated, may hold values from -1.5 to 1.5
Outputs:
- source_soft: bfloat16 [32768, 300], P(('src', 'tgt'))
- target_soft: bfloat16 [16384, 300], P('tgt')
- polar_map: float32 [300, 300], replicated
All inputs are finite; a program needn't handle non-finite values.
Results may differ from a plain program's by a relative error of at most 0.014.
The roundings to bfloat16 on the way count: a program that leaves them out, or rounds other values in their place, can miss the bound.
Values may be sent and summed in bfloat16 or wider, within the bound.
A program may use at most 64 MiB of HBM per device.

v0:
```python
import math

import jax
import jax.numpy as jnp
from jax import lax
from jax.sharding import PartitionSpec as P

ITERS = 2
NEWTON_STEPS = 8


def polar_steps(covariance):
    highest = lax.Precision.HIGHEST
    current = covariance / jnp.sqrt(jnp.sum(covariance * covariance) + 1e-06)
    for newton in range(NEWTON_STEPS):
        gram_matrix = jnp.dot(current.T, current, precision=highest)
        current = 1.5 * current - 0.5 * jnp.dot(current, gram_matrix, precision=highest)
    return current


def translation_sums(row_weights, col_weights, source, target, share_target, src_index):
    source_sum = lax.psum_scatter(
        jnp.dot(row_weights, target, preferred_element_type=jnp.float32),
        "tgt",
        scatter_dimension=0,
        tiled=True,
    )
    target_full = lax.psum(
        lax.dot_general(
            col_weights, source, (((0,), (0,)), ((), ())), preferred_element_type=jnp.float32
        ),
        "src",
    )
    target_sum = lax.dynamic_slice_in_dim(target_full, src_index * share_target, share_target, 0)
    return (source_sum, target_sum, target_full)


def body(source, target, start_map):
    highest = lax.Precision.HIGHEST
    score_scale = 2.0 / math.sqrt(source.shape[1])
    rows_source = source.shape[0]
    rows_target = target.shape[0]
    src_devices = lax.axis_size("src")
    tgt_devices = lax.axis_size("tgt")
    src_index = lax.axis_index("src")
    tgt_index = lax.axis_index("tgt")
    share_source = rows_source // tgt_devices
    share_target = rows_target // src_devices
    source_piece = lax.dynamic_slice_in_dim(
        source, tgt_index * share_source, share_source, 0
    ).astype(jnp.float32)
    target_piece = lax.dynamic_slice_in_dim(
        target, src_index * share_target, share_target, 0
    ).astype(jnp.float32)
    current = start_map
    source_sum = None
    target_sum = None
    target_full = None
    for iteration in range(ITERS):
        mapped = jnp.dot(
            source, current.astype(jnp.bfloat16), preferred_element_type=jnp.float32
        ).astype(jnp.bfloat16)
        scores = (
            lax.dot_general(
                mapped, target, (((1,), (1,)), ((), ())), preferred_element_type=jnp.float32
            )
            * score_scale
        )
        row_local = jnp.max(scores, axis=1)
        col_local = jnp.max(scores, axis=0)
        row_top = lax.pmax(row_local, "tgt")
        col_top = lax.pmax(col_local, "src")
        row_total = lax.psum(jnp.sum(jnp.exp(scores - row_top[:, None]), axis=1), "tgt")
        col_total = lax.psum(jnp.sum(jnp.exp(scores - col_top[None, :]), axis=0), "src")
        row_weights = (jnp.exp(scores - row_top[:, None]) / row_total[:, None]).astype(jnp.bfloat16)
        col_weights = (jnp.exp(scores - col_top[None, :]) / col_total[None, :]).astype(jnp.bfloat16)
        source_sum, target_sum, target_full = translation_sums(
            row_weights, col_weights, source, target, share_target, src_index
        )
        covariance = jnp.dot(source_piece.T, source_sum, precision=highest)
        covariance = covariance + jnp.dot(target_sum.T, target_piece, precision=highest)
        covariance = lax.psum(covariance, ("src", "tgt"))
        current = polar_steps(covariance)
    source_share = source_sum.astype(jnp.bfloat16)
    target_soft = target_full.astype(jnp.bfloat16)
    return (source_share, target_soft, current)


def solution(mesh):
    in_specs = (P("src", None), P("tgt", None), P())
    out_specs = (P(("src", "tgt"), None), P("tgt", None), P())
    return jax.shard_map(body, mesh=mesh, in_specs=in_specs, out_specs=out_specs, check_vma=False)
```

profile of v0, /device:TPU:2, one launch (start us, length us, event | category | flops | bytes accessed | tf_op | source)
XLA Modules:
  0.0 1263.8 jit_solution(214851185553863919)
XLA Ops:
  8.1 1.2 copy-done
  9.3 7.3 multiply_reduce_fusion.2
  16.6 78.9 %pmax.29 = f32[2048]{0:T(1024)S(1)} all-reduce(f32[2048]{0:T(1024)S(1)} %get-tuple-element.9), channel_id=1, replica_groups=mesh['src'=32,'tgt'=8] {'src'}, use_global_device_ids=true, to_apply=%region_6.0 | all-reduce | flops 2048 | bytes 16384 | tf_op jit(solution)/shard_map/pmax | solution.py:72
  95.5 10.0 pmax.28
  105.6 5.2 fusion.1
  110.8 12.4 psum.56
  123.2 7.0 fusion.6
  130.3 70.6 %psum.57 = f32[2048]{0:T(1024)S(1)} all-reduce(f32[2048]{0:T(1024)S(1)} %get-tuple-element.7), channel_id=1, replica_groups=mesh['src'=32,'tgt'=8] {'src'}, use_global_device_ids=true, to_apply=%region_8.0 | all-reduce | flops 2048 | bytes 16384 | tf_op jit(solution)/shard_map/psum | solution.py:74
  201.0 7.6 fusion.4
  208.7 1.3 fusion.37
  210.0 153.4 %all-reduce.5.cloned.1.call-done = f32[2048,300]{1,0:T(8,128)} async-done(((f32[2048,300]{1,0:T(8,128)}), f32[2048,300]{1,0:T(8,128)}) %all-reduce.5.cloned.1.call-update) | async-done | bytes 2457616 | tf_op jit(solution)/shard_map/psum | solution.py:28
  363.3 2.2 convolution_add_fusion.1
  365.8 248.9 %all-reduce.7.cloned.1.call-done = f32[300,300]{1,0:T(8,128)} async-done(((f32[300,300]{1,0:T(8,128)}), f32[300,300]{1,0:T(8,128)}) %all-reduce.7.cloned.1.call-update) | async-done | bytes 360016 | tf_op jit(solution)/shard_map/psum | solution.py:82
  614.7 1.7 multiply_reduce_fusion.5
  617.1 2.4 fusion.29
  619.5 2.2 fusion.25
  621.7 1.2 fusion.49
  624.0 1.2 fusion.50
  626.3 1.2 fusion.51
  628.6 1.2 fusion.52
  630.9 1.7 fusion.53
  633.6 1.2 fusion.54
  638.2 5.3 multiply_reduce_fusion
  643.5 72.1 %pmax.31 = f32[2048]{0:T(1024)S(1)} all-reduce(f32[2048]{0:T(1024)S(1)} %get-tuple-element.5), channel_id=1, replica_groups=mesh['src'=32,'tgt'=8] {'src'}, use_global_device_ids=true, to_apply=%region_18.0 | all-reduce | flops 2048 | bytes 16384 | tf_op jit(solution)/shard_map/pmax | solution.py:72
  715.6 10.0 pmax.30
  725.6 5.2 fusion.3
  730.9 12.6 %psum.60 = f32[1024]{0:T(1024)S(1)} all-reduce(f32[1024]{0:T(1024)S(1)} %get-tuple-element.4), channel_id=1, replica_groups=mesh['src'=32,'tgt'=8] {'tgt'}, use_global_device_ids=true, to_apply=%region_15.0 | all-reduce | flops 1024 | bytes 8192 | tf_op jit(solution)/shard_map/psum | solution.py:73
  743.5 6.4 fusion.7
  750.0 70.8 %psum.61 = f32[2048]{0:T(1024)S(1)} all-reduce(f32[2048]{0:T(1024)S(1)} %get-tuple-element.3), channel_id=1, replica_groups=mesh['src'=32,'tgt'=8] {'src'}, use_global_device_ids=true, to_apply=%region_20.0 | all-reduce | flops 2048 | bytes 16384 | tf_op jit(solution)/shard_map/psum | solution.py:74
  820.8 6.8 fusion.5
  828.0 1.3 fusion.35
  829.2 151.9 %all-reduce.9.cloned.1.call-done = f32[2048,300]{0,1:T(8,128)} async-done(((f32[2048,300]{0,1:T(8,128)}), f32[2048,300]{0,1:T(8,128)}) %all-reduce.9.cloned.1.call-update) | async-done | bytes 2457616 | tf_op jit(solution)/shard_map/psum | solution.py:28
  981.1 2.1 convolution_add_fusion
  983.2 1.6 convert_element_type.40
  984.8 2.9 convert_element_type.42
  987.7 244.7 %all-reduce.11.cloned.1.call-done = f32[300,300]{1,0:T(8,128)} async-done(((f32[300,300]{1,0:T(8,128)}), f32[300,300]{1,0:T(8,128)}) %all-reduce.11.cloned.1.call-update) | async-done | bytes 360016 | tf_op jit(solution)/shard_map/psum | solution.py:82
  1232.4 1.7 multiply_reduce_fusion.4
  1234.8 2.4 fusion.30
  1237.2 2.2 fusion.17
  1239.4 1.2 fusion.56
  1241.7 1.2 fusion.57
  1244.0 1.2 fusion.58
  1246.3 1.2 fusion.59
  1247.6 1.3 fusion.13
  1248.8 1.2 fusion.60
  1251.1 1.2 fusion.61
  1253.4 1.2 fusion.62
  1254.6 1.8 fusion.10
  (30 shorter events, 14.5 us)
Async XLA Ops:
  8.0 1.3 copy-start
  8.0 200.7 %reduce-scatter.3.cloned.1.call-start = ((), (), s32[]{:S(2)}) async-start(), calls=%async_computation.2 | async-start | bytes 1769472 | tf_op jit(solution)/shard_map/reduce_scatter | solution.py:22
  123.2 77.8 %copy-start.1 = (bf16[1024,300]{0,1:T(8,128)(2,1)S(1)}, bf16[1024,300]{0,1:T(8,128)(2,1)}, u32[]{:S(2)}) copy-start(bf16[1024,300]{0,1:T(8,128)(2,1)} %param.3) | copy-start | bytes 1843204
  130.3 233.1 %all-reduce.5.cloned.1.call-start = ((), (), s32[]{:S(2)}) async-start(), calls=%async_computation.3 | async-start | bytes 6291456 | tf_op jit(solution)/shard_map/psum | solution.py:28
  208.6 406.1 %all-reduce.7.cloned.1.call-start = ((), (), s32[]{:S(2)}) async-start(), calls=%async_computation.4 | async-start | bytes 933888 | tf_op jit(solution)/shard_map/psum | solution.py:82
  365.5 462.4 %reduce-scatter.5.cloned.1.call-start = ((), (), s32[]{:S(2)}) async-start(), calls=%async_computation.5 | async-start | bytes 1400832 | tf_op jit(solution)/shard_map/reduce_scatter | solution.py:22
  749.9 231.1 %all-reduce.9.cloned.1.call-start = ((), (), s32[]{:S(2)}) async-start(), calls=%async_computation.6 | async-start | bytes 4980736 | tf_op jit(solution)/shard_map/psum | solution.py:28
  827.7 404.7 %all-reduce.11.cloned.1.call-start = ((), (), s32[]{:S(2)}) async-start(), calls=%async_computation.7 | async-start | bytes 933888 | tf_op jit(solution)/shard_map/psum | solution.py:82
Sparse Core Ops, SparseCore 0:
  130.4 26.5 reduce-scatter.2
  365.6 248.9 all-reduce.6
  750.1 27.8 reduce-scatter.4
  983.3 249.0 all-reduce.10
Sparse Core Ops, SparseCore 1:
  208.7 154.6 all-reduce.4
  827.8 153.2 all-reduce.8
where the time goes:
time: 1270 us; the launch traced here: 1260 us
  waiting for transfers between devices  799 us (63%)
  blocking collectives  338 us (27%)
  matrix products  89.8 us (7%)
  other arithmetic  18.4 us (1%)
  between operations  17.2 us (1%)
    psum x2, waiting for transfers between devices, body(): covariance = lax.psum(covariance, ('src', 'tgt'))  494 us
    psum x2, waiting for transfers between devices, translation_sums(): lax.psum(lax.dot_general(col_weights, source, (((0,), (0,)), ((), ())), p...  305 us
    pmax x2, blocking collectives, body(): col_top = lax.pmax(col_local, 'src')  151 us
    psum x2, blocking collectives, body(): lax.psum(jnp.sum(jnp.exp(scores - col_top[None, :]), axis=0), 'src')  141 us
  transfers between devices with their start and end apart: 6, of which 4 were waited for; matrix products, arithmetic and copies ran while one was open for 2% of the time, Pallas kernels for 0%

commit v1 on v0

v1 whole, which is shorter than its diff:
```python
import math

import jax
import jax.numpy as jnp
from jax import lax
from jax.sharding import PartitionSpec as P

ITERS = 2
NEWTON_STEPS = 8


def polar_steps(covariance):
    highest = lax.Precision.HIGHEST
    current = covariance / jnp.sqrt(jnp.sum(covariance * covariance) + 1e-06)
    for newton in range(NEWTON_STEPS):
        gram_matrix = jnp.dot(current.T, current, precision=highest)
        current = 1.5 * current - 0.5 * jnp.dot(current, gram_matrix, precision=highest)
    return current


def merge_stats(top, total, axis):
    gathered = lax.all_gather(jnp.stack([top, total]), axis)
    tops, totals = gathered[:, 0], gathered[:, 1]
    best = jnp.max(tops, axis=0)
    return best, jnp.sum(totals * jnp.exp(tops - best[None]), axis=0)


def body(source, target, start_map):
    highest = lax.Precision.HIGHEST
    score_scale = 2.0 / math.sqrt(source.shape[1])
    source_f32 = source.astype(jnp.float32)
    target_f32 = target.astype(jnp.float32)
    current = start_map
    for iteration in range(ITERS):
        mapped = jnp.dot(
            source, current.astype(jnp.bfloat16), preferred_element_type=jnp.float32
        ).astype(jnp.bfloat16)
        scores = (
            lax.dot_general(
                mapped, target, (((1,), (1,)), ((), ())), preferred_element_type=jnp.float32
            )
            * score_scale
        )
        row_local = jnp.max(scores, axis=1)
        col_local = jnp.max(scores, axis=0)
        row_part = jnp.sum(jnp.exp(scores - row_local[:, None]), axis=1)
        col_part = jnp.sum(jnp.exp(scores - col_local[None, :]), axis=0)
        row_top, row_total = merge_stats(row_local, row_part, "tgt")
        col_top, col_total = merge_stats(col_local, col_part, "src")
        row_weights = (jnp.exp(scores - row_top[:, None]) / row_total[:, None]).astype(jnp.bfloat16)
        col_weights = (jnp.exp(scores - col_top[None, :]) / col_total[None, :]).astype(jnp.bfloat16)
        source_part = jnp.dot(row_weights, target, preferred_element_type=jnp.float32)
        target_part = lax.dot_general(
            col_weights, source, (((0,), (0,)), ((), ())), preferred_element_type=jnp.float32
        )
        covariance = jnp.dot(source_f32.T, source_part, precision=highest)
        covariance = covariance + jnp.dot(target_part.T, target_f32, precision=highest)
        covariance = lax.psum(covariance, ("src", "tgt"))
        if iteration == ITERS - 1:
            source_soft = lax.psum_scatter(
                source_part, "tgt", scatter_dimension=0, tiled=True
            ).astype(jnp.bfloat16)
            target_soft = lax.psum(target_part, "src").astype(jnp.bfloat16)
        current = polar_steps(covariance)
    return (source_soft, target_soft, current)


def solution(mesh):
    in_specs = (P("src", None), P("tgt", None), P())
    out_specs = (P(("src", "tgt"), None), P("tgt", None), P())
    return jax.shard_map(body, mesh=mesh, in_specs=in_specs, out_specs=out_specs, check_vma=False)
```

time: 1270 us -> 771 us (0.61)
  waiting for transfers between devices: 799 us -> 338 us
  blocking collectives: 338 us -> 294 us
    psum x2 -> x0, waiting for transfers between devices: 305 us -> none  [translation_sums(): lax.psum(lax.dot_general(col_weights, source, (((0,), (0,)), ((), ())), p...]
    pmax x4 -> x0, blocking collectives: 171 us -> none  [the longest x2 151 us: body(): col_top = lax.pmax(col_local, 'src')]
    psum x2, waiting for transfers between devices: 494 us -> 331 us  [body(): covariance = lax.psum(covariance, ('src', 'tgt'))]
    all_gather x0 -> x4, blocking collectives: none -> 126 us  [merge_stats(): gathered = lax.all_gather(jnp.stack([top, total]), axis)]
    psum x4 -> x1, blocking collectives: 167 us -> 168 us  [body(): target_soft = lax.psum(target_part, 'src').astype(jnp.bfloat16)]
  transfers between devices with their start and end apart: 6 -> 3, of which waited for: 4 -> 3; matrix products, arithmetic and copies ran while one was open for 2% -> 3% of each run, Pallas kernels for 0% -> 0%
where the time goes in v1:
time: 771 us; the launch traced here: 760 us
  waiting for transfers between devices  338 us (44%)
  blocking collectives  294 us (38%)
  matrix products  88.1 us (11%)
  other arithmetic  19.2 us (2%)
  between operations  16 us (2%)
    psum x2, waiting for transfers between devices, body(): covariance = lax.psum(covariance, ('src', 'tgt'))  331 us
    psum x1, blocking collectives, body(): target_soft = lax.psum(target_part, 'src').astype(jnp.bfloat16)  168 us
    all_gather x4, blocking collectives, merge_stats(): gathered = lax.all_gather(jnp.stack([top, total]), axis)  126 us
    dot_general x16, matrix products, polar_steps(): gram_matrix = jnp.dot(current.T, current, precision=highest)  30.9 us
    dot_general x16, matrix products, polar_steps(): jnp.dot(current, gram_matrix, precision=highest)  22.2 us
  transfers between devices with their start and end apart: 3, of which 3 were waited for; matrix products, arithmetic and copies ran while one was open for 3% of the time, Pallas kernels for 0%

profile of v1, /device:TPU:2, one launch (start us, length us, event | category | flops | bytes accessed | tf_op | source)
XLA Modules:
  0.0 759.6 jit_solution(12833689186775290613)
XLA Ops:
  7.2 1.2 copy-done
  8.5 7.3 multiply_reduce_fusion.3
  15.8 5.1 exponential_reduce_fusion.3
  21.6 1.4 exponential_reduce_fusion.2
  23.0 52.8 %all-gather.5 = f32[32,2,2048]{2,1,0:T(2,128)S(1)} all-gather(f32[1,2,2048]{2,1,0:T(2,128)S(1)} %maximum_bitcast_fusion), channel_id=3, replica_groups=mesh['src'=32,'tgt'=8] {'src'}, dimensions={0}, use_global_device_ids=true | all-gather | bytes 540672 | tf_op jit(solution)/shard_map/all_gather | solution.py:22
  76.5 2.5 fusion
  78.9 2.2 fusion.46
  81.2 13.1 %all-gather.4 = f32[8,2,1024]{2,1,0:T(2,128)S(1)} all-gather(f32[1,2,1024]{2,1,0:T(2,128)S(1)} %maximum_bitcast_fusion.2), channel_id=2, replica_groups=mesh['src'=32,'tgt'=8] {'tgt'}, dimensions={0}, use_global_device_ids=true | all-gather | bytes 73728 | tf_op jit(solution)/shard_map/all_gather | solution.py:22
  94.4 2.5 fusion.2
  96.9 3.4 fusion.22
  100.4 249.3 %all-reduce.4.cloned.1.call-done = f32[300,300]{0,1:T(8,128)} async-done(((f32[300,300]{0,1:T(8,128)}), f32[300,300]{0,1:T(8,128)}) %all-reduce.4.cloned.1.call-update) | async-done | bytes 360016 | tf_op jit(solution)/shard_map/psum | solution.py:58
  349.8 1.7 multiply_reduce_fusion.5
  352.2 2.2 fusion.32
  354.5 2.4 fusion.21
  356.9 1.0 fusion.47
  357.9 1.2 fusion.20
  360.2 1.3 fusion.19
  361.5 1.0 fusion.49
  362.5 1.2 fusion.18
  364.8 1.3 fusion.17
  366.1 12.7 %fusion.51 = f32[300,300]{1,0:T(8,128)S(1)} fusion(f32[300,300]{0,1:T(8,128)S(1)} %fusion.17), kind=kOutput, calls=%fused_computation.101 | convolution fusion | flops 324000000 | bytes 720000 | tf_op jit(solution)/shard_map/dot_general | solution.py:16
  378.8 1.2 fusion.16
  381.1 1.3 fusion.15
  383.4 1.2 fusion.23
  384.6 5.3 multiply_reduce_fusion
  389.9 6.0 exponential_reduce_fusion
  395.9 12.5 %all-gather.6 = f32[8,2,1024]{2,1,0:T(2,128)S(1)} all-gather(f32[1,2,1024]{2,1,0:T(2,128)S(1)} %maximum_bitcast_fusion.3), channel_id=4, replica_groups=mesh['src'=32,'tgt'=8] {'tgt'}, dimensions={0}, use_global_device_ids=true | all-gather | bytes 73728 | tf_op jit(solution)/shard_map/all_gather | solution.py:22
  408.5 3.2 fusion.3
  411.8 1.1 convolution_bitcast_fusion
  412.9 47.8 %all-gather.7 = f32[32,2,2048]{2,1,0:T(2,128)S(1)} all-gather(f32[1,2,2048]{2,1,0:T(2,128)S(1)} %maximum_bitcast_fusion.1), channel_id=5, replica_groups=mesh['src'=32,'tgt'=8] {'src'}, dimensions={0}, use_global_device_ids=true | all-gather | bytes 540672 | tf_op jit(solution)/shard_map/all_gather | solution.py:22
  461.4 4.5 fusion.1
  466.0 1.4 copy-done.2
  467.4 2.9 convolution_add_fusion
  470.4 167.5 %all-reduce.7 = bf16[2048,300]{0,1:T(8,128)(2,1)} all-reduce(f32[2048,300]{0,1:T(8,128)} %copy-done.2), channel_id=1, replica_groups=mesh['src'=32,'tgt'=8] {'src'}, use_global_device_ids=true, to_apply=%region_19.0 | all-reduce | flops 614400 | bytes 3686400 | tf_op jit(solution)/shard_map/psum | solution.py:63
  638.0 81.9 %all-reduce.6.cloned.1.call-done = f32[300,300]{0,1:T(8,128)} async-done(((f32[300,300]{0,1:T(8,128)}), f32[300,300]{0,1:T(8,128)}) %all-reduce.6.cloned.1.call-update) | async-done | bytes 360016 | tf_op jit(solution)/shard_map/psum | solution.py:58
  719.9 1.7 multiply_reduce_fusion.4
  722.3 2.2 fusion.33
  724.5 2.4 fusion.13
  728.0 1.2 fusion.12
  730.3 1.3 fusion.11
  732.6 1.2 fusion.10
  734.8 1.3 fusion.9
  736.1 1.3 fusion.58
  737.4 1.2 fusion.8
  739.7 1.3 fusion.7
  742.0 1.2 fusion.6
  744.2 6.8 reduce-scatter.2.cloned.1.call-done
  751.1 1.6 convert_element_type.40
  (39 shorter events, 13.8 us)
Async XLA Ops:
  7.2 1.3 copy-start
  7.2 342.6 %all-reduce.4.cloned.1.call-start = ((), (), s32[]{:S(2)}) async-start(), calls=%async_computation.1 | async-start | bytes 933888 | tf_op jit(solution)/shard_map/psum | solution.py:58
  15.8 5.8 copy-start.1
  15.8 60.7 %copy-start.4 = (bf16[1024,300]{0,1:T(8,128)(2,1)S(1)}, bf16[1024,300]{0,1:T(8,128)(2,1)}, u32[]{:S(2)}) copy-start(bf16[1024,300]{0,1:T(8,128)(2,1)} %param.3) | copy-start | bytes 1843204
  100.4 619.5 %all-reduce.6.cloned.1.call-start = ((), (), s32[]{:S(2)}) async-start(), calls=%async_computation.3 | async-start | bytes 933888 | tf_op jit(solution)/shard_map/psum | solution.py:58
  389.9 18.6 %copy-start.3 = (f32[1024,2048]{1,0:T(8,128)S(1)}, f32[1024,2048]{1,0:T(8,128)}, u32[]{:S(2)}) copy-start(f32[1024,2048]{1,0:T(8,128)} %get-tuple-element.29) | copy-start | bytes 25165828
  411.8 54.2 %copy-start.5 = (f32[1024,300]{0,1:T(8,128)}, f32[1024,300]{0,1:T(8,128)S(1)}, u32[]{:S(2)}) copy-start(f32[1024,300]{0,1:T(8,128)S(1)} %fusion.3) | copy-start | bytes 3686404
  466.0 1.4 copy-start.2
  470.4 280.7 %reduce-scatter.2.cloned.1.call-start = ((), (), s32[]{:S(2)}) async-start(), calls=%async_computation.2 | async-start | bytes 1400832 | tf_op jit(solution)/shard_map/reduce_scatter | solution.py:60
Sparse Core Ops, SparseCore 0:
  100.5 249.2 all-reduce.3
  470.5 249.3 all-reduce.5
  722.4 28.6 reduce-scatter.1

commit v2 on v1

--- a/solution.py
+++ b/solution.py
@@ -1,9 +1,15 @@
 import math
+
+import functools
 
 import jax
 import jax.numpy as jnp
 from jax import lax
+from jax.experimental import pallas as pl
+from jax.experimental.pallas import tpu as pltpu
 from jax.sharding import PartitionSpec as P
+
+MESH = pl.DeviceIdType.MESH
 
 ITERS = 2
 NEWTON_STEPS = 8
@@ -16,6 +22,90 @@
         gram_matrix = jnp.dot(current.T, current, precision=highest)
         current = 1.5 * current - 0.5 * jnp.dot(current, gram_matrix, precision=highest)
     return current
+
+
+def all_reduce_kernel(n_src, n_tgt, x_ref, out_ref, gather_src, gather_tgt,
+                      send_a, recv_a, send_b, recv_b, send_c, recv_c):
+    me_s = lax.axis_index("src")
+    me_t = lax.axis_index("tgt")
+
+    def copy(src, dst, send, recv, device):
+        return pltpu.make_async_remote_copy(
+            src_ref=src, dst_ref=dst, send_sem=send, recv_sem=recv,
+            device_id=device, device_id_type=MESH)
+
+    def start_a(d, carry):
+        k = lax.rem(me_s + d, n_src)
+        copy(x_ref.at[k], gather_src.at[me_s], send_a.at[k], recv_a.at[me_s], (k, me_t)).start()
+        return carry
+    lax.fori_loop(1, n_src, start_a, 0)
+    gather_src[me_s] = x_ref[me_s]
+
+    def wait_a(d, carry):
+        k = lax.rem(me_s + d, n_src)
+        copy(x_ref.at[k], gather_src.at[me_s], send_a.at[k], recv_a.at[me_s], (k, me_t)).wait_send()
+        j = lax.rem(me_s + n_src - d, n_src)
+        copy(x_ref.at[j], gather_src.at[j], send_a.at[j], recv_a.at[j], (j, me_t)).wait_recv()
+        return carry
+    lax.fori_loop(1, n_src, wait_a, 0)
+    gather_tgt[me_t] = jnp.sum(gather_src[...], axis=0)
+
+    def start_b(d, carry):
+        k = lax.rem(me_t + d, n_tgt)
+        copy(gather_tgt.at[me_t], gather_tgt.at[me_t], send_b.at[k], recv_b.at[me_t], (me_s, k)).start()
+        return carry
+    lax.fori_loop(1, n_tgt, start_b, 0)
+
+    def wait_b(d, carry):
+        k = lax.rem(me_t + d, n_tgt)
+        copy(gather_tgt.at[me_t], gather_tgt.at[me_t], send_b.at[k], recv_b.at[me_t], (me_s, k)).wait_send()
+        j = lax.rem(me_t + n_tgt - d, n_tgt)
+        copy(gather_tgt.at[j], gather_tgt.at[j], send_b.at[j], recv_b.at[j], (me_s, j)).wait_recv()
+        return carry
+    lax.fori_loop(1, n_tgt, wait_b, 0)
+    out_ref[me_s] = jnp.sum(gather_tgt[...], axis=0)
+
+    def start_c(d, carry):
+        k = lax.rem(me_s + d, n_src)
+        copy(out_ref.at[me_s], out_ref.at[me_s], send_c.at[k], recv_c.at[me_s], (k, me_t)).start()
+        return carry
+    lax.fori_loop(1, n_src, start_c, 0)
+
+    def wait_c(d, carry):
+        k = lax.rem(me_s + d, n_src)
+        copy(out_ref.at[me_s], out_ref.at[me_s], send_c.at[k], recv_c.at[me_s], (k, me_t)).wait_send()
+        j = lax.rem(me_s + n_src - d, n_src)
+        copy(out_ref.at[j], out_ref.at[j], send_c.at[j], recv_c.at[j], (j, me_t)).wait_recv()
+        return carry
+    lax.fori_loop(1, n_src, wait_c, 0)
+
+
+def all_reduce(matrix):
+    n_src = lax.axis_size("src")
+    n_tgt = lax.axis_size("tgt")
+    size = matrix.size
+    lines = -(-size // 128)
+    rows = -(-lines // (n_src * 8)) * 8
+    flat = jnp.pad(matrix.reshape(-1), (0, n_src * rows * 128 - size)).reshape(n_src, rows, 128)
+    vmem = pl.BlockSpec(memory_space=pltpu.VMEM)
+    out = pl.pallas_call(
+        functools.partial(all_reduce_kernel, n_src, n_tgt),
+        out_shape=jax.ShapeDtypeStruct(flat.shape, jnp.float32),
+        in_specs=[vmem],
+        out_specs=vmem,
+        scratch_shapes=[
+            pltpu.VMEM((n_src, rows, 128), jnp.float32),
+            pltpu.VMEM((n_tgt, rows, 128), jnp.float32),
+            pltpu.SemaphoreType.DMA((n_src,)),
+            pltpu.SemaphoreType.DMA((n_src,)),
+            pltpu.SemaphoreType.DMA((n_tgt,)),
+            pltpu.SemaphoreType.DMA((n_tgt,)),
+            pltpu.SemaphoreType.DMA((n_src,)),
+            pltpu.SemaphoreType.DMA((n_src,)),
+        ],
+        compiler_params=pltpu.CompilerParams(has_side_effects=True),
+    )(flat)
+    return out.reshape(-1)[:size].reshape(matrix.shape)
 
 
 def merge_stats(top, total, axis):
@@ -55,7 +145,7 @@
         )
         covariance = jnp.dot(source_f32.T, source_part, precision=highest)
         covariance = covariance + jnp.dot(target_part.T, target_f32, precision=highest)
-        covariance = lax.psum(covariance, ("src", "tgt"))
+        covariance = all_reduce(covariance)
         if iteration == ITERS - 1:
             source_soft = lax.psum_scatter(
                 source_part, "tgt", scatter_dimension=0, tiled=True

time: 771 us -> 499 us (0.65)
  waiting for transfers between devices: 338 us -> 0.02 us
  Pallas kernels: 0 us -> 82.9 us
  matrix products: 88.1 us -> 71.9 us
    psum x2 -> x0, waiting for transfers between devices: 331 us -> none  [body(): covariance = lax.psum(covariance, ('src', 'tgt'))]
    pallas_call x0 -> x2, Pallas kernels: none -> 82.9 us  [all_reduce(): pl.pallas_call(functools.partial(all_reduce_kernel, n_src, n_tgt), out_sh...]
    dot_general x16, matrix products: 30.9 us -> 19.7 us  [polar_steps(): gram_matrix = jnp.dot(current.T, current, precision=highest)]
  transfers between devices with their start and end apart: 3 -> 1, of which waited for: 3 -> 0; matrix products, arithmetic and copies ran while one was open for 3% -> 7% of each run, Pallas kernels for 0% -> 8%
where the time goes in v2:
time: 499 us; the launch traced here: 493 us
  blocking collectives  295 us (59%)
  Pallas kernels  82.9 us (17%)
  matrix products  71.9 us (14%)
  other arithmetic  20.5 us (4%)
  between operations  16.1 us (3%)
  local copies, waits for them, and re-layouts  6.5 us (1%)
    psum x1, blocking collectives, body(): target_soft = lax.psum(target_part, 'src').astype(jnp.bfloat16)  168 us
    all_gather x4, blocking collectives, merge_stats(): gathered = lax.all_gather(jnp.stack([top, total]), axis)  128 us
    pallas_call x2, Pallas kernels, all_reduce(): pl.pallas_call(functools.partial(all_reduce_kernel, n_src, n_tgt), out_sh...  82.9 us
    dot_general x16, matrix products, polar_steps(): gram_matrix = jnp.dot(current.T, current, precision=highest)  19.7 us
    dot_general x16, matrix products, polar_steps(): jnp.dot(current, gram_matrix, precision=highest)  17.9 us
    dot_general x2, matrix products, body(): lax.dot_general(mapped, target, (((1,), (1,)), ((), ())), preferred_eleme...  12.7 us
    reduce_sum x2, other arithmetic, body(): col_part = jnp.sum(jnp.exp(scores - col_local[None, :]), axis=0)  12 us
  transfers between devices with their start and end apart: 1, of which 0 were waited for; matrix products, arithmetic and copies ran while one was open for 7% of the time, Pallas kernels for 8%

profile of v2, /device:TPU:2, one launch (start us, length us, event | category | flops | bytes accessed | tf_op | source)
XLA Modules:
  0.0 493.3 jit_solution(7052340297209008590)
XLA Ops:
  7.2 1.2 copy-done
  8.5 7.4 %multiply_reduce_fusion.2 = (f32[2048]{0:T(1024)S(1)}, f32[1024]{0:T(1024)S(1)}, f32[1024,2048]{1,0:T(8,128)}) fusion(bf16[2048,300]{0,1:T(8,128)(2,1)S(1)} %copy-done, bf16[1024,300]{0,1:T(8,128)(2,1)} %param.3, f32[300,300]{1,0:T(8,128)} %param.5), kind=kOutput, calls=%fused_computation.10 | convolution fusion | flops 1449296768 | bytes 10604096 | tf_op jit(solution)/shard_map/dot_general | solution.py:129
  15.8 6.0 %exponential_reduce_fusion.2 = (f32[2048]{0:T(1024)S(1)}, f32[1024]{0:T(1024)S(1)}) fusion(f32[1024,2048]{1,0:T(8,128)} %get-tuple-element.23, f32[2048]{0:T(1024)S(1)} %get-tuple-element.9, f32[1024]{0:T(1024)S(1)} %get-tuple-element.10), kind=kLoop, calls=%fused_computation.5 | loop fusion | flops 10482688 | bytes 8413184 | tf_op jit(solution)/shard_map/reduce_sum | solution.py:137
  21.8 12.8 %all-gather.4 = f32[8,2,1024]{2,1,0:T(2,128)S(1)} all-gather(f32[1,2,1024]{2,1,0:T(2,128)S(1)} %maximum_bitcast_fusion.2), channel_id=2, replica_groups=mesh['src'=32,'tgt'=8] {'tgt'}, dimensions={0}, use_global_device_ids=true | all-gather | bytes 73728 | tf_op jit(solution)/shard_map/all_gather | solution.py:112
  34.8 3.2 fusion.2
  38.0 1.1 convolution_bitcast_fusion.1
  39.2 53.1 %all-gather.5 = f32[32,2,2048]{2,1,0:T(2,128)S(1)} all-gather(f32[1,2,2048]{2,1,0:T(2,128)S(1)} %maximum_bitcast_fusion), channel_id=3, replica_groups=mesh['src'=32,'tgt'=8] {'src'}, dimensions={0}, use_global_device_ids=true | all-gather | bytes 540672 | tf_op jit(solution)/shard_map/all_gather | solution.py:112
  93.0 2.2 fusion
  95.1 2.1 convolution_add_fusion.1
  98.7 41.3 %shard_map.58 = f32[32,24,128]{2,1,0:T(8,128)} custom-call(f32[32,24,128]{2,1,0:T(8,128)} %bitcast.158), custom_call_target="tpu_custom_call" | custom-call | tf_op jit(solution)/shard_map/pallas_call | solution.py:91
  140.0 1.7 multiply_reduce_fusion.5
  143.9 1.2 fusion.43
  145.1 1.0 fusion.21
  146.2 1.2 fusion.44
  148.5 1.2 fusion.45
  149.7 1.0 fusion.19
  150.8 1.2 fusion.46
  153.1 1.2 fusion.47
  154.3 1.3 fusion.17
  155.6 1.2 fusion.48
  157.9 1.2 fusion.49
  160.2 1.2 fusion.50
  161.4 1.1 fusion.22
  162.5 5.3 %multiply_reduce_fusion = (f32[2048]{0:T(1024)S(1)}, f32[1024]{0:T(1024)S(1)}, f32[1024,2048]{1,0:T(8,128)}) fusion(bf16[2048,300]{0,1:T(8,128)(2,1)S(1)} %copy-done, bf16[300,300]{1,0:T(8,128)(2,1)S(1)} %fusion.22, bf16[1024,300]{0,1:T(8,128)(2,1)S(1)} %copy-done.4), kind=kOutput, calls=%fused_computation.8 | convolution fusion | flops 1449206784 | bytes 10424096 | tf_op jit(solution)/shard_map/dot_general | solution.py:129
  167.8 6.0 %exponential_reduce_fusion = (f32[2048]{0:T(1024)S(1)}, f32[1024]{0:T(1024)S(1)}) fusion(f32[1024,2048]{1,0:T(8,128)} %get-tuple-element.24, f32[2048]{0:T(1024)S(1)} %get-tuple-element.5, f32[1024]{0:T(1024)S(1)} %get-tuple-element.6), kind=kLoop, calls=%fused_computation.1 | loop fusion | flops 10482688 | bytes 8413184 | tf_op jit(solution)/shard_map/reduce_sum | solution.py:137
  173.9 12.1 %all-gather.6 = f32[8,2,1024]{2,1,0:T(2,128)S(1)} all-gather(f32[1,2,1024]{2,1,0:T(2,128)S(1)} %maximum_bitcast_fusion.3), channel_id=4, replica_groups=mesh['src'=32,'tgt'=8] {'tgt'}, dimensions={0}, use_global_device_ids=true | all-gather | bytes 73728 | tf_op jit(solution)/shard_map/all_gather | solution.py:112
  186.1 3.8 fusion.3
  190.0 2.4 convolution_bitcast_fusion
  192.4 49.6 %all-gather.7 = f32[32,2,2048]{2,1,0:T(2,128)S(1)} all-gather(f32[1,2,2048]{2,1,0:T(2,128)S(1)} %maximum_bitcast_fusion.1), channel_id=5, replica_groups=mesh['src'=32,'tgt'=8] {'src'}, dimensions={0}, use_global_device_ids=true | all-gather | bytes 540672 | tf_op jit(solution)/shard_map/all_gather | solution.py:112
  242.7 4.5 fusion.1
  247.2 1.4 copy-done.1
  248.7 2.1 convolution_add_fusion
  252.2 41.6 %shard_map.59 = f32[32,24,128]{2,1,0:T(8,128)} custom-call(f32[32,24,128]{2,1,0:T(8,128)} %bitcast.157), custom_call_target="tpu_custom_call" | custom-call | tf_op jit(solution)/shard_map/pallas_call | solution.py:91
  293.9 1.7 multiply_reduce_fusion.4
  297.7 1.2 fusion.51
  299.0 1.0 fusion.13
  300.0 1.2 fusion.52
  302.3 1.2 fusion.53
  304.6 1.2 fusion.54
  306.9 1.2 fusion.55
  308.1 1.3 fusion.9
  309.4 1.2 fusion.56
  311.7 1.2 fusion.57
  312.9 1.0 fusion.7
  314.0 1.2 fusion.58
  315.2 1.8 fusion.6
  317.0 167.6 %all-reduce.3 = bf16[2048,300]{0,1:T(8,128)(2,1)} all-reduce(f32[2048,300]{0,1:T(8,128)} %copy-done.1), channel_id=1, replica_groups=mesh['src'=32,'tgt'=8] {'src'}, use_global_device_ids=true, to_apply=%region_18.19 | all-reduce | flops 614400 | bytes 3686400 | tf_op jit(solution)/shard_map/psum | solution.py:153
  484.6 1.6 convert_element_type.43
  (41 shorter events, 15.8 us)
Async XLA Ops:
  7.2 1.3 copy-start
  7.2 477.5 %reduce-scatter.2.cloned.1.call-start = ((), (), s32[]{:S(2)}) async-start(), calls=%async_computation.1 | async-start | bytes 1400832 | tf_op jit(solution)/shard_map/reduce_scatter | solution.py:150
  15.8 18.9 %copy-start.3 = (f32[1024,2048]{1,0:T(8,128)S(1)}, f32[1024,2048]{1,0:T(8,128)}, u32[]{:S(2)}) copy-start(f32[1024,2048]{1,0:T(8,128)} %get-tuple-element.23) | copy-start | bytes 25165828
  34.8 3.3 copy-start.4
  167.8 18.3 %copy-start.2 = (f32[1024,2048]{1,0:T(8,128)S(1)}, f32[1024,2048]{1,0:T(8,128)}, u32[]{:S(2)}) copy-start(f32[1024,2048]{1,0:T(8,128)} %get-tuple-element.24) | copy-start | bytes 25165828
  247.2 1.4 copy-start.1
Sparse Core Ops, SparseCore 0:
  190.1 31.4 reduce-scatter.1

commit v3 on v2

--- a/solution.py
+++ b/solution.py
@@ -108,11 +108,140 @@
     return out.reshape(-1)[:size].reshape(matrix.shape)
 
 
-def merge_stats(top, total, axis):
-    gathered = lax.all_gather(jnp.stack([top, total]), axis)
+def src_sum_kernel(n_src, x_ref, out_ref, gather, send_a, recv_a, send_c, recv_c):
+    me_s = lax.axis_index("src")
+    me_t = lax.axis_index("tgt")
+
+    def copy(src, dst, send, recv, device):
+        return pltpu.make_async_remote_copy(
+            src_ref=src, dst_ref=dst, send_sem=send, recv_sem=recv,
+            device_id=device, device_id_type=MESH)
+
+    def start_a(d, carry):
+        k = lax.rem(me_s + d, n_src)
+        copy(x_ref.at[k], gather.at[me_s], send_a.at[k], recv_a.at[me_s], (k, me_t)).start()
+        return carry
+    lax.fori_loop(1, n_src, start_a, 0)
+    gather[me_s] = x_ref[me_s]
+
+    def wait_a(d, carry):
+        k = lax.rem(me_s + d, n_src)
+        copy(x_ref.at[k], gather.at[me_s], send_a.at[k], recv_a.at[me_s], (k, me_t)).wait_send()
+        j = lax.rem(me_s + n_src - d, n_src)
+        copy(x_ref.at[j], gather.at[j], send_a.at[j], recv_a.at[j], (j, me_t)).wait_recv()
+        return carry
+    lax.fori_loop(1, n_src, wait_a, 0)
+    out_ref[me_s] = jnp.sum(gather[...], axis=0).astype(out_ref.dtype)
+
+    def start_c(d, carry):
+        k = lax.rem(me_s + d, n_src)
+        copy(out_ref.at[me_s], out_ref.at[me_s], send_c.at[k], recv_c.at[me_s], (k, me_t)).start()
+        return carry
+    lax.fori_loop(1, n_src, start_c, 0)
+
+    def wait_c(d, carry):
+        k = lax.rem(me_s + d, n_src)
+        copy(out_ref.at[me_s], out_ref.at[me_s], send_c.at[k], recv_c.at[me_s], (k, me_t)).wait_send()
+        j = lax.rem(me_s + n_src - d, n_src)
+        copy(out_ref.at[j], out_ref.at[j], send_c.at[j], recv_c.at[j], (j, me_t)).wait_recv()
+        return carry
+    lax.fori_loop(1, n_src, wait_c, 0)
+
+
+def src_sum(part, dtype):
+    n_src = lax.axis_size("src")
+    rows, width = part.shape
+    chunks = part.reshape(n_src, rows // n_src, width)
+    vmem = pl.BlockSpec(memory_space=pltpu.VMEM)
+    out = pl.pallas_call(
+        functools.partial(src_sum_kernel, n_src),
+        out_shape=jax.ShapeDtypeStruct(chunks.shape, dtype),
+        in_specs=[vmem],
+        out_specs=vmem,
+        scratch_shapes=[
+            pltpu.VMEM(chunks.shape, jnp.float32),
+            pltpu.SemaphoreType.DMA((n_src,)),
+            pltpu.SemaphoreType.DMA((n_src,)),
+            pltpu.SemaphoreType.DMA((n_src,)),
+            pltpu.SemaphoreType.DMA((n_src,)),
+        ],
+        compiler_params=pltpu.CompilerParams(has_side_effects=True),
+    )(chunks)
+    return out.reshape(rows, width)
+
+
+def stats_gather_kernel(n_src, n_tgt, row_ref, col_ref, row_out, col_out,
+                        send_r, recv_r, send_c, recv_c):
+    me_s = lax.axis_index("src")
+    me_t = lax.axis_index("tgt")
+
+    def row_copy(k, slot):
+        return pltpu.make_async_remote_copy(
+            src_ref=row_ref, dst_ref=row_out.at[slot], send_sem=send_r.at[k],
+            recv_sem=recv_r.at[slot], device_id=(me_s, k), device_id_type=MESH)
+
+    def col_copy(k, slot):
+        return pltpu.make_async_remote_copy(
+            src_ref=col_ref, dst_ref=col_out.at[slot], send_sem=send_c.at[k],
+            recv_sem=recv_c.at[slot], device_id=(k, me_t), device_id_type=MESH)
+
+    def start_c(d, carry):
+        col_copy(lax.rem(me_s + d, n_src), me_s).start()
+        return carry
+    lax.fori_loop(1, n_src, start_c, 0)
+
+    def start_r(d, carry):
+        row_copy(lax.rem(me_t + d, n_tgt), me_t).start()
+        return carry
+    lax.fori_loop(1, n_tgt, start_r, 0)
+    row_out[me_t] = row_ref[...]
+    col_out[me_s] = col_ref[...]
+
+    def wait_r(d, carry):
+        row_copy(lax.rem(me_t + d, n_tgt), me_t).wait_send()
+        j = lax.rem(me_t + n_tgt - d, n_tgt)
+        row_copy(j, j).wait_recv()
+        return carry
+    lax.fori_loop(1, n_tgt, wait_r, 0)
+
+    def wait_c(d, carry):
+        col_copy(lax.rem(me_s + d, n_src), me_s).wait_send()
+        j = lax.rem(me_s + n_src - d, n_src)
+        col_copy(j, j).wait_recv()
+        return carry
+    lax.fori_loop(1, n_src, wait_c, 0)
+
+
+def merge(gathered):
     tops, totals = gathered[:, 0], gathered[:, 1]
     best = jnp.max(tops, axis=0)
     return best, jnp.sum(totals * jnp.exp(tops - best[None]), axis=0)
+
+
+def gather_stats(row_top, row_part, col_top, col_part):
+    n_src = lax.axis_size("src")
+    n_tgt = lax.axis_size("tgt")
+    n_row, n_col = row_top.shape[0], col_top.shape[0]
+    rows = jnp.stack([row_top, row_part]).reshape(2 * n_row // 128, 128)
+    cols = jnp.stack([col_top, col_part]).reshape(2 * n_col // 128, 128)
+    vmem = pl.BlockSpec(memory_space=pltpu.VMEM)
+    row_all, col_all = pl.pallas_call(
+        functools.partial(stats_gather_kernel, n_src, n_tgt),
+        out_shape=(jax.ShapeDtypeStruct((n_tgt,) + rows.shape, jnp.float32),
+                   jax.ShapeDtypeStruct((n_src,) + cols.shape, jnp.float32)),
+        in_specs=[vmem, vmem],
+        out_specs=(vmem, vmem),
+        scratch_shapes=[
+            pltpu.SemaphoreType.DMA((n_tgt,)),
+            pltpu.SemaphoreType.DMA((n_tgt,)),
+            pltpu.SemaphoreType.DMA((n_src,)),
+            pltpu.SemaphoreType.DMA((n_src,)),
+        ],
+        compiler_params=pltpu.CompilerParams(has_side_effects=True),
+    )(rows, cols)
+    row_top, row_total = merge(row_all.reshape(n_tgt, 2, n_row))
+    col_top, col_total = merge(col_all.reshape(n_src, 2, n_col))
+    return row_top, row_total, col_top, col_total
 
 
 def body(source, target, start_map):
@@ -135,8 +264,7 @@
         col_local = jnp.max(scores, axis=0)
         row_part = jnp.sum(jnp.exp(scores - row_local[:, None]), axis=1)
         col_part = jnp.sum(jnp.exp(scores - col_local[None, :]), axis=0)
-        row_top, row_total = merge_stats(row_local, row_part, "tgt")
-        col_top, col_total = merge_stats(col_local, col_part, "src")
+        row_top, row_total, col_top, col_total = gather_stats(row_local, row_part, col_local, col_part)
         row_weights = (jnp.exp(scores - row_top[:, None]) / row_total[:, None]).astype(jnp.bfloat16)
         col_weights = (jnp.exp(scores - col_top[None, :]) / col_total[None, :]).astype(jnp.bfloat16)
         source_part = jnp.dot(row_weights, target, preferred_element_type=jnp.float32)
@@ -150,7 +278,7 @@
             source_soft = lax.psum_scatter(
                 source_part, "tgt", scatter_dimension=0, tiled=True
             ).astype(jnp.bfloat16)
-            target_soft = lax.psum(target_part, "src").astype(jnp.bfloat16)
+            target_soft = src_sum(target_part, jnp.bfloat16)
         current = polar_steps(covariance)
     return (source_soft, target_soft, current)
 

time: 499 us -> 421 us (0.84)
  blocking collectives: 295 us -> 0 us
  Pallas kernels: 82.9 us -> 282 us
  local copies, waits for them, and re-layouts: 6.5 us -> 17.4 us
  matrix products: 71.9 us -> 81.4 us
    pallas_call x0 -> x3, Pallas kernels: none -> 198 us  [the longest x1 135 us: src_sum(): pl.pallas_call(functools.partial(src_sum_kernel, n_src), out_shape=jax.Sh...]
    psum x1 -> x0, blocking collectives: 168 us -> none  [body(): target_soft = lax.psum(target_part, 'src').astype(jnp.bfloat16)]
    all_gather x4 -> x0, blocking collectives: 128 us -> none  [merge_stats(): gathered = lax.all_gather(jnp.stack([top, total]), axis)]
  transfers between devices with their start and end apart: 1 -> 1, of which waited for: 0 -> 0; matrix products, arithmetic and copies ran while one was open for 7% -> 9% of each run, Pallas kernels for 8% -> 43%
where the time goes in v3:
time: 421 us; the launch traced here: 416 us
  Pallas kernels  282 us (67%)
  matrix products  81.4 us (19%)
  other arithmetic  19.1 us (5%)
  local copies, waits for them, and re-layouts  17.4 us (4%)
  between operations  16.2 us (4%)
    pallas_call x1, Pallas kernels, src_sum(): pl.pallas_call(functools.partial(src_sum_kernel, n_src), out_shape=jax.Sh...  135 us
    pallas_call x2, Pallas kernels, all_reduce(): pl.pallas_call(functools.partial(all_reduce_kernel, n_src, n_tgt), out_sh...  84.1 us
    pallas_call x2, Pallas kernels, gather_stats(): pl.pallas_call(functools.partial(stats_gather_kernel, n_src, n_tgt), out_...  62.7 us
    dot_general x16, matrix products, polar_steps(): gram_matrix = jnp.dot(current.T, current, precision=highest)  19.7 us
    dot_general x16, matrix products, polar_steps(): jnp.dot(current, gram_matrix, precision=highest)  17.7 us
    dot_general x2, matrix products, body(): lax.dot_general(mapped, target, (((1,), (1,)), ((), ())), preferred_eleme...  12.6 us
    dot_general x2, matrix products, body(): jnp.dot(row_weights, target, preferred_element_type=jnp.float32)  11.6 us
    reduce_sum x2, other arithmetic, body(): col_part = jnp.sum(jnp.exp(scores - col_local[None, :]), axis=0)  10.6 us
  transfers between devices with their start and end apart: 1, of which 0 were waited for; matrix products, arithmetic and copies ran while one was open for 9% of the time, Pallas kernels for 43%

profile of v3, /device:TPU:2, one launch (start us, length us, event | category | flops | bytes accessed | tf_op | source)
XLA Modules:
  0.0 415.8 jit_solution(2344592115606783241)
XLA Ops:
  7.2 1.2 copy-done
  8.5 7.3 %multiply_reduce_fusion.2 = (f32[2048]{0:T(1024)S(1)}, f32[1024]{0:T(1024)S(1)}, f32[1024,2048]{1,0:T(8,128)}) fusion(bf16[2048,300]{0,1:T(8,128)(2,1)S(1)} %copy-done, bf16[1024,300]{0,1:T(8,128)(2,1)} %param.3, f32[300,300]{1,0:T(8,128)} %param.5), kind=kOutput, calls=%fused_computation.10 | convolution fusion | flops 1449296768 | bytes 10604096 | tf_op jit(solution)/shard_map/dot_general | solution.py:258
  15.8 5.3 %exponential_reduce_fusion.2 = (f32[2048]{0:T(1024)S(1)}, f32[1024]{0:T(1024)S(1)}) fusion(f32[1024,2048]{1,0:T(8,128)} %get-tuple-element.37, f32[2048]{0:T(1024)S(1)} %get-tuple-element.23, f32[1024]{0:T(1024)S(1)} %get-tuple-element.24), kind=kLoop, calls=%fused_computation.6 | loop fusion | flops 10482688 | bytes 8413184 | tf_op jit(solution)/shard_map/reduce_sum | solution.py:266
  22.3 33.6 %shard_map.58 = (f32[8,16,128]{2,1,0:T(8,128)}, f32[32,32,128]{2,1,0:T(8,128)}) custom-call(f32[16,128]{1,0:T(8,128)} %reshape.96.row_ref, f32[32,128]{1,0:T(8,128)} %reshape.97.col_ref), custom_call_target="tpu_custom_call" | custom-call | tf_op jit(solution)/shard_map/pallas_call | solution.py:228
  55.9 1.3 reshape.99
  57.9 5.9 %fusion = f32[2048,300]{1,0:T(8,128)S(1)} fusion(bf16[1024,300]{0,1:T(8,128)(2,1)S(1)} %copy-done.2, f32[1024,2048]{1,0:T(8,128)} %get-tuple-element.37, f32[2048]{0:T(1024)S(1)} %fusion.31, f32[2048]{0:T(1024)S(1)} %get-tuple-element.28), kind=kOutput, calls=%fused_computation.12 | convolution fusion | flops 1266679808 | bytes 11476992 | tf_op jit(solution)/shard_map/dot_general | solution.py:271
  63.8 2.2 fusion.48
  66.1 5.1 %fusion.2 = f32[1024,300]{1,0:T(8,128)S(1)} fusion(bf16[2048,300]{0,1:T(8,128)(2,1)S(1)} %copy-done, f32[1024,2048]{1,0:T(8,128)} %get-tuple-element.37, f32[1024]{0:T(1024)S(1)} %fusion.41, f32[1024]{0:T(1024)S(1)} %get-tuple-element.34), kind=kOutput, calls=%fused_computation.14 | convolution fusion | flops 1266679808 | bytes 10854400 | tf_op jit(solution)/shard_map/dot_general | solution.py:270
  71.2 2.6 fusion.22
  75.3 41.9 %shard_map.59 = f32[32,24,128]{2,1,0:T(8,128)} custom-call(f32[32,24,128]{2,1,0:T(8,128)} %bitcast.156), custom_call_target="tpu_custom_call" | custom-call | tf_op jit(solution)/shard_map/pallas_call | solution.py:91
  117.2 1.7 multiply_reduce_fusion.5
  121.1 1.2 fusion.49
  122.4 1.0 fusion.21
  123.4 1.2 fusion.50
  125.7 1.2 fusion.51
  128.0 1.2 fusion.52
  130.3 1.2 fusion.53
  131.5 1.3 fusion.17
  132.8 1.2 fusion.54
  135.1 1.2 fusion.55
  136.3 1.0 fusion.15
  137.4 1.2 fusion.56
  138.6 1.1 fusion.23
  139.7 5.3 %multiply_reduce_fusion = (f32[2048]{0:T(1024)S(1)}, f32[1024]{0:T(1024)S(1)}, f32[1024,2048]{1,0:T(8,128)}) fusion(bf16[2048,300]{0,1:T(8,128)(2,1)S(1)} %copy-done, bf16[300,300]{1,0:T(8,128)(2,1)S(1)} %fusion.23, bf16[1024,300]{0,1:T(8,128)(2,1)S(1)} %copy-done.2), kind=kOutput, calls=%fused_computation.8 | convolution fusion | flops 1449206784 | bytes 10424096 | tf_op jit(solution)/shard_map/dot_general | solution.py:258
  145.0 5.3 %exponential_reduce_fusion = (f32[2048]{0:T(1024)S(1)}, f32[1024]{0:T(1024)S(1)}) fusion(f32[1024,2048]{1,0:T(8,128)} %get-tuple-element.38, f32[2048]{0:T(1024)S(1)} %get-tuple-element.19, f32[1024]{0:T(1024)S(1)} %get-tuple-element.20), kind=kLoop, calls=%fused_computation.2 | loop fusion | flops 10482688 | bytes 8413184 | tf_op jit(solution)/shard_map/reduce_sum | solution.py:266
  151.5 29.2 %shard_map.60 = (f32[8,16,128]{2,1,0:T(8,128)}, f32[32,32,128]{2,1,0:T(8,128)}) custom-call(f32[16,128]{1,0:T(8,128)} %reshape.103.row_ref, f32[32,128]{1,0:T(8,128)} %reshape.104.col_ref), custom_call_target="tpu_custom_call" | custom-call | tf_op jit(solution)/shard_map/pallas_call | solution.py:228
  181.7 6.6 %fusion.3 = f32[1024,300]{0,1:T(8,128)} fusion(bf16[2048,300]{0,1:T(8,128)(2,1)S(1)} %copy-done, f32[1024,2048]{1,0:T(8,128)} %get-tuple-element.38, f32[1024]{0:T(1024)S(1)} %fusion.37, f32[1024]{0:T(1024)S(1)} %get-tuple-element.31), kind=kOutput, calls=%fused_computation.15 | convolution fusion | flops 1266679808 | bytes 10854400 | tf_op jit(solution)/shard_map/dot_general | solution.py:270
  188.3 2.4 convolution_bitcast_fusion
  191.7 4.5 %fusion.1 = f32[2048,300]{0,1:T(8,128)S(1)} fusion(bf16[1024,300]{0,1:T(8,128)(2,1)S(1)} %copy-done.2, f32[1024,2048]{1,0:T(8,128)} %get-tuple-element.38, f32[2048]{0:T(1024)S(1)} %fusion.27, f32[2048]{0:T(1024)S(1)} %get-tuple-element.25), kind=kOutput, calls=%fused_computation.13 | convolution fusion | flops 1266679808 | bytes 11476992 | tf_op jit(solution)/shard_map/dot_general | solution.py:271
  196.3 1.5 copy-done.1
  197.8 2.1 convolution_add_fusion
  201.3 42.2 %shard_map.62 = f32[32,24,128]{2,1,0:T(8,128)} custom-call(f32[32,24,128]{2,1,0:T(8,128)} %bitcast.155), custom_call_target="tpu_custom_call" | custom-call | tf_op jit(solution)/shard_map/pallas_call | solution.py:91
  243.5 1.7 multiply_reduce_fusion.4
  247.3 1.2 fusion.57
  249.6 1.2 fusion.58
  251.9 1.2 fusion.59
  253.1 1.0 fusion.11
  254.2 1.2 fusion.60
  255.4 3.4 copy.20
  258.8 134.8 %shard_map.61 = bf16[32,64,300]{2,1,0:T(8,128)(2,1)} custom-call(f32[32,64,300]{2,1,0:T(8,128)} %bitcast.149), custom_call_target="tpu_custom_call" | custom-call | tf_op jit(solution)/shard_map/pallas_call | solution.py:156
  393.7 2.5 copy.23
  397.2 1.2 fusion.61
  398.4 1.0 fusion.9
  399.5 1.2 fusion.62
  401.8 1.2 fusion.63
  404.1 1.2 fusion.64
  405.3 1.8 fusion.6
  407.1 1.6 convert_element_type.40
  (49 shorter events, 20.5 us)
Async XLA Ops:
  7.2 1.3 copy-start
  7.2 399.9 %reduce-scatter.2.cloned.1.call-start = ((), (), s32[]{:S(2)}) async-start(), calls=%async_computation.1 | async-start | bytes 1400832 | tf_op jit(solution)/shard_map/reduce_scatter | solution.py:278
  15.8 42.1 %copy-start.2 = (bf16[1024,300]{0,1:T(8,128)(2,1)S(1)}, bf16[1024,300]{0,1:T(8,128)(2,1)}, u32[]{:S(2)}) copy-start(bf16[1024,300]{0,1:T(8,128)(2,1)} %param.3) | copy-start | bytes 1843204
  57.9 8.1 %copy-start.4 = (f32[8,16,128]{2,1,0:T(8,128)S(1)}, f32[8,16,128]{2,1,0:T(8,128)}, u32[]{:S(2)}) copy-start(f32[8,16,128]{2,1,0:T(8,128)} %get-tuple-element.7) | copy-start | bytes 196612
  181.7 9.0 %copy-start.3 = (f32[32,32,128]{2,1,0:T(8,128)S(1)}, f32[32,32,128]{2,1,0:T(8,128)}, u32[]{:S(2)}) copy-start(f32[32,32,128]{2,1,0:T(8,128)} %get-tuple-element.10) | copy-start | bytes 1572868
  196.3 1.5 copy-start.1
Sparse Core Ops, SparseCore 0:
  188.4 29.3 reduce-scatter.1

commit v4 on v3

--- a/solution.py
+++ b/solution.py
@@ -24,10 +24,28 @@
     return current
 
 
+def peer_barrier(n_src, n_tgt):
+    me_s = lax.axis_index("src")
+    me_t = lax.axis_index("tgt")
+    barrier = pltpu.get_barrier_semaphore()
+
+    def greet_src(d, carry):
+        pl.semaphore_signal(barrier, 1, device_id=(lax.rem(me_s + d, n_src), me_t), device_id_type=MESH)
+        return carry
+    lax.fori_loop(1, n_src, greet_src, 0)
+
+    def greet_tgt(d, carry):
+        pl.semaphore_signal(barrier, 1, device_id=(me_s, lax.rem(me_t + d, n_tgt)), device_id_type=MESH)
+        return carry
+    lax.fori_loop(1, n_tgt, greet_tgt, 0)
+    pl.semaphore_wait(barrier, n_src + n_tgt - 2)
+
+
 def all_reduce_kernel(n_src, n_tgt, x_ref, out_ref, gather_src, gather_tgt,
                       send_a, recv_a, send_b, recv_b, send_c, recv_c):
     me_s = lax.axis_index("src")
     me_t = lax.axis_index("tgt")
+    peer_barrier(n_src, n_tgt)
 
     def copy(src, dst, send, recv, device):
         return pltpu.make_async_remote_copy(
@@ -103,7 +121,7 @@
             pltpu.SemaphoreType.DMA((n_src,)),
             pltpu.SemaphoreType.DMA((n_src,)),
         ],
-        compiler_params=pltpu.CompilerParams(has_side_effects=True),
+        compiler_params=pltpu.CompilerParams(collective_id=0, has_side_effects=True),
     )(flat)
     return out.reshape(-1)[:size].reshape(matrix.shape)
 
@@ -111,6 +129,7 @@
 def src_sum_kernel(n_src, x_ref, out_ref, gather, send_a, recv_a, send_c, recv_c):
     me_s = lax.axis_index("src")
     me_t = lax.axis_index("tgt")
+    peer_barrier(n_src, 1)
 
     def copy(src, dst, send, recv, device):
         return pltpu.make_async_remote_copy(
@@ -131,7 +150,7 @@
         copy(x_ref.at[j], gather.at[j], send_a.at[j], recv_a.at[j], (j, me_t)).wait_recv()
         return carry
     lax.fori_loop(1, n_src, wait_a, 0)
-    out_ref[me_s] = jnp.sum(gather[...], axis=0).astype(out_ref.dtype)
+    out_ref[me_s] = jnp.sum(gather[...].astype(jnp.float32), axis=0).astype(out_ref.dtype)
 
     def start_c(d, carry):
         k = lax.rem(me_s + d, n_src)
@@ -151,7 +170,7 @@
 def src_sum(part, dtype):
     n_src = lax.axis_size("src")
     rows, width = part.shape
-    chunks = part.reshape(n_src, rows // n_src, width)
+    chunks = part.astype(jnp.bfloat16).reshape(n_src, rows * width // (n_src * 128), 128)
     vmem = pl.BlockSpec(memory_space=pltpu.VMEM)
     out = pl.pallas_call(
         functools.partial(src_sum_kernel, n_src),
@@ -159,13 +178,13 @@
         in_specs=[vmem],
         out_specs=vmem,
         scratch_shapes=[
-            pltpu.VMEM(chunks.shape, jnp.float32),
+            pltpu.VMEM(chunks.shape, chunks.dtype),
             pltpu.SemaphoreType.DMA((n_src,)),
             pltpu.SemaphoreType.DMA((n_src,)),
             pltpu.SemaphoreType.DMA((n_src,)),
             pltpu.SemaphoreType.DMA((n_src,)),
         ],
-        compiler_params=pltpu.CompilerParams(has_side_effects=True),
+        compiler_params=pltpu.CompilerParams(collective_id=1, has_side_effects=True),
     )(chunks)
     return out.reshape(rows, width)
 
@@ -174,6 +193,7 @@
                         send_r, recv_r, send_c, recv_c):
     me_s = lax.axis_index("src")
     me_t = lax.axis_index("tgt")
+    peer_barrier(n_src, n_tgt)
 
     def row_copy(k, slot):
         return pltpu.make_async_remote_copy(
@@ -237,7 +257,7 @@
             pltpu.SemaphoreType.DMA((n_src,)),
             pltpu.SemaphoreType.DMA((n_src,)),
         ],
-        compiler_params=pltpu.CompilerParams(has_side_effects=True),
+        compiler_params=pltpu.CompilerParams(collective_id=2, has_side_effects=True),
     )(rows, cols)
     row_top, row_total = merge(row_all.reshape(n_tgt, 2, n_row))
     col_top, col_total = merge(col_all.reshape(n_src, 2, n_col))

time: 421 us -> 338 us (0.80)
  Pallas kernels: 282 us -> 187 us
  matrix products: 81.4 us -> 87.2 us
  local copies, waits for them, and re-layouts: 17.4 us -> 22.6 us
    pallas_call x1, Pallas kernels: 135 us -> 68.9 us  [src_sum(): pl.pallas_call(functools.partial(src_sum_kernel, n_src), out_shape=jax.Sh...]
    pallas_call x2, Pallas kernels: 62.7 us -> 47.4 us  [gather_stats(): pl.pallas_call(functools.partial(stats_gather_kernel, n_src, n_tgt), out_...]
    pallas_call x2, Pallas kernels: 84.1 us -> 70.8 us  [all_reduce(): pl.pallas_call(functools.partial(all_reduce_kernel, n_src, n_tgt), out_sh...]
    reshape x0 -> x2, local copies, waits for them, and re-layouts: none -> 9.46 us  [the longest x1 5.43 us: src_sum(): return out.reshape(rows, width)]
  transfers between devices with their start and end apart: 1 -> 1, of which waited for: 0 -> 0; matrix products, arithmetic and copies ran while one was open for 9% -> 15% of each run, Pallas kernels for 43% -> 31%
where the time goes in v4:
time: 338 us; the launch traced here: 332 us
  Pallas kernels  187 us (55%)
  matrix products  87.2 us (26%)
  local copies, waits for them, and re-layouts  22.6 us (7%)
  other arithmetic  19 us (6%)
  between operations  16.2 us (5%)
    pallas_call x2, Pallas kernels, all_reduce(): pl.pallas_call(functools.partial(all_reduce_kernel, n_src, n_tgt), out_sh...  70.8 us
    pallas_call x1, Pallas kernels, src_sum(): pl.pallas_call(functools.partial(src_sum_kernel, n_src), out_shape=jax.Sh...  68.9 us
    pallas_call x2, Pallas kernels, gather_stats(): pl.pallas_call(functools.partial(stats_gather_kernel, n_src, n_tgt), out_...  47.4 us
    dot_general x16, matrix products, polar_steps(): gram_matrix = jnp.dot(current.T, current, precision=highest)  20.5 us
    dot_general x16, matrix products, polar_steps(): jnp.dot(current, gram_matrix, precision=highest)  18.7 us
    dot_general x2, matrix products, body(): jnp.dot(row_weights, target, preferred_element_type=jnp.float32)  13.7 us
    dot_general x2, matrix products, body(): lax.dot_general(mapped, target, (((1,), (1,)), ((), ())), preferred_eleme...  12.6 us
    dot_general x2, matrix products, body(): lax.dot_general(col_weights, source, (((0,), (0,)), ((), ())), preferred_...  12.3 us
  transfers between devices with their start and end apart: 1, of which 0 were waited for; matrix products, arithmetic and copies ran while one was open for 15% of the time, Pallas kernels for 31%

profile of v4, /device:TPU:2, one launch (start us, length us, event | category | flops | bytes accessed | tf_op | source)
XLA Modules:
  0.0 332.1 jit_solution(15111334518145626035)
XLA Ops:
  7.2 1.2 copy-done
  8.5 7.3 %multiply_reduce_fusion.2 = (f32[2048]{0:T(1024)S(1)}, f32[1024]{0:T(1024)S(1)}, f32[1024,2048]{1,0:T(8,128)}) fusion(bf16[2048,300]{0,1:T(8,128)(2,1)S(1)} %copy-done, bf16[1024,300]{0,1:T(8,128)(2,1)} %param.3, f32[300,300]{1,0:T(8,128)} %param.5), kind=kOutput, calls=%fused_computation.10 | convolution fusion | flops 1449296768 | bytes 10604096 | tf_op jit(solution)/shard_map/dot_general | solution.py:278
  15.8 5.2 %exponential_reduce_fusion.2 = (f32[2048]{0:T(1024)S(1)}, f32[1024]{0:T(1024)S(1)}) fusion(f32[1024,2048]{1,0:T(8,128)} %get-tuple-element.37, f32[2048]{0:T(1024)S(1)} %get-tuple-element.23, f32[1024]{0:T(1024)S(1)} %get-tuple-element.24), kind=kLoop, calls=%fused_computation.6 | loop fusion | flops 10482688 | bytes 8413184 | tf_op jit(solution)/shard_map/reduce_sum | solution.py:286
  22.3 25.3 %shard_map.58 = (f32[8,16,128]{2,1,0:T(8,128)}, f32[32,32,128]{2,1,0:T(8,128)}) custom-call(f32[16,128]{1,0:T(8,128)} %reshape.96.row_ref, f32[32,128]{1,0:T(8,128)} %reshape.97.col_ref), custom_call_target="tpu_custom_call" | custom-call | tf_op jit(solution)/shard_map/pallas_call | solution.py:248
  48.6 7.1 %fusion.2 = f32[1024,300]{1,0:T(8,128)} fusion(bf16[2048,300]{0,1:T(8,128)(2,1)S(1)} %copy-done, f32[1024,2048]{1,0:T(8,128)} %get-tuple-element.37, f32[1024]{0:T(1024)S(1)} %fusion.41, f32[1024]{0:T(1024)S(1)} %get-tuple-element.34), kind=kOutput, calls=%fused_computation.14 | convolution fusion | flops 1266679808 | bytes 10854400 | tf_op jit(solution)/shard_map/dot_general | solution.py:290
  56.7 5.9 %fusion = f32[2048,300]{1,0:T(8,128)S(1)} fusion(bf16[1024,300]{0,1:T(8,128)(2,1)S(1)} %copy-done.1, f32[1024,2048]{1,0:T(8,128)} %get-tuple-element.37, f32[2048]{0:T(1024)S(1)} %fusion.31, f32[2048]{0:T(1024)S(1)} %get-tuple-element.28), kind=kOutput, calls=%fused_computation.12 | convolution fusion | flops 1266679808 | bytes 11476992 | tf_op jit(solution)/shard_map/dot_general | solution.py:291
  62.6 2.2 fusion.49
  64.8 2.6 fusion.22
  68.9 35.5 %shard_map.59 = f32[32,24,128]{2,1,0:T(8,128)} custom-call(f32[32,24,128]{2,1,0:T(8,128)} %bitcast.152), custom_call_target="tpu_custom_call" | custom-call | tf_op jit(solution)/shard_map/pallas_call | solution.py:109
  104.4 1.7 multiply_reduce_fusion.5
  108.2 1.2 fusion.50
  109.5 1.0 fusion.21
  110.5 1.2 fusion.51
  112.8 1.2 fusion.52
  115.1 1.2 fusion.53
  117.4 1.2 fusion.54
  118.6 1.3 fusion.17
  119.9 1.2 fusion.55
  122.2 1.2 fusion.56
  123.4 1.0 fusion.15
  124.5 1.2 fusion.57
  125.7 1.1 fusion.23
  126.8 5.3 %multiply_reduce_fusion = (f32[2048]{0:T(1024)S(1)}, f32[1024]{0:T(1024)S(1)}, f32[1024,2048]{1,0:T(8,128)}) fusion(bf16[2048,300]{0,1:T(8,128)(2,1)S(1)} %copy-done, bf16[300,300]{1,0:T(8,128)(2,1)S(1)} %fusion.23, bf16[1024,300]{0,1:T(8,128)(2,1)S(1)} %copy-done.1), kind=kOutput, calls=%fused_computation.8 | convolution fusion | flops 1449206784 | bytes 10424096 | tf_op jit(solution)/shard_map/dot_general | solution.py:278
  132.1 5.3 %exponential_reduce_fusion = (f32[2048]{0:T(1024)S(1)}, f32[1024]{0:T(1024)S(1)}) fusion(f32[1024,2048]{1,0:T(8,128)} %get-tuple-element.38, f32[2048]{0:T(1024)S(1)} %get-tuple-element.19, f32[1024]{0:T(1024)S(1)} %get-tuple-element.20), kind=kLoop, calls=%fused_computation.2 | loop fusion | flops 10482688 | bytes 8413184 | tf_op jit(solution)/shard_map/reduce_sum | solution.py:286
  138.6 22.1 %shard_map.60 = (f32[8,16,128]{2,1,0:T(8,128)}, f32[32,32,128]{2,1,0:T(8,128)}) custom-call(f32[16,128]{1,0:T(8,128)} %reshape.103.row_ref, f32[32,128]{1,0:T(8,128)} %reshape.104.col_ref), custom_call_target="tpu_custom_call" | custom-call | tf_op jit(solution)/shard_map/pallas_call | solution.py:248
  161.7 6.6 %fusion.3 = f32[1024,300]{0,1:T(8,128)} fusion(bf16[2048,300]{0,1:T(8,128)(2,1)S(1)} %copy-done, f32[1024,2048]{1,0:T(8,128)} %get-tuple-element.38, f32[1024]{0:T(1024)S(1)} %fusion.37, f32[1024]{0:T(1024)S(1)} %get-tuple-element.31), kind=kOutput, calls=%fused_computation.15 | convolution fusion | flops 1266679808 | bytes 10854400 | tf_op jit(solution)/shard_map/dot_general | solution.py:290
  168.3 2.4 convolution_bitcast_fusion
  171.7 6.4 %fusion.48 = (bf16[2048,300]{0,1:T(8,128)(2,1)}, f32[2048,300]{0,1:T(8,128)S(1)}) fusion(bf16[1024,300]{0,1:T(8,128)(2,1)S(1)} %copy-done.1, f32[1024,2048]{1,0:T(8,128)} %get-tuple-element.38, f32[2048]{0:T(1024)S(1)} %fusion.27, f32[2048]{0:T(1024)S(1)} %get-tuple-element.25), kind=kOutput, calls=%fused_computation.94 | convolution fusion | flops 1267294208 | bytes 12705792 | tf_op jit(solution)/shard_map/dot_general | solution.py:291
  178.1 2.1 convolution_add_fusion
  181.6 35.3 %shard_map.62 = f32[32,24,128]{2,1,0:T(8,128)} custom-call(f32[32,24,128]{2,1,0:T(8,128)} %bitcast.151), custom_call_target="tpu_custom_call" | custom-call | tf_op jit(solution)/shard_map/pallas_call | solution.py:109
  217.0 1.7 multiply_reduce_fusion.4
  220.8 1.2 fusion.58
  223.1 1.2 fusion.59
  225.4 1.2 fusion.60
  226.7 1.0 fusion.11
  227.7 2.0 fusion.61
  229.7 1.8 copy.20
  231.5 4.0 %reshape.107.x_ref = bf16[32,150,128]{2,1,0:T(8,128)(2,1)} reshape(bf16[2048,300]{1,0:T(8,128)(2,1)S(1)} %copy.20) | data formatting | bytes 2457600 | tf_op jit(solution)/shard_map/reshape | solution.py:173
  235.6 68.9 %shard_map.61 = bf16[32,150,128]{2,1,0:T(8,128)(2,1)} custom-call(bf16[32,150,128]{2,1,0:T(8,128)(2,1)} %reshape.107.x_ref), custom_call_target="tpu_custom_call" | custom-call | tf_op jit(solution)/shard_map/pallas_call | solution.py:175
  304.5 5.4 %reshape.108 = bf16[2048,300]{1,0:T(8,128)(2,1)S(1)} reshape(bf16[32,150,128]{2,1,0:T(8,128)(2,1)} %shard_map.61) | data formatting | bytes 2457600 | tf_op jit(solution)/shard_map/reshape | solution.py:189
  309.9 1.5 copy.23
  311.5 2.1 fusion.10
  313.5 1.2 fusion.62
  315.8 1.2 fusion.63
  318.1 1.2 fusion.64
  320.4 1.2 fusion.65
  321.6 1.8 fusion.6
  323.5 1.6 convert_element_type.43
  (51 shorter events, 21.6 us)
Async XLA Ops:
  7.2 1.3 copy-start
  7.2 316.3 %reduce-scatter.2.cloned.1.call-start = ((), (), s32[]{:S(2)}) async-start(), calls=%async_computation.1 | async-start | bytes 1400832 | tf_op jit(solution)/shard_map/reduce_scatter | solution.py:298
  48.6 7.1 %copy-start.4 = (f32[32,32,128]{2,1,0:T(8,128)S(1)}, f32[32,32,128]{2,1,0:T(8,128)}, u32[]{:S(2)}) copy-start(f32[32,32,128]{2,1,0:T(8,128)} %get-tuple-element.8) | copy-start | bytes 1572868
  48.6 8.1 %copy-start.1 = (bf16[1024,300]{0,1:T(8,128)(2,1)S(1)}, bf16[1024,300]{0,1:T(8,128)(2,1)}, u32[]{:S(2)}) copy-start(bf16[1024,300]{0,1:T(8,128)(2,1)} %param.3) | copy-start | bytes 1843204
  56.6 8.2 %copy-start.2 = (f32[1024,300]{1,0:T(8,128)S(1)}, f32[1024,300]{1,0:T(8,128)}, u32[]{:S(2)}) copy-start(f32[1024,300]{1,0:T(8,128)} %fusion.2) | copy-start | bytes 3686404
  161.7 9.0 %copy-start.3 = (f32[32,32,128]{2,1,0:T(8,128)S(1)}, f32[32,32,128]{2,1,0:T(8,128)}, u32[]{:S(2)}) copy-start(f32[32,32,128]{2,1,0:T(8,128)} %get-tuple-element.10) | copy-start | bytes 1572868
Sparse Core Ops, SparseCore 0:
  168.4 30.1 reduce-scatter.1

commit v5 on v1

--- a/solution.py
+++ b/solution.py
@@ -1,9 +1,15 @@
 import math
+
+import functools
 
 import jax
 import jax.numpy as jnp
 from jax import lax
+from jax.experimental import pallas as pl
+from jax.experimental.pallas import tpu as pltpu
 from jax.sharding import PartitionSpec as P
+
+MESH = pl.DeviceIdType.MESH
 
 ITERS = 2
 NEWTON_STEPS = 8
@@ -12,17 +18,197 @@
 def polar_steps(covariance):
     highest = lax.Precision.HIGHEST
     current = covariance / jnp.sqrt(jnp.sum(covariance * covariance) + 1e-06)
-    for newton in range(NEWTON_STEPS):
+
+    def newton(step, current):
         gram_matrix = jnp.dot(current.T, current, precision=highest)
-        current = 1.5 * current - 0.5 * jnp.dot(current, gram_matrix, precision=highest)
-    return current
-
-
-def merge_stats(top, total, axis):
-    gathered = lax.all_gather(jnp.stack([top, total]), axis)
+        return 1.5 * current - 0.5 * jnp.dot(current, gram_matrix, precision=highest)
+    return lax.fori_loop(0, NEWTON_STEPS, newton, current)
+
+
+def peer_barrier(n_src, n_tgt):
+    me_s = lax.axis_index("src")
+    me_t = lax.axis_index("tgt")
+    barrier = pltpu.get_barrier_semaphore()
+
+    def greet_src(d, carry):
+        pl.semaphore_signal(barrier, 1, device_id=(lax.rem(me_s + d, n_src), me_t), device_id_type=MESH)
+        return carry
+    lax.fori_loop(1, n_src, greet_src, 0)
+
+    def greet_tgt(d, carry):
+        pl.semaphore_signal(barrier, 1, device_id=(me_s, lax.rem(me_t + d, n_tgt)), device_id_type=MESH)
+        return carry
+    lax.fori_loop(1, n_tgt, greet_tgt, 0)
+    pl.semaphore_wait(barrier, n_src + n_tgt - 2)
+
+
+def remote(src, dst, send, recv, device):
+    return pltpu.make_async_remote_copy(
+        src_ref=src, dst_ref=dst, send_sem=send, recv_sem=recv,
+        device_id=device, device_id_type=MESH)
+
+
+def start_all(me, n, device, src, slot, send, recv):
+    def step(d, carry):
+        k = lax.rem(me + d, n)
+        remote(src(k), slot(me), send.at[k], recv.at[me], device(k)).start()
+        return carry
+    lax.fori_loop(1, n, step, 0)
+
+
+def wait_all(me, n, device, src, slot, send, recv):
+    def step(d, carry):
+        k = lax.rem(me + d, n)
+        remote(src(k), slot(me), send.at[k], recv.at[me], device(k)).wait_send()
+        j = lax.rem(me + n - d, n)
+        remote(src(j), slot(j), send.at[j], recv.at[j], device(j)).wait_recv()
+        return carry
+    lax.fori_loop(1, n, step, 0)
+
+
+def all_reduce_kernel(n_src, n_tgt, with_target, *refs):
+    if with_target:
+        (xc, xt, oc, ot, gather_src, gather_tgt, gather_t,
+         s_a, r_a, s_b, r_b, s_c, r_c, s_ta, r_ta, s_tc, r_tc) = refs
+    else:
+        xc, oc, gather_src, gather_tgt, s_a, r_a, s_b, r_b, s_c, r_c = refs
+    me_s = lax.axis_index("src")
+    me_t = lax.axis_index("tgt")
+    peer_barrier(n_src, n_tgt)
+    on_src = lambda k: (k, me_t)
+    on_tgt = lambda k: (me_s, k)
+
+    if with_target:
+        start_all(me_s, n_src, on_src, lambda k: xt.at[k], lambda i: gather_t.at[i], s_ta, r_ta)
+        gather_t[me_s] = xt[me_s]
+
+    start_all(me_s, n_src, on_src, lambda k: xc.at[k], lambda i: gather_src.at[i], s_a, r_a)
+    gather_src[me_s] = xc[me_s]
+    wait_all(me_s, n_src, on_src, lambda k: xc.at[k], lambda i: gather_src.at[i], s_a, r_a)
+    gather_tgt[me_t] = jnp.sum(gather_src[...], axis=0)
+
+    start_all(me_t, n_tgt, on_tgt, lambda k: gather_tgt.at[me_t], lambda i: gather_tgt.at[i], s_b, r_b)
+    wait_all(me_t, n_tgt, on_tgt, lambda k: gather_tgt.at[me_t], lambda i: gather_tgt.at[i], s_b, r_b)
+    oc[me_s] = jnp.sum(gather_tgt[...], axis=0)
+
+    start_all(me_s, n_src, on_src, lambda k: oc.at[me_s], lambda i: oc.at[i], s_c, r_c)
+    if with_target:
+        wait_all(me_s, n_src, on_src, lambda k: xt.at[k], lambda i: gather_t.at[i], s_ta, r_ta)
+        ot[me_s] = jnp.sum(gather_t[...].astype(jnp.float32), axis=0).astype(ot.dtype)
+        start_all(me_s, n_src, on_src, lambda k: ot.at[me_s], lambda i: ot.at[i], s_tc, r_tc)
+    wait_all(me_s, n_src, on_src, lambda k: oc.at[me_s], lambda i: oc.at[i], s_c, r_c)
+    if with_target:
+        wait_all(me_s, n_src, on_src, lambda k: ot.at[me_s], lambda i: ot.at[i], s_tc, r_tc)
+
+
+def all_reduce(matrix, target_part=None):
+    n_src = lax.axis_size("src")
+    n_tgt = lax.axis_size("tgt")
+    size = matrix.size
+    lines = -(-size // 128)
+    rows = -(-lines // (n_src * 8)) * 8
+    flat = jnp.pad(matrix.reshape(-1), (0, n_src * rows * 128 - size)).reshape(n_src, rows, 128)
+    vmem = pl.BlockSpec(memory_space=pltpu.VMEM)
+    sems = [pltpu.SemaphoreType.DMA((n,)) for n in (n_src, n_src, n_tgt, n_tgt, n_src, n_src)]
+    scratch = [pltpu.VMEM((n_src, rows, 128), jnp.float32), pltpu.VMEM((n_tgt, rows, 128), jnp.float32)]
+    if target_part is None:
+        out = pl.pallas_call(
+            functools.partial(all_reduce_kernel, n_src, n_tgt, False),
+            out_shape=jax.ShapeDtypeStruct(flat.shape, jnp.float32),
+            in_specs=[vmem],
+            out_specs=vmem,
+            scratch_shapes=scratch + sems,
+            compiler_params=pltpu.CompilerParams(collective_id=0, has_side_effects=True),
+        )(flat)
+        return out.reshape(-1)[:size].reshape(matrix.shape)
+    t_rows, width = target_part.shape
+    chunks = target_part.astype(jnp.bfloat16).reshape(n_src, t_rows * width // (n_src * 128), 128)
+    out, target_sum = pl.pallas_call(
+        functools.partial(all_reduce_kernel, n_src, n_tgt, True),
+        out_shape=(jax.ShapeDtypeStruct(flat.shape, jnp.float32),
+                   jax.ShapeDtypeStruct(chunks.shape, jnp.bfloat16)),
+        in_specs=[vmem, vmem],
+        out_specs=(vmem, vmem),
+        scratch_shapes=scratch + [pltpu.VMEM(chunks.shape, jnp.bfloat16)] + sems
+        + [pltpu.SemaphoreType.DMA((n_src,)) for _ in range(4)],
+        compiler_params=pltpu.CompilerParams(collective_id=1, has_side_effects=True),
+    )(flat, chunks)
+    return out.reshape(-1)[:size].reshape(matrix.shape), target_sum.reshape(t_rows, width)
+
+
+def stats_gather_kernel(n_src, n_tgt, row_ref, col_ref, row_out, col_out,
+                        send_r, recv_r, send_c, recv_c):
+    me_s = lax.axis_index("src")
+    me_t = lax.axis_index("tgt")
+    peer_barrier(n_src, n_tgt)
+
+    def row_copy(k, slot):
+        return pltpu.make_async_remote_copy(
+            src_ref=row_ref, dst_ref=row_out.at[slot], send_sem=send_r.at[k],
+            recv_sem=recv_r.at[slot], device_id=(me_s, k), device_id_type=MESH)
+
+    def col_copy(k, slot):
+        return pltpu.make_async_remote_copy(
+            src_ref=col_ref, dst_ref=col_out.at[slot], send_sem=send_c.at[k],
+            recv_sem=recv_c.at[slot], device_id=(k, me_t), device_id_type=MESH)
+
+    def start_c(d, carry):
+        col_copy(lax.rem(me_s + d, n_src), me_s).start()
+        return carry
+    lax.fori_loop(1, n_src, start_c, 0)
+
+    def start_r(d, carry):
+        row_copy(lax.rem(me_t + d, n_tgt), me_t).start()
+        return carry
+    lax.fori_loop(1, n_tgt, start_r, 0)
+    row_out[me_t] = row_ref[...]
+    col_out[me_s] = col_ref[...]
+
+    def wait_r(d, carry):
+        row_copy(lax.rem(me_t + d, n_tgt), me_t).wait_send()
+        j = lax.rem(me_t + n_tgt - d, n_tgt)
+        row_copy(j, j).wait_recv()
+        return carry
+    lax.fori_loop(1, n_tgt, wait_r, 0)
+
+    def wait_c(d, carry):
+        col_copy(lax.rem(me_s + d, n_src), me_s).wait_send()
+        j = lax.rem(me_s + n_src - d, n_src)
+        col_copy(j, j).wait_recv()
+        return carry
+    lax.fori_loop(1, n_src, wait_c, 0)
+
+
+def merge(gathered):
     tops, totals = gathered[:, 0], gathered[:, 1]
     best = jnp.max(tops, axis=0)
     return best, jnp.sum(totals * jnp.exp(tops - best[None]), axis=0)
+
+
+def gather_stats(row_top, row_part, col_top, col_part):
+    n_src = lax.axis_size("src")
+    n_tgt = lax.axis_size("tgt")
+    n_row, n_col = row_top.shape[0], col_top.shape[0]
+    rows = jnp.stack([row_top, row_part]).reshape(2 * n_row // 128, 128)
+    cols = jnp.stack([col_top, col_part]).reshape(2 * n_col // 128, 128)
+    vmem = pl.BlockSpec(memory_space=pltpu.VMEM)
+    row_all, col_all = pl.pallas_call(
+        functools.partial(stats_gather_kernel, n_src, n_tgt),
+        out_shape=(jax.ShapeDtypeStruct((n_tgt,) + rows.shape, jnp.float32),
+                   jax.ShapeDtypeStruct((n_src,) + cols.shape, jnp.float32)),
+        in_specs=[vmem, vmem],
+        out_specs=(vmem, vmem),
+        scratch_shapes=[
+            pltpu.SemaphoreType.DMA((n_tgt,)),
+            pltpu.SemaphoreType.DMA((n_tgt,)),
+            pltpu.SemaphoreType.DMA((n_src,)),
+            pltpu.SemaphoreType.DMA((n_src,)),
+        ],
+        compiler_params=pltpu.CompilerParams(collective_id=2, has_side_effects=True),
+    )(rows, cols)
+    row_top, row_total = merge(row_all.reshape(n_tgt, 2, n_row))
+    col_top, col_total = merge(col_all.reshape(n_src, 2, n_col))
+    return row_top, row_total, col_top, col_total
 
 
 def body(source, target, start_map):
@@ -45,8 +231,7 @@
         col_local = jnp.max(scores, axis=0)
         row_part = jnp.sum(jnp.exp(scores - row_local[:, None]), axis=1)
         col_part = jnp.sum(jnp.exp(scores - col_local[None, :]), axis=0)
-        row_top, row_total = merge_stats(row_local, row_part, "tgt")
-        col_top, col_total = merge_stats(col_local, col_part, "src")
+        row_top, row_total, col_top, col_total = gather_stats(row_local, row_part, col_local, col_part)
         row_weights = (jnp.exp(scores - row_top[:, None]) / row_total[:, None]).astype(jnp.bfloat16)
         col_weights = (jnp.exp(scores - col_top[None, :]) / col_total[None, :]).astype(jnp.bfloat16)
         source_part = jnp.dot(row_weights, target, preferred_element_type=jnp.float32)
@@ -55,12 +240,13 @@
         )
         covariance = jnp.dot(source_f32.T, source_part, precision=highest)
         covariance = covariance + jnp.dot(target_part.T, target_f32, precision=highest)
-        covariance = lax.psum(covariance, ("src", "tgt"))
         if iteration == ITERS - 1:
             source_soft = lax.psum_scatter(
                 source_part, "tgt", scatter_dimension=0, tiled=True
             ).astype(jnp.bfloat16)
-            target_soft = lax.psum(target_part, "src").astype(jnp.bfloat16)
+            covariance, target_soft = all_reduce(covariance, target_part)
+        else:
+            covariance = all_reduce(covariance)
         current = polar_steps(covariance)
     return (source_soft, target_soft, current)
 

time: 771 us -> 323 us (0.42)
  waiting for transfers between devices: 338 us -> 0.02 us
  blocking collectives: 294 us -> 0 us
  Pallas kernels: 0 us -> 174 us
  local copies, waits for them, and re-layouts: 4.37 us -> 24.7 us
    psum x2 -> x0, waiting for transfers between devices: 331 us -> none  [body(): covariance = lax.psum(covariance, ('src', 'tgt'))]
    pallas_call x0 -> x4, Pallas kernels: none -> 174 us  [the longest x1 89.6 us: all_reduce(): pl.pallas_call(functools.partial(all_reduce_kernel, n_src, n_tgt, True),...]
    psum x1 -> x0, blocking collectives: 168 us -> none  [body(): target_soft = lax.psum(target_part, 'src').astype(jnp.bfloat16)]
    all_gather x4 -> x0, blocking collectives: 126 us -> none  [merge_stats(): gathered = lax.all_gather(jnp.stack([top, total]), axis)]
    dot_general x32, matrix products: 53.1 us -> 36.1 us  [the longest x16 19.5 us: newton(): jnp.dot(current, gram_matrix, precision=highest)]
    reshape x0 -> x12, local copies, waits for them, and re-layouts: none -> 15.2 us  [the longest x1 5.4 us: all_reduce(): target_sum.reshape(t_rows, width)]
  transfers between devices with their start and end apart: 3 -> 1, of which waited for: 3 -> 0; matrix products, arithmetic and copies ran while one was open for 3% -> 15% of each run, Pallas kernels for 0% -> 28%
where the time goes in v5:
time: 323 us; the launch traced here: 317 us
  Pallas kernels  174 us (54%)
  matrix products  81.9 us (25%)
  local copies, waits for them, and re-layouts  24.7 us (8%)
  other arithmetic  19.4 us (6%)
  between operations  15.9 us (5%)
    pallas_call x1, Pallas kernels, all_reduce(): pl.pallas_call(functools.partial(all_reduce_kernel, n_src, n_tgt, True),...  89.6 us
    pallas_call x2, Pallas kernels, gather_stats(): pl.pallas_call(functools.partial(stats_gather_kernel, n_src, n_tgt), out_...  47.5 us
    pallas_call x1, Pallas kernels, all_reduce(): pl.pallas_call(functools.partial(all_reduce_kernel, n_src, n_tgt, False),...  36.9 us
    dot_general x16, matrix products, newton(): jnp.dot(current, gram_matrix, precision=highest)  19.5 us
    dot_general x16, matrix products, newton(): gram_matrix = jnp.dot(current.T, current, precision=highest)  16.5 us
    dot_general x2, matrix products, body(): lax.dot_general(mapped, target, (((1,), (1,)), ((), ())), preferred_eleme...  12.6 us
    dot_general x2, matrix products, body(): lax.dot_general(col_weights, source, (((0,), (0,)), ((), ())), preferred_...  12.2 us
    dot_general x2, matrix products, body(): jnp.dot(row_weights, target, preferred_element_type=jnp.float32)  11.6 us
  transfers between devices with their start and end apart: 1, of which 0 were waited for; matrix products, arithmetic and copies ran while one was open for 15% of the time, Pallas kernels for 28%

profile of v5, /device:TPU:2, one launch (start us, length us, event | category | flops | bytes accessed | tf_op | source)
XLA Modules:
  0.0 316.5 jit_solution(3445991213621482972)
XLA Ops:
  7.2 1.2 copy-done
  8.5 7.3 %multiply_reduce_fusion.2 = (f32[2048]{0:T(1024)S(1)}, f32[1024]{0:T(1024)S(1)}, f32[1024,2048]{1,0:T(8,128)}) fusion(bf16[2048,300]{0,1:T(8,128)(2,1)S(1)} %copy-done, bf16[1024,300]{0,1:T(8,128)(2,1)} %param.7, f32[300,300]{1,0:T(8,128)} %param.9), kind=kOutput, calls=%fused_computation.16 | convolution fusion | flops 1449296768 | bytes 10604096 | tf_op jit(solution)/shard_map/dot_general | solution.py:225
  15.8 5.6 %exponential_reduce_fusion.2 = (f32[2048]{0:T(1024)S(1)}, f32[1024]{0:T(1024)S(1)}) fusion(f32[1024,2048]{1,0:T(8,128)} %get-tuple-element.79, f32[2048]{0:T(1024)S(1)} %get-tuple-element.57, f32[1024]{0:T(1024)S(1)} %get-tuple-element.58), kind=kLoop, calls=%fused_computation.12 | loop fusion | flops 10482688 | bytes 8413184 | tf_op jit(solution)/shard_map/reduce_sum | solution.py:233
  22.6 25.3 %shard_map.58 = (f32[8,16,128]{2,1,0:T(8,128)}, f32[32,32,128]{2,1,0:T(8,128)}) custom-call(f32[16,128]{1,0:T(8,128)} %reshape.74.row_ref, f32[32,128]{1,0:T(8,128)} %reshape.75.col_ref), custom_call_target="tpu_custom_call" | custom-call | tf_op jit(solution)/shard_map/pallas_call | solution.py:195
  48.0 1.3 reshape.77
  50.0 5.9 %fusion.4 = f32[2048,300]{1,0:T(8,128)S(1)} fusion(bf16[1024,300]{0,1:T(8,128)(2,1)S(1)} %copy-done.1, f32[1024,2048]{1,0:T(8,128)} %get-tuple-element.79, f32[2048]{0:T(1024)S(1)} %fusion.18, f32[2048]{0:T(1024)S(1)} %get-tuple-element.70), kind=kOutput, calls=%fused_computation.18 | convolution fusion | flops 1266679808 | bytes 11476992 | tf_op jit(solution)/shard_map/dot_general | solution.py:238
  55.8 2.2 fusion.42
  58.2 5.1 %fusion.6 = f32[1024,300]{1,0:T(8,128)S(1)} fusion(bf16[2048,300]{0,1:T(8,128)(2,1)S(1)} %copy-done, f32[1024,2048]{1,0:T(8,128)} %get-tuple-element.79, f32[1024]{0:T(1024)S(1)} %fusion.30, f32[1024]{0:T(1024)S(1)} %get-tuple-element.76), kind=kOutput, calls=%fused_computation.20 | convolution fusion | flops 1266679808 | bytes 10854400 | tf_op jit(solution)/shard_map/dot_general | solution.py:237
  63.3 2.6 fusion.10
  67.4 36.9 %shard_map.59 = f32[32,24,128]{2,1,0:T(8,128)} custom-call(f32[32,24,128]{2,1,0:T(8,128)} %bitcast.120), custom_call_target="tpu_custom_call" | custom-call | tf_op jit(solution)/shard_map/pallas_call | solution.py:115
  104.3 1.7 multiply_reduce_fusion.5
  108.4 18.6 %while.20 = (s32[]{:T(128)}, f32[300,300]{0,1:T(8,128)S(1)}, s32[]{:T(128)}) while((s32[]{:T(128)}, f32[300,300]{0,1:T(8,128)S(1)}, s32[]{:T(128)}) %tuple.54), condition=%wide.region_10.11_spmd, body=%wide.region_9.10_spmd.sunk | while | flops 648270016 | bytes 2520045 | solution.py:25
  108.4 1.0 fusion.83
  109.5 1.2 fusion.84
  110.7 1.0 fusion.83
  111.8 1.2 fusion.84
  113.1 1.0 fusion.83
  114.1 1.2 fusion.84
  115.4 1.0 fusion.83
  116.4 1.2 fusion.84
  118.7 1.2 fusion.84
  121.1 1.2 fusion.84
  123.4 1.2 fusion.84
  125.7 1.2 fusion.84
  126.9 5.3 %multiply_reduce_fusion = (f32[2048]{0:T(1024)S(1)}, f32[1024]{0:T(1024)S(1)}, f32[1024,2048]{1,0:T(8,128)}) fusion(bf16[2048,300]{0,1:T(8,128)(2,1)S(1)} %copy-done, bf16[1024,300]{0,1:T(8,128)(2,1)S(1)} %copy-done.1, f32[300,300]{0,1:T(8,128)S(1)} %get-tuple-element.35), kind=kOutput, calls=%fused_computation.14 | convolution fusion | flops 1449296768 | bytes 10604096 | tf_op jit(solution)/shard_map/dot_general | solution.py:225
  132.2 5.3 %exponential_reduce_fusion = (f32[2048]{0:T(1024)S(1)}, f32[1024]{0:T(1024)S(1)}) fusion(f32[1024,2048]{1,0:T(8,128)} %get-tuple-element.80, f32[2048]{0:T(1024)S(1)} %get-tuple-element.53, f32[1024]{0:T(1024)S(1)} %get-tuple-element.54), kind=kLoop, calls=%fused_computation.8 | loop fusion | flops 10482688 | bytes 8413184 | tf_op jit(solution)/shard_map/reduce_sum | solution.py:233
  138.8 22.2 %shard_map.60 = (f32[8,16,128]{2,1,0:T(8,128)}, f32[32,32,128]{2,1,0:T(8,128)}) custom-call(f32[16,128]{1,0:T(8,128)} %reshape.81.row_ref, f32[32,128]{1,0:T(8,128)} %reshape.82.col_ref), custom_call_target="tpu_custom_call" | custom-call | tf_op jit(solution)/shard_map/pallas_call | solution.py:195
  161.9 6.6 %fusion.7 = f32[1024,300]{0,1:T(8,128)} fusion(bf16[2048,300]{0,1:T(8,128)(2,1)S(1)} %copy-done, f32[1024,2048]{1,0:T(8,128)} %get-tuple-element.80, f32[1024]{0:T(1024)S(1)} %fusion.26, f32[1024]{0:T(1024)S(1)} %get-tuple-element.73), kind=kOutput, calls=%fused_computation.21 | convolution fusion | flops 1266679808 | bytes 10854400 | tf_op jit(solution)/shard_map/dot_general | solution.py:237
  168.5 2.4 convolution_bitcast_fusion
  171.9 6.4 %fusion.39 = (bf16[2048,300]{0,1:T(8,128)(2,1)}, f32[2048,300]{0,1:T(8,128)S(1)}) fusion(bf16[1024,300]{0,1:T(8,128)(2,1)S(1)} %copy-done.1, f32[1024,2048]{1,0:T(8,128)} %get-tuple-element.80, f32[2048]{0:T(1024)S(1)} %fusion.14, f32[2048]{0:T(1024)S(1)} %get-tuple-element.67), kind=kOutput, calls=%fused_computation.68 | convolution fusion | flops 1267294208 | bytes 12705792 | tf_op jit(solution)/shard_map/dot_general | solution.py:238
  178.3 2.1 convolution_add_fusion
  181.8 1.8 copy.24
  183.7 4.0 %reshape.87.refs_1_ = bf16[32,150,128]{2,1,0:T(8,128)(2,1)} reshape(bf16[2048,300]{1,0:T(8,128)(2,1)S(1)} %copy.24) | data formatting | bytes 2457600 | tf_op jit(solution)/shard_map/reshape | solution.py:125
  187.7 89.6 %shard_map.61 = (f32[32,24,128]{2,1,0:T(8,128)}, bf16[32,150,128]{2,1,0:T(8,128)(2,1)}) custom-call(f32[32,24,128]{2,1,0:T(8,128)} %bitcast.121, bf16[32,150,128]{2,1,0:T(8,128)(2,1)} %reshape.87.refs_1_), custom_call_target="tpu_custom_call" | custom-call | tf_op jit(solution)/shard_map/pallas_call | solution.py:126
  277.3 5.4 %reshape.88 = bf16[2048,300]{1,0:T(8,128)(2,1)S(1)} reshape(bf16[32,150,128]{2,1,0:T(8,128)(2,1)} %get-tuple-element.38) | data formatting | bytes 2457600 | tf_op jit(solution)/shard_map/reshape | solution.py:136
  282.7 1.5 copy.26
  284.2 1.7 multiply_reduce_fusion.4
  288.3 18.6 %while.21 = (s32[]{:T(128)}, f32[300,300]{0,1:T(8,128)S(1)}, s32[]{:T(128)}) while((s32[]{:T(128)}, f32[300,300]{0,1:T(8,128)S(1)}, s32[]{:T(128)}) %tuple.57), condition=%wide.region_22.23_spmd, body=%wide.region_21.22_spmd.sunk | while | flops 648270016 | bytes 2520045 | solution.py:25
  289.4 1.2 fusion.90
  290.7 1.0 fusion.89
  291.7 1.2 fusion.90
  294.1 1.2 fusion.90
  296.4 1.2 fusion.90
  298.7 1.2 fusion.90
  301.0 1.2 fusion.90
  303.4 1.2 fusion.90
  305.7 1.2 fusion.90
  307.9 1.6 convert_element_type.43
  (69 shorter events, 24.4 us)
Async XLA Ops:
  7.2 1.3 copy-start
  7.2 300.7 %reduce-scatter.2.cloned.1.call-start = ((), (), s32[]{:S(2)}) async-start(), calls=%async_computation.1 | async-start | bytes 1400832 | tf_op jit(solution)/shard_map/reduce_scatter | solution.py:244
  15.8 34.2 %copy-start.1 = (bf16[1024,300]{0,1:T(8,128)(2,1)S(1)}, bf16[1024,300]{0,1:T(8,128)(2,1)}, u32[]{:S(2)}) copy-start(bf16[1024,300]{0,1:T(8,128)(2,1)} %param.7) | copy-start | bytes 1843204
  50.0 8.1 %copy-start.3 = (f32[8,16,128]{2,1,0:T(8,128)S(1)}, f32[8,16,128]{2,1,0:T(8,128)}, u32[]{:S(2)}) copy-start(f32[8,16,128]{2,1,0:T(8,128)} %get-tuple-element.33) | copy-start | bytes 196612
  161.9 9.0 %copy-start.2 = (f32[32,32,128]{2,1,0:T(8,128)S(1)}, f32[32,32,128]{2,1,0:T(8,128)}, u32[]{:S(2)}) copy-start(f32[32,32,128]{2,1,0:T(8,128)} %get-tuple-element.37) | copy-start | bytes 1572868
Sparse Core Ops, SparseCore 0:
  168.7 30.5 reduce-scatter.1

commit v6 on v5

--- a/solution.py
+++ b/solution.py
@@ -16,7 +16,7 @@
 
 
 def polar_steps(covariance):
-    highest = lax.Precision.HIGHEST
+    highest = lax.Precision.HIGH
     current = covariance / jnp.sqrt(jnp.sum(covariance * covariance) + 1e-06)
 
     def newton(step, current):

time: 323 us -> 307 us (0.950)
  matrix products: 81.9 us -> 67.3 us
    dot_general x16, matrix products: 19.5 us -> 11.8 us  [newton(): jnp.dot(current, gram_matrix, precision=highest)]
    dot_general x16, matrix products: 16.5 us -> 9.59 us  [newton(): gram_matrix = jnp.dot(current.T, current, precision=highest)]
  transfers between devices with their start and end apart: 1 -> 1, of which waited for: 0 -> 0; matrix products, arithmetic and copies ran while one was open for 15% -> 14% of each run, Pallas kernels for 28% -> 30%
where the time goes in v6:
time: 307 us; the launch traced here: 301 us
  Pallas kernels  173 us (56%)
  matrix products  67.3 us (22%)
  local copies, waits for them, and re-layouts  24.7 us (8%)
  other arithmetic  19.4 us (6%)
  between operations  15.9 us (5%)
    pallas_call x1, Pallas kernels, all_reduce(): pl.pallas_call(functools.partial(all_reduce_kernel, n_src, n_tgt, True),...  89.7 us
    pallas_call x2, Pallas kernels, gather_stats(): pl.pallas_call(functools.partial(stats_gather_kernel, n_src, n_tgt), out_...  47.5 us
    pallas_call x1, Pallas kernels, all_reduce(): pl.pallas_call(functools.partial(all_reduce_kernel, n_src, n_tgt, False),...  36.3 us
    dot_general x2, matrix products, body(): lax.dot_general(mapped, target, (((1,), (1,)), ((), ())), preferred_eleme...  12.6 us
    dot_general x2, matrix products, body(): lax.dot_general(col_weights, source, (((0,), (0,)), ((), ())), preferred_...  12.2 us
    dot_general x16, matrix products, newton(): jnp.dot(current, gram_matrix, precision=highest)  11.8 us
    dot_general x2, matrix products, body(): jnp.dot(row_weights, target, preferred_element_type=jnp.float32)  11.6 us
    reduce_sum x2, other arithmetic, body(): col_part = jnp.sum(jnp.exp(scores - col_local[None, :]), axis=0)  10.8 us
  transfers between devices with their start and end apart: 1, of which 0 were waited for; matrix products, arithmetic and copies ran while one was open for 14% of the time, Pallas kernels for 30%

profile of v6, /device:TPU:2, one launch (start us, length us, event | category | flops | bytes accessed | tf_op | source)
XLA Modules:
  0.0 301.4 jit_solution(4587663815972907900)
XLA Ops:
  7.2 1.2 copy-done
  8.5 7.3 %multiply_reduce_fusion.2 = (f32[2048]{0:T(1024)S(1)}, f32[1024]{0:T(1024)S(1)}, f32[1024,2048]{1,0:T(8,128)}) fusion(bf16[2048,300]{0,1:T(8,128)(2,1)S(1)} %copy-done, bf16[1024,300]{0,1:T(8,128)(2,1)} %param.7, f32[300,300]{1,0:T(8,128)} %param.9), kind=kOutput, calls=%fused_computation.16 | convolution fusion | flops 1449296768 | bytes 10604096 | tf_op jit(solution)/shard_map/dot_general | solution.py:225
  15.8 5.6 %exponential_reduce_fusion.2 = (f32[2048]{0:T(1024)S(1)}, f32[1024]{0:T(1024)S(1)}) fusion(f32[1024,2048]{1,0:T(8,128)} %get-tuple-element.79, f32[2048]{0:T(1024)S(1)} %get-tuple-element.57, f32[1024]{0:T(1024)S(1)} %get-tuple-element.58), kind=kLoop, calls=%fused_computation.12 | loop fusion | flops 10482688 | bytes 8413184 | tf_op jit(solution)/shard_map/reduce_sum | solution.py:233
  22.6 25.3 %shard_map.58 = (f32[8,16,128]{2,1,0:T(8,128)}, f32[32,32,128]{2,1,0:T(8,128)}) custom-call(f32[16,128]{1,0:T(8,128)} %reshape.74.row_ref, f32[32,128]{1,0:T(8,128)} %reshape.75.col_ref), custom_call_target="tpu_custom_call" | custom-call | tf_op jit(solution)/shard_map/pallas_call | solution.py:195
  48.0 1.3 reshape.77
  50.0 5.9 %fusion.4 = f32[2048,300]{1,0:T(8,128)S(1)} fusion(bf16[1024,300]{0,1:T(8,128)(2,1)S(1)} %copy-done.1, f32[1024,2048]{1,0:T(8,128)} %get-tuple-element.79, f32[2048]{0:T(1024)S(1)} %fusion.18, f32[2048]{0:T(1024)S(1)} %get-tuple-element.70), kind=kOutput, calls=%fused_computation.18 | convolution fusion | flops 1266679808 | bytes 11476992 | tf_op jit(solution)/shard_map/dot_general | solution.py:238
  55.8 2.2 fusion.42
  58.2 5.1 %fusion.6 = f32[1024,300]{1,0:T(8,128)S(1)} fusion(bf16[2048,300]{0,1:T(8,128)(2,1)S(1)} %copy-done, f32[1024,2048]{1,0:T(8,128)} %get-tuple-element.79, f32[1024]{0:T(1024)S(1)} %fusion.30, f32[1024]{0:T(1024)S(1)} %get-tuple-element.76), kind=kOutput, calls=%fused_computation.20 | convolution fusion | flops 1266679808 | bytes 10854400 | tf_op jit(solution)/shard_map/dot_general | solution.py:237
  63.3 2.6 fusion.10
  66.6 0.8 pad.7
  67.4 36.3 %shard_map.59 = f32[32,24,128]{2,1,0:T(8,128)} custom-call(f32[32,24,128]{2,1,0:T(8,128)} %bitcast.120), custom_call_target="tpu_custom_call" | custom-call | tf_op jit(solution)/shard_map/pallas_call | solution.py:115
  103.7 1.7 multiply_reduce_fusion.5
  106.1 1.0 slice_divide_fusion.1
  107.8 11.3 %while.20 = (s32[]{:T(128)}, f32[300,300]{0,1:T(8,128)S(1)}, s32[]{:T(128)}) while((s32[]{:T(128)}, f32[300,300]{0,1:T(8,128)S(1)}, s32[]{:T(128)}) %tuple.54), condition=%wide.region_10.11_spmd, body=%wide.region_9.10_spmd.sunk | while | flops 324270016 | bytes 2520045 | solution.py:25
  108.4 0.7 fusion.84
  111.2 0.7 fusion.84
  112.6 0.7 fusion.84
  114.1 0.7 fusion.84
  115.5 0.7 fusion.84
  116.9 0.7 fusion.84
  118.3 0.7 fusion.84
  119.0 5.3 %multiply_reduce_fusion = (f32[2048]{0:T(1024)S(1)}, f32[1024]{0:T(1024)S(1)}, f32[1024,2048]{1,0:T(8,128)}) fusion(bf16[2048,300]{0,1:T(8,128)(2,1)S(1)} %copy-done, bf16[1024,300]{0,1:T(8,128)(2,1)S(1)} %copy-done.1, f32[300,300]{0,1:T(8,128)S(1)} %get-tuple-element.35), kind=kOutput, calls=%fused_computation.14 | convolution fusion | flops 1449296768 | bytes 10604096 | tf_op jit(solution)/shard_map/dot_general | solution.py:225
  124.3 5.3 %exponential_reduce_fusion = (f32[2048]{0:T(1024)S(1)}, f32[1024]{0:T(1024)S(1)}) fusion(f32[1024,2048]{1,0:T(8,128)} %get-tuple-element.80, f32[2048]{0:T(1024)S(1)} %get-tuple-element.53, f32[1024]{0:T(1024)S(1)} %get-tuple-element.54), kind=kLoop, calls=%fused_computation.8 | loop fusion | flops 10482688 | bytes 8413184 | tf_op jit(solution)/shard_map/reduce_sum | solution.py:233
  130.9 22.2 %shard_map.60 = (f32[8,16,128]{2,1,0:T(8,128)}, f32[32,32,128]{2,1,0:T(8,128)}) custom-call(f32[16,128]{1,0:T(8,128)} %reshape.81.row_ref, f32[32,128]{1,0:T(8,128)} %reshape.82.col_ref), custom_call_target="tpu_custom_call" | custom-call | tf_op jit(solution)/shard_map/pallas_call | solution.py:195
  153.0 0.9 reshape.83
  154.0 6.6 %fusion.7 = f32[1024,300]{0,1:T(8,128)} fusion(bf16[2048,300]{0,1:T(8,128)(2,1)S(1)} %copy-done, f32[1024,2048]{1,0:T(8,128)} %get-tuple-element.80, f32[1024]{0:T(1024)S(1)} %fusion.26, f32[1024]{0:T(1024)S(1)} %get-tuple-element.73), kind=kOutput, calls=%fused_computation.21 | convolution fusion | flops 1266679808 | bytes 10854400 | tf_op jit(solution)/shard_map/dot_general | solution.py:237
  160.6 2.4 convolution_bitcast_fusion
  164.0 6.4 %fusion.39 = (bf16[2048,300]{0,1:T(8,128)(2,1)}, f32[2048,300]{0,1:T(8,128)S(1)}) fusion(bf16[1024,300]{0,1:T(8,128)(2,1)S(1)} %copy-done.1, f32[1024,2048]{1,0:T(8,128)} %get-tuple-element.80, f32[2048]{0:T(1024)S(1)} %fusion.14, f32[2048]{0:T(1024)S(1)} %get-tuple-element.67), kind=kOutput, calls=%fused_computation.68 | convolution fusion | flops 1267294208 | bytes 12705792 | tf_op jit(solution)/shard_map/dot_general | solution.py:238
  170.4 2.1 convolution_add_fusion
  173.2 0.8 pad.8
  173.9 1.8 copy.24
  175.8 4.0 %reshape.87.refs_1_ = bf16[32,150,128]{2,1,0:T(8,128)(2,1)} reshape(bf16[2048,300]{1,0:T(8,128)(2,1)S(1)} %copy.24) | data formatting | bytes 2457600 | tf_op jit(solution)/shard_map/reshape | solution.py:125
  179.8 89.7 %shard_map.61 = (f32[32,24,128]{2,1,0:T(8,128)}, bf16[32,150,128]{2,1,0:T(8,128)(2,1)}) custom-call(f32[32,24,128]{2,1,0:T(8,128)} %bitcast.121, bf16[32,150,128]{2,1,0:T(8,128)(2,1)} %reshape.87.refs_1_), custom_call_target="tpu_custom_call" | custom-call | tf_op jit(solution)/shard_map/pallas_call | solution.py:126
  269.5 5.4 %reshape.88 = bf16[2048,300]{1,0:T(8,128)(2,1)S(1)} reshape(bf16[32,150,128]{2,1,0:T(8,128)(2,1)} %get-tuple-element.38) | data formatting | bytes 2457600 | tf_op jit(solution)/shard_map/reshape | solution.py:136
  274.9 1.5 copy.26
  276.4 1.7 multiply_reduce_fusion.4
  278.8 1.0 slice_divide_fusion
  280.5 11.3 %while.21 = (s32[]{:T(128)}, f32[300,300]{0,1:T(8,128)S(1)}, s32[]{:T(128)}) while((s32[]{:T(128)}, f32[300,300]{0,1:T(8,128)S(1)}, s32[]{:T(128)}) %tuple.57), condition=%wide.region_22.23_spmd, body=%wide.region_21.22_spmd.sunk | while | flops 324270016 | bytes 2520045 | solution.py:25
  281.1 0.7 fusion.90
  282.5 0.7 fusion.90
  284.0 0.7 fusion.90
  285.4 0.7 fusion.90
  286.8 0.7 fusion.90
  288.2 0.7 fusion.90
  289.6 0.7 fusion.90
  291.0 0.7 fusion.90
  291.8 1.0 copy.27
  292.7 1.6 convert_element_type.43
  (69 shorter events, 17.9 us)
Async XLA Ops:
  7.2 1.3 copy-start
  7.2 285.6 %reduce-scatter.2.cloned.1.call-start = ((), (), s32[]{:S(2)}) async-start(), calls=%async_computation.1 | async-start | bytes 1400832 | tf_op jit(solution)/shard_map/reduce_scatter | solution.py:244
  15.8 34.2 %copy-start.1 = (bf16[1024,300]{0,1:T(8,128)(2,1)S(1)}, bf16[1024,300]{0,1:T(8,128)(2,1)}, u32[]{:S(2)}) copy-start(bf16[1024,300]{0,1:T(8,128)(2,1)} %param.7) | copy-start | bytes 1843204
  50.0 8.1 %copy-start.3 = (f32[8,16,128]{2,1,0:T(8,128)S(1)}, f32[8,16,128]{2,1,0:T(8,128)}, u32[]{:S(2)}) copy-start(f32[8,16,128]{2,1,0:T(8,128)} %get-tuple-element.33) | copy-start | bytes 196612
  154.0 9.0 %copy-start.2 = (f32[32,32,128]{2,1,0:T(8,128)S(1)}, f32[32,32,128]{2,1,0:T(8,128)}, u32[]{:S(2)}) copy-start(f32[32,32,128]{2,1,0:T(8,128)} %get-tuple-element.37) | copy-start | bytes 1572868
Sparse Core Ops, SparseCore 0:
  160.8 30.6 reduce-scatter.1

commit v7 on v6

--- a/solution.py
+++ b/solution.py
@@ -68,8 +68,8 @@
 
 def all_reduce_kernel(n_src, n_tgt, with_target, *refs):
     if with_target:
-        (xc, xt, oc, ot, gather_src, gather_tgt, gather_t,
-         s_a, r_a, s_b, r_b, s_c, r_c, s_ta, r_ta, s_tc, r_tc) = refs
+        (xc, xt, oc, ot, gather_src, gather_tgt, g1, g2, s1,
+         s_a, r_a, s_b, r_b, s_c, r_c, s_1, r_1, s_2, r_2, s_3, r_3, s_4, r_4) = refs
     else:
         xc, oc, gather_src, gather_tgt, s_a, r_a, s_b, r_b, s_c, r_c = refs
     me_s = lax.axis_index("src")
@@ -79,26 +79,39 @@
     on_tgt = lambda k: (me_s, k)
 
     if with_target:
-        start_all(me_s, n_src, on_src, lambda k: xt.at[k], lambda i: gather_t.at[i], s_ta, r_ta)
-        gather_t[me_s] = xt[me_s]
+        n_y, n_z = xt.shape[0], xt.shape[1]
+        my_z = me_s // n_y
+        my_y = me_s % n_y
+        on_y = lambda k: (my_z * n_y + k, me_t)
+        on_z = lambda k: (k * n_y + my_y, me_t)
+        start_all(my_y, n_y, on_y, lambda k: xt.at[k], lambda i: g1.at[i], s_1, r_1)
+        g1[my_y] = xt[my_y]
 
     start_all(me_s, n_src, on_src, lambda k: xc.at[k], lambda i: gather_src.at[i], s_a, r_a)
     gather_src[me_s] = xc[me_s]
     wait_all(me_s, n_src, on_src, lambda k: xc.at[k], lambda i: gather_src.at[i], s_a, r_a)
     gather_tgt[me_t] = jnp.sum(gather_src[...], axis=0)
 
+    if with_target:
+        wait_all(my_y, n_y, on_y, lambda k: xt.at[k], lambda i: g1.at[i], s_1, r_1)
+        s1[...] = jnp.sum(g1[...].astype(jnp.float32), axis=0).astype(s1.dtype)
+        start_all(my_z, n_z, on_z, lambda k: s1.at[k], lambda i: g2.at[i], s_2, r_2)
+        g2[my_z] = s1[my_z]
+
     start_all(me_t, n_tgt, on_tgt, lambda k: gather_tgt.at[me_t], lambda i: gather_tgt.at[i], s_b, r_b)
     wait_all(me_t, n_tgt, on_tgt, lambda k: gather_tgt.at[me_t], lambda i: gather_tgt.at[i], s_b, r_b)
     oc[me_s] = jnp.sum(gather_tgt[...], axis=0)
-
     start_all(me_s, n_src, on_src, lambda k: oc.at[me_s], lambda i: oc.at[i], s_c, r_c)
-    if with_target:
-        wait_all(me_s, n_src, on_src, lambda k: xt.at[k], lambda i: gather_t.at[i], s_ta, r_ta)
-        ot[me_s] = jnp.sum(gather_t[...].astype(jnp.float32), axis=0).astype(ot.dtype)
-        start_all(me_s, n_src, on_src, lambda k: ot.at[me_s], lambda i: ot.at[i], s_tc, r_tc)
+
+    if with_target:
+        wait_all(my_z, n_z, on_z, lambda k: s1.at[k], lambda i: g2.at[i], s_2, r_2)
+        ot[my_y, my_z] = jnp.sum(g2[...].astype(jnp.float32), axis=0).astype(ot.dtype)
+        start_all(my_z, n_z, on_z, lambda k: ot.at[my_y, my_z], lambda i: ot.at[my_y, i], s_3, r_3)
     wait_all(me_s, n_src, on_src, lambda k: oc.at[me_s], lambda i: oc.at[i], s_c, r_c)
     if with_target:
-        wait_all(me_s, n_src, on_src, lambda k: ot.at[me_s], lambda i: ot.at[i], s_tc, r_tc)
+        wait_all(my_z, n_z, on_z, lambda k: ot.at[my_y, my_z], lambda i: ot.at[my_y, i], s_3, r_3)
+        start_all(my_y, n_y, on_y, lambda k: ot.at[my_y], lambda i: ot.at[i], s_4, r_4)
+        wait_all(my_y, n_y, on_y, lambda k: ot.at[my_y], lambda i: ot.at[i], s_4, r_4)
 
 
 def all_reduce(matrix, target_part=None):
@@ -122,18 +135,25 @@
         )(flat)
         return out.reshape(-1)[:size].reshape(matrix.shape)
     t_rows, width = target_part.shape
-    chunks = target_part.astype(jnp.bfloat16).reshape(n_src, t_rows * width // (n_src * 128), 128)
+    n_y = 4 if n_src % 4 == 0 else n_src
+    n_z = n_src // n_y
+    lanes = t_rows * width // (n_src * 128)
+    chunks = target_part.astype(jnp.bfloat16).reshape(n_z, n_y, lanes, 128).transpose(1, 0, 2, 3)
     out, target_sum = pl.pallas_call(
         functools.partial(all_reduce_kernel, n_src, n_tgt, True),
         out_shape=(jax.ShapeDtypeStruct(flat.shape, jnp.float32),
                    jax.ShapeDtypeStruct(chunks.shape, jnp.bfloat16)),
         in_specs=[vmem, vmem],
         out_specs=(vmem, vmem),
-        scratch_shapes=scratch + [pltpu.VMEM(chunks.shape, jnp.bfloat16)] + sems
-        + [pltpu.SemaphoreType.DMA((n_src,)) for _ in range(4)],
+        scratch_shapes=scratch
+        + [pltpu.VMEM(chunks.shape, jnp.bfloat16), pltpu.VMEM((n_z, lanes, 128), jnp.bfloat16),
+           pltpu.VMEM((n_z, lanes, 128), jnp.bfloat16)]
+        + sems
+        + [pltpu.SemaphoreType.DMA((n,)) for n in (n_y, n_y, n_z, n_z, n_z, n_z, n_y, n_y)],
         compiler_params=pltpu.CompilerParams(collective_id=1, has_side_effects=True),
     )(flat, chunks)
-    return out.reshape(-1)[:size].reshape(matrix.shape), target_sum.reshape(t_rows, width)
+    target_sum = target_sum.transpose(1, 0, 2, 3).reshape(t_rows, width)
+    return out.reshape(-1)[:size].reshape(matrix.shape), target_sum
 
 
 def stats_gather_kernel(n_src, n_tgt, row_ref, col_ref, row_out, col_out,

time: 307 us -> 292 us (0.951)
  Pallas kernels: 173 us -> 154 us
  local copies, waits for them, and re-layouts: 24.7 us -> 30.4 us
    pallas_call x1, Pallas kernels: 89.7 us -> 69.7 us  [all_reduce(): pl.pallas_call(functools.partial(all_reduce_kernel, n_src, n_tgt, True),...]
    reshape x2 -> x3, local copies, waits for them, and re-layouts: 9.39 us -> 11.6 us  [the longest x2 6.43 us: all_reduce(): target_part.astype(jnp.bfloat16).reshape(n_z, n_y, lanes, 128)]
  transfers between devices with their start and end apart: 1 -> 1, of which waited for: 0 -> 0; matrix products, arithmetic and copies ran while one was open for 14% -> 16% of each run, Pallas kernels for 30% -> 24%
where the time goes in v7:
time: 292 us; the launch traced here: 286 us
  Pallas kernels  154 us (53%)
  matrix products  67.3 us (23%)
  local copies, waits for them, and re-layouts  30.4 us (10%)
  other arithmetic  18.4 us (6%)
  between operations  15.9 us (5%)
    pallas_call x1, Pallas kernels, all_reduce(): pl.pallas_call(functools.partial(all_reduce_kernel, n_src, n_tgt, True),...  69.7 us
    pallas_call x2, Pallas kernels, gather_stats(): pl.pallas_call(functools.partial(stats_gather_kernel, n_src, n_tgt), out_...  47.5 us
    pallas_call x1, Pallas kernels, all_reduce(): pl.pallas_call(functools.partial(all_reduce_kernel, n_src, n_tgt, False),...  36.4 us
    dot_general x2, matrix products, body(): lax.dot_general(mapped, target, (((1,), (1,)), ((), ())), preferred_eleme...  12.6 us
    dot_general x2, matrix products, body(): lax.dot_general(col_weights, source, (((0,), (0,)), ((), ())), preferred_...  12.2 us
    dot_general x16, matrix products, newton(): jnp.dot(current, gram_matrix, precision=highest)  11.8 us
    dot_general x2, matrix products, body(): jnp.dot(row_weights, target, preferred_element_type=jnp.float32)  11.6 us
    reduce_sum x2, other arithmetic, body(): col_part = jnp.sum(jnp.exp(scores - col_local[None, :]), axis=0)  10.8 us
  transfers between devices with their start and end apart: 1, of which 0 were waited for; matrix products, arithmetic and copies ran while one was open for 16% of the time, Pallas kernels for 24%

profile of v7, /device:TPU:2, one launch (start us, length us, event | category | flops | bytes accessed | tf_op | source)
XLA Modules:
  0.0 286.2 jit_solution(5275136493048682021)
XLA Ops:
  7.2 1.2 copy-done
  8.5 7.3 %multiply_reduce_fusion.2 = (f32[2048]{0:T(1024)S(1)}, f32[1024]{0:T(1024)S(1)}, f32[1024,2048]{1,0:T(8,128)}) fusion(bf16[2048,300]{0,1:T(8,128)(2,1)S(1)} %copy-done, bf16[1024,300]{0,1:T(8,128)(2,1)} %param.7, f32[300,300]{1,0:T(8,128)} %param.9), kind=kOutput, calls=%fused_computation.16 | convolution fusion | flops 1449296768 | bytes 10604096 | tf_op jit(solution)/shard_map/dot_general | solution.py:245
  15.8 5.6 %exponential_reduce_fusion.2 = (f32[2048]{0:T(1024)S(1)}, f32[1024]{0:T(1024)S(1)}) fusion(f32[1024,2048]{1,0:T(8,128)} %get-tuple-element.79, f32[2048]{0:T(1024)S(1)} %get-tuple-element.57, f32[1024]{0:T(1024)S(1)} %get-tuple-element.58), kind=kLoop, calls=%fused_computation.12 | loop fusion | flops 10482688 | bytes 8413184 | tf_op jit(solution)/shard_map/reduce_sum | solution.py:253
  22.6 25.3 %shard_map.58 = (f32[8,16,128]{2,1,0:T(8,128)}, f32[32,32,128]{2,1,0:T(8,128)}) custom-call(f32[16,128]{1,0:T(8,128)} %reshape.74.row_ref, f32[32,128]{1,0:T(8,128)} %reshape.75.col_ref), custom_call_target="tpu_custom_call" | custom-call | tf_op jit(solution)/shard_map/pallas_call | solution.py:215
  48.0 1.3 reshape.77
  50.0 5.9 %fusion.4 = f32[2048,300]{1,0:T(8,128)S(1)} fusion(bf16[1024,300]{0,1:T(8,128)(2,1)S(1)} %copy-done.1, f32[1024,2048]{1,0:T(8,128)} %get-tuple-element.79, f32[2048]{0:T(1024)S(1)} %fusion.18, f32[2048]{0:T(1024)S(1)} %get-tuple-element.70), kind=kOutput, calls=%fused_computation.18 | convolution fusion | flops 1266679808 | bytes 11476992 | tf_op jit(solution)/shard_map/dot_general | solution.py:258
  55.9 2.2 fusion.42
  58.2 5.1 %fusion.6 = f32[1024,300]{1,0:T(8,128)S(1)} fusion(bf16[2048,300]{0,1:T(8,128)(2,1)S(1)} %copy-done, f32[1024,2048]{1,0:T(8,128)} %get-tuple-element.79, f32[1024]{0:T(1024)S(1)} %fusion.30, f32[1024]{0:T(1024)S(1)} %get-tuple-element.76), kind=kOutput, calls=%fused_computation.20 | convolution fusion | flops 1266679808 | bytes 10854400 | tf_op jit(solution)/shard_map/dot_general | solution.py:257
  63.3 2.7 fusion.10
  66.6 0.8 pad.7
  67.4 36.4 %shard_map.59 = f32[32,24,128]{2,1,0:T(8,128)} custom-call(f32[32,24,128]{2,1,0:T(8,128)} %bitcast.125), custom_call_target="tpu_custom_call" | custom-call | tf_op jit(solution)/shard_map/pallas_call | solution.py:128
  103.8 1.7 multiply_reduce_fusion.5
  106.2 1.0 slice_divide_fusion.1
  107.9 11.3 %while.20 = (s32[]{:T(128)}, f32[300,300]{0,1:T(8,128)S(1)}, s32[]{:T(128)}) while((s32[]{:T(128)}, f32[300,300]{0,1:T(8,128)S(1)}, s32[]{:T(128)}) %tuple.54), condition=%wide.region_10.11_spmd, body=%wide.region_9.10_spmd.sunk | while | flops 324270016 | bytes 2520045 | solution.py:25
  108.5 0.7 fusion.84
  110.0 0.7 fusion.84
  111.4 0.7 fusion.84
  112.8 0.7 fusion.84
  114.2 0.7 fusion.84
  115.6 0.7 fusion.84
  117.0 0.7 fusion.84
  118.4 0.7 fusion.84
  119.2 5.3 %multiply_reduce_fusion = (f32[2048]{0:T(1024)S(1)}, f32[1024]{0:T(1024)S(1)}, f32[1024,2048]{1,0:T(8,128)}) fusion(bf16[2048,300]{0,1:T(8,128)(2,1)S(1)} %copy-done, bf16[1024,300]{0,1:T(8,128)(2,1)S(1)} %copy-done.1, f32[300,300]{0,1:T(8,128)S(1)} %get-tuple-element.35), kind=kOutput, calls=%fused_computation.14 | convolution fusion | flops 1449296768 | bytes 10604096 | tf_op jit(solution)/shard_map/dot_general | solution.py:245
  124.5 5.3 %exponential_reduce_fusion = (f32[2048]{0:T(1024)S(1)}, f32[1024]{0:T(1024)S(1)}) fusion(f32[1024,2048]{1,0:T(8,128)} %get-tuple-element.80, f32[2048]{0:T(1024)S(1)} %get-tuple-element.53, f32[1024]{0:T(1024)S(1)} %get-tuple-element.54), kind=kLoop, calls=%fused_computation.8 | loop fusion | flops 10482688 | bytes 8413184 | tf_op jit(solution)/shard_map/reduce_sum | solution.py:253
  131.0 22.1 %shard_map.60 = (f32[8,16,128]{2,1,0:T(8,128)}, f32[32,32,128]{2,1,0:T(8,128)}) custom-call(f32[16,128]{1,0:T(8,128)} %reshape.81.row_ref, f32[32,128]{1,0:T(8,128)} %reshape.82.col_ref), custom_call_target="tpu_custom_call" | custom-call | tf_op jit(solution)/shard_map/pallas_call | solution.py:215
  153.1 0.9 reshape.83
  154.1 6.5 %fusion.7 = f32[1024,300]{0,1:T(8,128)} fusion(bf16[2048,300]{0,1:T(8,128)(2,1)S(1)} %copy-done, f32[1024,2048]{1,0:T(8,128)} %get-tuple-element.80, f32[1024]{0:T(1024)S(1)} %fusion.26, f32[1024]{0:T(1024)S(1)} %get-tuple-element.73), kind=kOutput, calls=%fused_computation.21 | convolution fusion | flops 1266679808 | bytes 10854400 | tf_op jit(solution)/shard_map/dot_general | solution.py:257
  160.7 2.4 convolution_bitcast_fusion
  163.1 1.3 reshape.84
  165.1 6.4 %fusion.39 = (bf16[2048,300]{0,1:T(8,128)(2,1)}, f32[2048,300]{0,1:T(8,128)S(1)}) fusion(bf16[1024,300]{0,1:T(8,128)(2,1)S(1)} %copy-done.1, f32[1024,2048]{1,0:T(8,128)} %get-tuple-element.80, f32[2048]{0:T(1024)S(1)} %fusion.14, f32[2048]{0:T(1024)S(1)} %get-tuple-element.67), kind=kOutput, calls=%fused_computation.69 | convolution fusion | flops 1267294208 | bytes 12705792 | tf_op jit(solution)/shard_map/dot_general | solution.py:258
  171.5 2.1 convolution_add_fusion
  174.3 0.8 pad.8
  175.0 1.8 copy.22
  176.9 4.0 %reshape.87 = bf16[8,4,150,128]{3,2,1,0:T(8,128)(2,1)} reshape(bf16[2048,300]{1,0:T(8,128)(2,1)S(1)} %copy.22) | data formatting | bytes 2457600 | tf_op jit(solution)/shard_map/reshape | solution.py:141
  180.9 2.4 copy.83
  183.3 69.7 %shard_map.61 = (f32[32,24,128]{2,1,0:T(8,128)}, bf16[4,8,150,128]{3,2,1,0:T(8,128)(2,1)}) custom-call(f32[32,24,128]{2,1,0:T(8,128)} %bitcast.126, bf16[4,8,150,128]{3,2,1,0:T(8,128)(2,1)} %bitcast.122), custom_call_target="tpu_custom_call" | custom-call | tf_op jit(solution)/shard_map/pallas_call | solution.py:142
  253.0 2.5 copy.24
  255.4 5.2 %reshape.88 = bf16[2048,300]{1,0:T(8,128)(2,1)S(1)} reshape(bf16[8,4,150,128]{3,2,1,0:T(8,128)(2,1)} %copy.24) | data formatting | bytes 2457600 | tf_op jit(solution)/shard_map/reshape | solution.py:155
  260.6 1.5 copy.26
  262.2 1.7 multiply_reduce_fusion.4
  265.3 11.3 %while.21 = (s32[]{:T(128)}, f32[300,300]{0,1:T(8,128)S(1)}, s32[]{:T(128)}) while((s32[]{:T(128)}, f32[300,300]{0,1:T(8,128)S(1)}, s32[]{:T(128)}) %tuple.57), condition=%wide.region_22.23_spmd, body=%wide.region_21.22_spmd.sunk | while | flops 324270016 | bytes 2520045 | solution.py:25
  265.9 0.7 fusion.90
  267.3 0.7 fusion.90
  268.7 0.7 fusion.90
  270.2 0.7 fusion.90
  273.0 0.7 fusion.90
  276.6 1.0 copy.27
  277.5 1.6 convert_element_type.43
  (71 shorter events, 19.2 us)
Async XLA Ops:
  7.2 1.3 copy-start
  7.2 270.4 %reduce-scatter.2.cloned.1.call-start = ((), (), s32[]{:S(2)}) async-start(), calls=%async_computation.1 | async-start | bytes 1400832 | tf_op jit(solution)/shard_map/reduce_scatter | solution.py:264
  15.8 34.2 %copy-start.1 = (bf16[1024,300]{0,1:T(8,128)(2,1)S(1)}, bf16[1024,300]{0,1:T(8,128)(2,1)}, u32[]{:S(2)}) copy-start(bf16[1024,300]{0,1:T(8,128)(2,1)} %param.7) | copy-start | bytes 1843204
  50.0 8.1 %copy-start.3 = (f32[8,16,128]{2,1,0:T(8,128)S(1)}, f32[8,16,128]{2,1,0:T(8,128)}, u32[]{:S(2)}) copy-start(f32[8,16,128]{2,1,0:T(8,128)} %get-tuple-element.33) | copy-start | bytes 196612
  252.9 11.6 %copy-start.2 = (f32[32,24,128]{2,1,0:T(8,128)S(1)}, f32[32,24,128]{2,1,0:T(8,128)}, u32[]{:S(2)}) copy-start(f32[32,24,128]{2,1,0:T(8,128)} %get-tuple-element.39) | copy-start | bytes 1179652
Sparse Core Ops, SparseCore 0:
  160.8 30.5 reduce-scatter.1

commit v8 on v7

--- a/solution.py
+++ b/solution.py
@@ -137,8 +137,8 @@
     t_rows, width = target_part.shape
     n_y = 4 if n_src % 4 == 0 else n_src
     n_z = n_src // n_y
-    lanes = t_rows * width // (n_src * 128)
-    chunks = target_part.astype(jnp.bfloat16).reshape(n_z, n_y, lanes, 128).transpose(1, 0, 2, 3)
+    piece = t_rows // n_src
+    chunks = target_part.astype(jnp.bfloat16).reshape(n_y, n_z, piece, width)
     out, target_sum = pl.pallas_call(
         functools.partial(all_reduce_kernel, n_src, n_tgt, True),
         out_shape=(jax.ShapeDtypeStruct(flat.shape, jnp.float32),
@@ -146,13 +146,13 @@
         in_specs=[vmem, vmem],
         out_specs=(vmem, vmem),
         scratch_shapes=scratch
-        + [pltpu.VMEM(chunks.shape, jnp.bfloat16), pltpu.VMEM((n_z, lanes, 128), jnp.bfloat16),
-           pltpu.VMEM((n_z, lanes, 128), jnp.bfloat16)]
+        + [pltpu.VMEM(chunks.shape, jnp.bfloat16), pltpu.VMEM((n_z, piece, width), jnp.bfloat16),
+           pltpu.VMEM((n_z, piece, width), jnp.bfloat16)]
         + sems
         + [pltpu.SemaphoreType.DMA((n,)) for n in (n_y, n_y, n_z, n_z, n_z, n_z, n_y, n_y)],
         compiler_params=pltpu.CompilerParams(collective_id=1, has_side_effects=True),
     )(flat, chunks)
-    target_sum = target_sum.transpose(1, 0, 2, 3).reshape(t_rows, width)
+    target_sum = target_sum.reshape(t_rows, width)
     return out.reshape(-1)[:size].reshape(matrix.shape), target_sum
 
 

time: 292 us -> 282 us (0.966); the launches traced: 286 us -> 281 us
  local copies, waits for them, and re-layouts: 30.4 us -> 17 us
  Pallas kernels: 154 us -> 161 us
    reshape x3 -> x0, local copies, waits for them, and re-layouts: 11.6 us -> none  [the longest x2 6.43 us: all_reduce(): target_part.astype(jnp.bfloat16).reshape(n_z, n_y, lanes, 128)]
    pallas_call x1, Pallas kernels: 69.7 us -> 78.3 us  [all_reduce(): pl.pallas_call(functools.partial(all_reduce_kernel, n_src, n_tgt, True),...]
  transfers between devices with their start and end apart: 1 -> 1, of which waited for: 0 -> 0; matrix products, arithmetic and copies ran while one was open for 16% -> 12% of each run, Pallas kernels for 24% -> 28%
where the time goes in v8:
time: 282 us; the launch traced here: 281 us
  Pallas kernels  161 us (57%)
  matrix products  67.3 us (24%)
  other arithmetic  19.1 us (7%)
  local copies, waits for them, and re-layouts  17 us (6%)
  between operations  15.7 us (6%)
    pallas_call x1, Pallas kernels, all_reduce(): pl.pallas_call(functools.partial(all_reduce_kernel, n_src, n_tgt, True),...  78.3 us
    pallas_call x2, Pallas kernels, gather_stats(): pl.pallas_call(functools.partial(stats_gather_kernel, n_src, n_tgt), out_...  47.4 us
    pallas_call x1, Pallas kernels, all_reduce(): pl.pallas_call(functools.partial(all_reduce_kernel, n_src, n_tgt, False),...  35.5 us
    dot_general x2, matrix products, body(): lax.dot_general(mapped, target, (((1,), (1,)), ((), ())), preferred_eleme...  12.6 us
    dot_general x2, matrix products, body(): lax.dot_general(col_weights, source, (((0,), (0,)), ((), ())), preferred_...  12.2 us
    dot_general x16, matrix products, newton(): jnp.dot(current, gram_matrix, precision=highest)  11.8 us
    dot_general x2, matrix products, body(): jnp.dot(row_weights, target, preferred_element_type=jnp.float32)  11.6 us
    reduce_sum x2, other arithmetic, body(): col_part = jnp.sum(jnp.exp(scores - col_local[None, :]), axis=0)  10.6 us
  transfers between devices with their start and end apart: 1, of which 0 were waited for; matrix products, arithmetic and copies ran while one was open for 12% of the time, Pallas kernels for 28%

profile of v8, /device:TPU:2, one launch (start us, length us, event | category | flops | bytes accessed | tf_op | source)
XLA Modules:
  0.0 280.8 jit_solution(17821355521453990179)
XLA Ops:
  7.2 1.2 copy-done
  8.5 7.3 %multiply_reduce_fusion.2 = (f32[2048]{0:T(1024)S(1)}, f32[1024]{0:T(1024)S(1)}, f32[1024,2048]{1,0:T(8,128)}) fusion(bf16[2048,300]{0,1:T(8,128)(2,1)S(1)} %copy-done, bf16[1024,300]{0,1:T(8,128)(2,1)} %param.7, f32[300,300]{1,0:T(8,128)} %param.9), kind=kOutput, calls=%fused_computation.16 | convolution fusion | flops 1449296768 | bytes 10604096 | tf_op jit(solution)/shard_map/dot_general | solution.py:245
  15.8 5.3 %exponential_reduce_fusion.2 = (f32[2048]{0:T(1024)S(1)}, f32[1024]{0:T(1024)S(1)}) fusion(f32[1024,2048]{1,0:T(8,128)} %get-tuple-element.79, f32[2048]{0:T(1024)S(1)} %get-tuple-element.57, f32[1024]{0:T(1024)S(1)} %get-tuple-element.58), kind=kLoop, calls=%fused_computation.12 | loop fusion | flops 10482688 | bytes 8413184 | tf_op jit(solution)/shard_map/reduce_sum | solution.py:253
  21.7 0.6 reshape.75.col_ref
  22.3 25.3 %shard_map.58 = (f32[8,16,128]{2,1,0:T(8,128)}, f32[32,32,128]{2,1,0:T(8,128)}) custom-call(f32[16,128]{1,0:T(8,128)} %reshape.74.row_ref, f32[32,128]{1,0:T(8,128)} %reshape.75.col_ref), custom_call_target="tpu_custom_call" | custom-call | tf_op jit(solution)/shard_map/pallas_call | solution.py:215
  47.7 1.3 reshape.77
  49.7 5.9 %fusion.4 = f32[2048,300]{1,0:T(8,128)S(1)} fusion(bf16[1024,300]{0,1:T(8,128)(2,1)S(1)} %copy-done.1, f32[1024,2048]{1,0:T(8,128)} %get-tuple-element.79, f32[2048]{0:T(1024)S(1)} %fusion.18, f32[2048]{0:T(1024)S(1)} %get-tuple-element.70), kind=kOutput, calls=%fused_computation.18 | convolution fusion | flops 1266679808 | bytes 11476992 | tf_op jit(solution)/shard_map/dot_general | solution.py:258
  55.6 2.2 fusion.42
  57.9 5.1 %fusion.6 = f32[1024,300]{1,0:T(8,128)S(1)} fusion(bf16[2048,300]{0,1:T(8,128)(2,1)S(1)} %copy-done, f32[1024,2048]{1,0:T(8,128)} %get-tuple-element.79, f32[1024]{0:T(1024)S(1)} %fusion.30, f32[1024]{0:T(1024)S(1)} %get-tuple-element.76), kind=kOutput, calls=%fused_computation.20 | convolution fusion | flops 1266679808 | bytes 10854400 | tf_op jit(solution)/shard_map/dot_general | solution.py:257
  63.0 2.6 fusion.10
  66.3 0.8 pad.7
  67.1 35.5 %shard_map.59 = f32[32,24,128]{2,1,0:T(8,128)} custom-call(f32[32,24,128]{2,1,0:T(8,128)} %bitcast.123), custom_call_target="tpu_custom_call" | custom-call | tf_op jit(solution)/shard_map/pallas_call | solution.py:128
  102.6 1.7 multiply_reduce_fusion.5
  104.9 1.0 slice_divide_fusion.1
  106.6 11.3 %while.20 = (s32[]{:T(128)}, f32[300,300]{0,1:T(8,128)S(1)}, s32[]{:T(128)}) while((s32[]{:T(128)}, f32[300,300]{0,1:T(8,128)S(1)}, s32[]{:T(128)}) %tuple.54), condition=%wide.region_10.11_spmd, body=%wide.region_9.10_spmd.sunk | while | flops 324270016 | bytes 2520045 | solution.py:25
  107.3 0.7 fusion.84
  108.7 0.7 fusion.84
  110.1 0.7 fusion.84
  111.5 0.7 fusion.84
  112.9 0.7 fusion.84
  114.3 0.7 fusion.84
  115.7 0.7 fusion.84
  117.2 0.7 fusion.84
  117.9 5.3 %multiply_reduce_fusion = (f32[2048]{0:T(1024)S(1)}, f32[1024]{0:T(1024)S(1)}, f32[1024,2048]{1,0:T(8,128)}) fusion(bf16[2048,300]{0,1:T(8,128)(2,1)S(1)} %copy-done, bf16[1024,300]{0,1:T(8,128)(2,1)S(1)} %copy-done.1, f32[300,300]{0,1:T(8,128)S(1)} %get-tuple-element.35), kind=kOutput, calls=%fused_computation.14 | convolution fusion | flops 1449296768 | bytes 10604096 | tf_op jit(solution)/shard_map/dot_general | solution.py:245
  123.2 5.3 %exponential_reduce_fusion = (f32[2048]{0:T(1024)S(1)}, f32[1024]{0:T(1024)S(1)}) fusion(f32[1024,2048]{1,0:T(8,128)} %get-tuple-element.80, f32[2048]{0:T(1024)S(1)} %get-tuple-element.53, f32[1024]{0:T(1024)S(1)} %get-tuple-element.54), kind=kLoop, calls=%fused_computation.8 | loop fusion | flops 10482688 | bytes 8413184 | tf_op jit(solution)/shard_map/reduce_sum | solution.py:253
  129.7 22.1 %shard_map.60 = (f32[8,16,128]{2,1,0:T(8,128)}, f32[32,32,128]{2,1,0:T(8,128)}) custom-call(f32[16,128]{1,0:T(8,128)} %reshape.81.row_ref, f32[32,128]{1,0:T(8,128)} %reshape.82.col_ref), custom_call_target="tpu_custom_call" | custom-call | tf_op jit(solution)/shard_map/pallas_call | solution.py:215
  151.8 0.9 reshape.83
  152.8 6.6 %fusion.7 = f32[1024,300]{0,1:T(8,128)} fusion(bf16[2048,300]{0,1:T(8,128)(2,1)S(1)} %copy-done, f32[1024,2048]{1,0:T(8,128)} %get-tuple-element.80, f32[1024]{0:T(1024)S(1)} %fusion.26, f32[1024]{0:T(1024)S(1)} %get-tuple-element.73), kind=kOutput, calls=%fused_computation.21 | convolution fusion | flops 1266679808 | bytes 10854400 | tf_op jit(solution)/shard_map/dot_general | solution.py:257
  159.4 2.4 convolution_bitcast_fusion
  162.8 6.4 %fusion.39 = (bf16[2048,300]{0,1:T(8,128)(2,1)}, f32[2048,300]{0,1:T(8,128)S(1)}) fusion(bf16[1024,300]{0,1:T(8,128)(2,1)S(1)} %copy-done.1, f32[1024,2048]{1,0:T(8,128)} %get-tuple-element.80, f32[2048]{0:T(1024)S(1)} %fusion.14, f32[2048]{0:T(1024)S(1)} %get-tuple-element.67), kind=kOutput, calls=%fused_computation.68 | convolution fusion | flops 1267294208 | bytes 12705792 | tf_op jit(solution)/shard_map/dot_general | solution.py:258
  169.2 2.1 convolution_add_fusion
  171.9 0.8 pad.8
  172.7 2.5 copy.24
  175.3 78.3 %shard_map.61 = (f32[32,24,128]{2,1,0:T(8,128)}, bf16[4,8,64,300]{3,2,1,0:T(8,128)(2,1)}) custom-call(f32[32,24,128]{2,1,0:T(8,128)} %bitcast.125, bf16[4,8,64,300]{3,2,1,0:T(8,128)(2,1)} %bitcast.120), custom_call_target="tpu_custom_call" | custom-call | tf_op jit(solution)/shard_map/pallas_call | solution.py:142
  253.6 2.5 copy.26
  256.1 1.7 multiply_reduce_fusion.4
  258.5 1.0 slice_divide_fusion
  260.2 11.3 %while.21 = (s32[]{:T(128)}, f32[300,300]{0,1:T(8,128)S(1)}, s32[]{:T(128)}) while((s32[]{:T(128)}, f32[300,300]{0,1:T(8,128)S(1)}, s32[]{:T(128)}) %tuple.57), condition=%wide.region_22.23_spmd, body=%wide.region_21.22_spmd.sunk | while | flops 324270016 | bytes 2520045 | solution.py:25
  260.8 0.7 fusion.90
  262.2 0.7 fusion.90
  263.6 0.7 fusion.90
  265.1 0.7 fusion.90
  266.5 0.7 fusion.90
  267.9 0.7 fusion.90
  269.3 0.7 fusion.90
  270.7 0.7 fusion.90
  271.5 1.0 copy.27
  272.4 1.6 convert_element_type.43
  (67 shorter events, 16.6 us)
Async XLA Ops:
  7.2 1.3 copy-start
  7.2 265.3 %reduce-scatter.2.cloned.1.call-start = ((), (), s32[]{:S(2)}) async-start(), calls=%async_computation.1 | async-start | bytes 1400832 | tf_op jit(solution)/shard_map/reduce_scatter | solution.py:264
  15.8 33.9 %copy-start.1 = (bf16[1024,300]{0,1:T(8,128)(2,1)S(1)}, bf16[1024,300]{0,1:T(8,128)(2,1)}, u32[]{:S(2)}) copy-start(bf16[1024,300]{0,1:T(8,128)(2,1)} %param.7) | copy-start | bytes 1843204
  49.7 8.1 %copy-start.3 = (f32[8,16,128]{2,1,0:T(8,128)S(1)}, f32[8,16,128]{2,1,0:T(8,128)}, u32[]{:S(2)}) copy-start(f32[8,16,128]{2,1,0:T(8,128)} %get-tuple-element.33) | copy-start | bytes 196612
  152.8 9.0 %copy-start.2 = (f32[32,32,128]{2,1,0:T(8,128)S(1)}, f32[32,32,128]{2,1,0:T(8,128)}, u32[]{:S(2)}) copy-start(f32[32,32,128]{2,1,0:T(8,128)} %get-tuple-element.37) | copy-start | bytes 1572868
Sparse Core Ops, SparseCore 0:
  159.5 29.8 reduce-scatter.1

commit v9 on v8

--- a/solution.py
+++ b/solution.py
@@ -68,8 +68,8 @@
 
 def all_reduce_kernel(n_src, n_tgt, with_target, *refs):
     if with_target:
-        (xc, xt, oc, ot, gather_src, gather_tgt, g1, g2, s1,
-         s_a, r_a, s_b, r_b, s_c, r_c, s_1, r_1, s_2, r_2, s_3, r_3, s_4, r_4) = refs
+        (xc, xt, xs, oc, ot, os, gather_src, gather_tgt, g1, g2, s1, gs,
+         s_a, r_a, s_b, r_b, s_c, r_c, s_1, r_1, s_2, r_2, s_3, r_3, s_4, r_4, s_s, r_s) = refs
     else:
         xc, oc, gather_src, gather_tgt, s_a, r_a, s_b, r_b, s_c, r_c = refs
     me_s = lax.axis_index("src")
@@ -85,7 +85,9 @@
         on_y = lambda k: (my_z * n_y + k, me_t)
         on_z = lambda k: (k * n_y + my_y, me_t)
         start_all(my_y, n_y, on_y, lambda k: xt.at[k], lambda i: g1.at[i], s_1, r_1)
+        start_all(me_t, n_tgt, on_tgt, lambda k: xs.at[k], lambda i: gs.at[i], s_s, r_s)
         g1[my_y] = xt[my_y]
+        gs[me_t] = xs[me_t]
 
     start_all(me_s, n_src, on_src, lambda k: xc.at[k], lambda i: gather_src.at[i], s_a, r_a)
     gather_src[me_s] = xc[me_s]
@@ -111,10 +113,12 @@
     if with_target:
         wait_all(my_z, n_z, on_z, lambda k: ot.at[my_y, my_z], lambda i: ot.at[my_y, i], s_3, r_3)
         start_all(my_y, n_y, on_y, lambda k: ot.at[my_y], lambda i: ot.at[i], s_4, r_4)
+        wait_all(me_t, n_tgt, on_tgt, lambda k: xs.at[k], lambda i: gs.at[i], s_s, r_s)
+        os[...] = jnp.sum(gs[...], axis=0).astype(os.dtype)
         wait_all(my_y, n_y, on_y, lambda k: ot.at[my_y], lambda i: ot.at[i], s_4, r_4)
 
 
-def all_reduce(matrix, target_part=None):
+def all_reduce(matrix, target_part=None, source_part=None):
     n_src = lax.axis_size("src")
     n_tgt = lax.axis_size("tgt")
     size = matrix.size
@@ -139,21 +143,24 @@
     n_z = n_src // n_y
     piece = t_rows // n_src
     chunks = target_part.astype(jnp.bfloat16).reshape(n_y, n_z, piece, width)
-    out, target_sum = pl.pallas_call(
+    s_rows = source_part.shape[0]
+    pieces = source_part.reshape(n_tgt, s_rows // n_tgt, width)
+    out, target_sum, source_sum = pl.pallas_call(
         functools.partial(all_reduce_kernel, n_src, n_tgt, True),
         out_shape=(jax.ShapeDtypeStruct(flat.shape, jnp.float32),
-                   jax.ShapeDtypeStruct(chunks.shape, jnp.bfloat16)),
-        in_specs=[vmem, vmem],
-        out_specs=(vmem, vmem),
+                   jax.ShapeDtypeStruct(chunks.shape, jnp.bfloat16),
+                   jax.ShapeDtypeStruct(pieces.shape[1:], jnp.bfloat16)),
+        in_specs=[vmem, vmem, vmem],
+        out_specs=(vmem, vmem, vmem),
         scratch_shapes=scratch
         + [pltpu.VMEM(chunks.shape, jnp.bfloat16), pltpu.VMEM((n_z, piece, width), jnp.bfloat16),
-           pltpu.VMEM((n_z, piece, width), jnp.bfloat16)]
+           pltpu.VMEM((n_z, piece, width), jnp.bfloat16), pltpu.VMEM(pieces.shape, jnp.float32)]
         + sems
-        + [pltpu.SemaphoreType.DMA((n,)) for n in (n_y, n_y, n_z, n_z, n_z, n_z, n_y, n_y)],
+        + [pltpu.SemaphoreType.DMA((n,)) for n in (n_y, n_y, n_z, n_z, n_z, n_z, n_y, n_y, n_tgt, n_tgt)],
         compiler_params=pltpu.CompilerParams(collective_id=1, has_side_effects=True),
-    )(flat, chunks)
+    )(flat, chunks, pieces)
     target_sum = target_sum.reshape(t_rows, width)
-    return out.reshape(-1)[:size].reshape(matrix.shape), target_sum
+    return out.reshape(-1)[:size].reshape(matrix.shape), target_sum, source_sum
 
 
 def stats_gather_kernel(n_src, n_tgt, row_ref, col_ref, row_out, col_out,
@@ -261,10 +268,7 @@
         covariance = jnp.dot(source_f32.T, source_part, precision=highest)
         covariance = covariance + jnp.dot(target_part.T, target_f32, precision=highest)
         if iteration == ITERS - 1:
-            source_soft = lax.psum_scatter(
-                source_part, "tgt", scatter_dimension=0, tiled=True
-            ).astype(jnp.bfloat16)
-            covariance, target_soft = all_reduce(covariance, target_part)
+            covariance, target_soft, source_soft = all_reduce(covariance, target_part, source_part)
         else:
             covariance = all_reduce(covariance)
         current = polar_steps(covariance)

time: 282 us -> 269 us (0.954)
  between operations: 15.7 us -> 2.32 us
  transfers between devices with their start and end apart: 1 -> 0, of which waited for: 0 -> 0; matrix products, arithmetic and copies ran while one was open for 12% -> 0% of each run, Pallas kernels for 28% -> 0%
where the time goes in v9:
time: 269 us; the launch traced here: 268 us
  Pallas kernels  162 us (60%)
  matrix products  67.5 us (25%)
  local copies, waits for them, and re-layouts  18.4 us (7%)
  other arithmetic  17.5 us (7%)
    pallas_call x1, Pallas kernels, all_reduce(): pl.pallas_call(functools.partial(all_reduce_kernel, n_src, n_tgt, True),...  79.2 us
    pallas_call x2, Pallas kernels, gather_stats(): pl.pallas_call(functools.partial(stats_gather_kernel, n_src, n_tgt), out_...  47.4 us
    pallas_call x1, Pallas kernels, all_reduce(): pl.pallas_call(functools.partial(all_reduce_kernel, n_src, n_tgt, False),...  35.4 us
    dot_general x2, matrix products, body(): lax.dot_general(col_weights, source, (((0,), (0,)), ((), ())), preferred_...  13.2 us
    dot_general x2, matrix products, body(): lax.dot_general(mapped, target, (((1,), (1,)), ((), ())), preferred_eleme...  12.6 us
    dot_general x2, matrix products, body(): jnp.dot(row_weights, target, preferred_element_type=jnp.float32)  12.2 us
    dot_general x16, matrix products, newton(): jnp.dot(current, gram_matrix, precision=highest)  11.8 us
    reduce_sum x2, other arithmetic, body(): col_part = jnp.sum(jnp.exp(scores - col_local[None, :]), axis=0)  10.5 us

profile of v9, /device:TPU:2, one launch (start us, length us, event | category | flops | bytes accessed | tf_op | source)
XLA Modules:
  0.0 268.3 jit_solution(6742203275225935636)
XLA Ops:
  0.6 1.3 copy-done
  1.9 7.3 %multiply_reduce_fusion.2 = (f32[2048]{0:T(1024)S(1)}, f32[1024]{0:T(1024)S(1)}, f32[1024,2048]{1,0:T(8,128)}) fusion(bf16[2048,300]{0,1:T(8,128)(2,1)S(1)} %copy-done, bf16[1024,300]{0,1:T(8,128)(2,1)} %param.7, f32[300,300]{1,0:T(8,128)} %param.9), kind=kOutput, calls=%fused_computation.16 | convolution fusion | flops 1449296768 | bytes 10604096 | tf_op jit(solution)/shard_map/dot_general | solution.py:252
  9.2 5.2 %exponential_reduce_fusion.2 = (f32[2048]{0:T(1024)S(1)}, f32[1024]{0:T(1024)S(1)}) fusion(f32[1024,2048]{1,0:T(8,128)} %get-tuple-element.81, f32[2048]{0:T(1024)S(1)} %get-tuple-element.59, f32[1024]{0:T(1024)S(1)} %get-tuple-element.60), kind=kLoop, calls=%fused_computation.12 | loop fusion | flops 10482688 | bytes 8413184 | tf_op jit(solution)/shard_map/reduce_sum | solution.py:260
  15.7 25.3 %shard_map.58 = (f32[8,16,128]{2,1,0:T(8,128)}, f32[32,32,128]{2,1,0:T(8,128)}) custom-call(f32[16,128]{1,0:T(8,128)} %reshape.77.row_ref, f32[32,128]{1,0:T(8,128)} %reshape.78.col_ref), custom_call_target="tpu_custom_call" | custom-call | tf_op jit(solution)/shard_map/pallas_call | solution.py:222
  41.0 0.9 reshape.79
  42.0 7.1 %fusion.6 = f32[1024,300]{1,0:T(8,128)} fusion(bf16[2048,300]{0,1:T(8,128)(2,1)S(1)} %copy-done, f32[1024,2048]{1,0:T(8,128)} %get-tuple-element.81, f32[1024]{0:T(1024)S(1)} %fusion.30, f32[1024]{0:T(1024)S(1)} %get-tuple-element.78), kind=kOutput, calls=%fused_computation.20 | convolution fusion | flops 1266679808 | bytes 10854400 | tf_op jit(solution)/shard_map/dot_general | solution.py:264
  50.1 5.9 %fusion.4 = f32[2048,300]{1,0:T(8,128)S(1)} fusion(bf16[1024,300]{0,1:T(8,128)(2,1)S(1)} %copy-done.2, f32[1024,2048]{1,0:T(8,128)} %get-tuple-element.81, f32[2048]{0:T(1024)S(1)} %fusion.18, f32[2048]{0:T(1024)S(1)} %get-tuple-element.72), kind=kOutput, calls=%fused_computation.18 | convolution fusion | flops 1266679808 | bytes 11476992 | tf_op jit(solution)/shard_map/dot_general | solution.py:265
  56.1 2.2 fusion.42
  58.3 2.6 fusion.10
  61.6 0.8 pad.7
  62.4 35.4 %shard_map.59 = f32[32,24,128]{2,1,0:T(8,128)} custom-call(f32[32,24,128]{2,1,0:T(8,128)} %bitcast.126), custom_call_target="tpu_custom_call" | custom-call | tf_op jit(solution)/shard_map/pallas_call | solution.py:132
  97.8 1.7 multiply_reduce_fusion.5
  100.2 1.0 slice_divide_fusion.1
  101.9 11.3 %while.20 = (s32[]{:T(128)}, f32[300,300]{0,1:T(8,128)S(1)}, s32[]{:T(128)}) while((s32[]{:T(128)}, f32[300,300]{0,1:T(8,128)S(1)}, s32[]{:T(128)}) %tuple.54), condition=%wide.region_10.11_spmd, body=%wide.region_9.10_spmd.sunk | while | flops 324270016 | bytes 2520045 | solution.py:25
  102.6 0.7 fusion.84
  104.0 0.7 fusion.84
  105.4 0.7 fusion.84
  106.8 0.7 fusion.84
  108.2 0.7 fusion.84
  109.6 0.7 fusion.84
  111.0 0.7 fusion.84
  112.4 0.7 fusion.84
  113.2 5.3 %multiply_reduce_fusion = (f32[2048]{0:T(1024)S(1)}, f32[1024]{0:T(1024)S(1)}, f32[1024,2048]{1,0:T(8,128)}) fusion(bf16[2048,300]{0,1:T(8,128)(2,1)S(1)} %copy-done, bf16[1024,300]{0,1:T(8,128)(2,1)S(1)} %copy-done.2, f32[300,300]{0,1:T(8,128)S(1)} %get-tuple-element.36), kind=kOutput, calls=%fused_computation.14 | convolution fusion | flops 1449296768 | bytes 10604096 | tf_op jit(solution)/shard_map/dot_general | solution.py:252
  118.5 5.3 %exponential_reduce_fusion = (f32[2048]{0:T(1024)S(1)}, f32[1024]{0:T(1024)S(1)}) fusion(f32[1024,2048]{1,0:T(8,128)} %get-tuple-element.82, f32[2048]{0:T(1024)S(1)} %get-tuple-element.55, f32[1024]{0:T(1024)S(1)} %get-tuple-element.56), kind=kLoop, calls=%fused_computation.8 | loop fusion | flops 10482688 | bytes 8413184 | tf_op jit(solution)/shard_map/reduce_sum | solution.py:260
  125.0 22.1 %shard_map.60 = (f32[8,16,128]{2,1,0:T(8,128)}, f32[32,32,128]{2,1,0:T(8,128)}) custom-call(f32[16,128]{1,0:T(8,128)} %reshape.84.row_ref, f32[32,128]{1,0:T(8,128)} %reshape.85.col_ref), custom_call_target="tpu_custom_call" | custom-call | tf_op jit(solution)/shard_map/pallas_call | solution.py:222
  147.1 1.3 reshape.87
  149.1 7.2 %fusion.39 = (bf16[2048,300]{0,1:T(8,128)(2,1)}, f32[2048,300]{0,1:T(8,128)}) fusion(bf16[1024,300]{0,1:T(8,128)(2,1)S(1)} %copy-done.2, f32[1024,2048]{1,0:T(8,128)} %get-tuple-element.82, f32[2048]{0:T(1024)S(1)} %fusion.14, f32[2048]{0:T(1024)S(1)} %get-tuple-element.69), kind=kOutput, calls=%fused_computation.68 | convolution fusion | flops 1267294208 | bytes 12705792 | tf_op jit(solution)/shard_map/dot_general | solution.py:265
  156.5 5.1 %fusion.7 = f32[1024,300]{0,1:T(8,128)S(1)} fusion(bf16[2048,300]{0,1:T(8,128)(2,1)S(1)} %copy-done, f32[1024,2048]{1,0:T(8,128)} %get-tuple-element.82, f32[1024]{0:T(1024)S(1)} %fusion.26, f32[1024]{0:T(1024)S(1)} %get-tuple-element.75), kind=kOutput, calls=%fused_computation.21 | convolution fusion | flops 1266679808 | bytes 10854400 | tf_op jit(solution)/shard_map/dot_general | solution.py:264
  161.7 1.1 convolution_bitcast_fusion
  162.8 2.1 convolution_add_fusion
  165.6 0.8 pad.8
  166.4 2.5 copy.26
  168.9 1.6 copy.27
  170.5 79.2 %shard_map.61 = (f32[32,24,128]{2,1,0:T(8,128)}, bf16[4,8,64,300]{3,2,1,0:T(8,128)(2,1)}, bf16[128,300]{1,0:T(8,128)(2,1)}) custom-call(f32[32,24,128]{2,1,0:T(8,128)} %bitcast.125, bf16[4,8,64,300]{3,2,1,0:T(8,128)(2,1)} %bitcast.121, f32[8,128,300]{2,1,0:T(8,128)} %bitcast.122), custom_call_target="tpu_custom_call" | custom-call | tf_op jit(solution)/shard_map/pallas_call | solution.py:148
  249.7 1.7 multiply_reduce_fusion.4
  252.1 1.0 slice_divide_fusion
  253.8 11.3 %while.21 = (s32[]{:T(128)}, f32[300,300]{0,1:T(8,128)S(1)}, s32[]{:T(128)}) while((s32[]{:T(128)}, f32[300,300]{0,1:T(8,128)S(1)}, s32[]{:T(128)}) %tuple.57), condition=%wide.region_21.22_spmd, body=%wide.region_20.21_spmd.sunk | while | flops 324270016 | bytes 2520045 | solution.py:25
  254.4 0.7 fusion.90
  255.8 0.7 fusion.90
  257.3 0.7 fusion.90
  258.7 0.7 fusion.90
  260.1 0.7 fusion.90
  261.5 0.7 fusion.90
  262.9 0.7 fusion.90
  264.3 0.7 fusion.90
  265.1 1.0 copy.31
  266.1 1.5 copy.30
  267.6 0.7 copy.29
  (73 shorter events, 17.1 us)
Async XLA Ops:
  0.6 1.3 copy-start
  42.0 7.1 %copy-start.5 = (f32[32,32,128]{2,1,0:T(8,128)S(1)}, f32[32,32,128]{2,1,0:T(8,128)}, u32[]{:S(2)}) copy-start(f32[32,32,128]{2,1,0:T(8,128)} %get-tuple-element.35) | copy-start | bytes 1572868
  42.0 8.1 %copy-start.2 = (bf16[1024,300]{0,1:T(8,128)(2,1)S(1)}, bf16[1024,300]{0,1:T(8,128)(2,1)}, u32[]{:S(2)}) copy-start(bf16[1024,300]{0,1:T(8,128)(2,1)} %param.7) | copy-start | bytes 1843204
  50.1 8.2 %copy-start.3 = (f32[1024,300]{1,0:T(8,128)S(1)}, f32[1024,300]{1,0:T(8,128)}, u32[]{:S(2)}) copy-start(f32[1024,300]{1,0:T(8,128)} %fusion.6) | copy-start | bytes 3686404
  149.1 7.2 %copy-start.7 = (f32[8,16,128]{2,1,0:T(8,128)S(1)}, f32[8,16,128]{2,1,0:T(8,128)}, u32[]{:S(2)}) copy-start(f32[8,16,128]{2,1,0:T(8,128)} %get-tuple-element.37) | copy-start | bytes 196612
  156.5 6.3 %copy-start.1 = (f32[2048,300]{0,1:T(8,128)S(1)}, f32[2048,300]{0,1:T(8,128)}, u32[]{:S(2)}) copy-start(f32[2048,300]{0,1:T(8,128)} %get-tuple-element.84) | copy-start | bytes 7372804
  253.8 12.3 %copy-start.4 = (bf16[4,8,64,300]{3,2,1,0:T(8,128)(2,1)S(1)}, bf16[4,8,64,300]{3,2,1,0:T(8,128)(2,1)}, u32[]{:S(2)}) copy-start(bf16[4,8,64,300]{3,2,1,0:T(8,128)(2,1)} %get-tuple-element.40) | copy-start | bytes 3686404
  253.8 13.8 %copy-start.6 = (bf16[128,300]{1,0:T(8,128)(2,1)S(1)}, bf16[128,300]{1,0:T(8,128)(2,1)}, u32[]{:S(2)}) copy-start(bf16[128,300]{1,0:T(8,128)(2,1)} %get-tuple-element.50) | copy-start | bytes 230404

commit v10 on v9

--- a/solution.py
+++ b/solution.py
@@ -15,14 +15,32 @@
 NEWTON_STEPS = 8
 
 
+def polar_kernel(steps, c_ref, o_ref):
+    highest = lax.Precision.HIGHEST
+    c = c_ref[...]
+    norm = jnp.sum(jnp.sum(c * c, axis=1, keepdims=True), axis=0, keepdims=True)
+    current = c / jnp.sqrt(norm + 1e-06)
+
+    def newton(step, current):
+        outer = lax.dot_general(current, current, (((1,), (1,)), ((), ())),
+                                precision=highest, preferred_element_type=jnp.float32)
+        return 1.5 * current - 0.5 * jnp.dot(outer, current, precision=highest,
+                                              preferred_element_type=jnp.float32)
+    o_ref[...] = lax.fori_loop(0, steps, newton, current)
+
+
 def polar_steps(covariance):
-    highest = lax.Precision.HIGH
-    current = covariance / jnp.sqrt(jnp.sum(covariance * covariance) + 1e-06)
-
-    def newton(step, current):
-        gram_matrix = jnp.dot(current.T, current, precision=highest)
-        return 1.5 * current - 0.5 * jnp.dot(current, gram_matrix, precision=highest)
-    return lax.fori_loop(0, NEWTON_STEPS, newton, current)
+    size = covariance.shape[0]
+    padded = -(-size // 128) * 128
+    c = jnp.pad(covariance, ((0, padded - size), (0, padded - size)))
+    vmem = pl.BlockSpec(memory_space=pltpu.VMEM)
+    out = pl.pallas_call(
+        functools.partial(polar_kernel, NEWTON_STEPS),
+        out_shape=jax.ShapeDtypeStruct(c.shape, jnp.float32),
+        in_specs=[vmem],
+        out_specs=vmem,
+    )(c)
+    return out[:size, :size]
 
 
 def peer_barrier(n_src, n_tgt):

time: 269 us -> 302 us (1.12); the launches traced: 268 us -> 297 us
  Pallas kernels: 162 us -> 210 us
  matrix products: 67.5 us -> 47.9 us
  local copies, waits for them, and re-layouts: 18.4 us -> 25.6 us
  other arithmetic: 17.5 us -> 12 us
    pallas_call x0 -> x2, Pallas kernels: none -> 48.3 us  [polar_steps(): pl.pallas_call(functools.partial(polar_kernel, NEWTON_STEPS), out_shape=j...]
    dot_general x32 -> x0, matrix products: 21.4 us -> none  [the longest x16 11.8 us: newton(): jnp.dot(current, gram_matrix, precision=highest)]
    slice x0 -> x3, local copies, waits for them, and re-layouts: none -> 3.84 us  [the longest x1 1.82 us: polar_steps(): return out[:size, :size]]
    reduce_sum x2 -> x0, other arithmetic: 3.36 us -> none  [polar_steps(): current = covariance / jnp.sqrt(jnp.sum(covariance * covariance) + 1e-06)]
where the time goes in v10:
time: 302 us; the launch traced here: 297 us
  Pallas kernels  210 us (70%)
  matrix products  47.9 us (16%)
  local copies, waits for them, and re-layouts  25.6 us (8%)
  other arithmetic  12 us (4%)
    pallas_call x1, Pallas kernels, all_reduce(): pl.pallas_call(functools.partial(all_reduce_kernel, n_src, n_tgt, True),...  79.3 us
    pallas_call x2, Pallas kernels, polar_steps(): pl.pallas_call(functools.partial(polar_kernel, NEWTON_STEPS), out_shape=j...  48.3 us
    pallas_call x2, Pallas kernels, gather_stats(): pl.pallas_call(functools.partial(stats_gather_kernel, n_src, n_tgt), out_...  47.4 us
    pallas_call x1, Pallas kernels, all_reduce(): pl.pallas_call(functools.partial(all_reduce_kernel, n_src, n_tgt, False),...  35.4 us
    dot_general x2, matrix products, body(): lax.dot_general(mapped, target, (((1,), (1,)), ((), ())), preferred_eleme...  14.5 us
    dot_general x2, matrix products, body(): lax.dot_general(col_weights, source, (((0,), (0,)), ((), ())), preferred_...  13.1 us
    dot_general x2, matrix products, body(): jnp.dot(row_weights, target, preferred_element_type=jnp.float32)  12.2 us
    reduce_sum x2, other arithmetic, body(): col_part = jnp.sum(jnp.exp(scores - col_local[None, :]), axis=0)  10.5 us

profile of v10, /device:TPU:2, one launch (start us, length us, event | category | flops | bytes accessed | tf_op | source)
XLA Modules:
  0.0 297.1 jit_solution(48673463626063673)
XLA Ops:
  0.6 1.3 copy-done
  1.9 7.3 %multiply_reduce_fusion.2 = (f32[2048]{0:T(1024)S(1)}, f32[1024]{0:T(1024)S(1)}, f32[1024,2048]{1,0:T(8,128)}) fusion(bf16[2048,300]{0,1:T(8,128)(2,1)S(1)} %copy-done, bf16[1024,300]{0,1:T(8,128)(2,1)} %param.3, f32[300,300]{1,0:T(8,128)} %param.5), kind=kOutput, calls=%fused_computation.10 | convolution fusion | flops 1449296768 | bytes 10604096 | tf_op jit(solution)/shard_map/dot_general | solution.py:270
  9.2 5.2 %exponential_reduce_fusion.2 = (f32[2048]{0:T(1024)S(1)}, f32[1024]{0:T(1024)S(1)}) fusion(f32[1024,2048]{1,0:T(8,128)} %get-tuple-element.43, f32[2048]{0:T(1024)S(1)} %get-tuple-element.29, f32[1024]{0:T(1024)S(1)} %get-tuple-element.30), kind=kLoop, calls=%fused_computation.6 | loop fusion | flops 10482688 | bytes 8413184 | tf_op jit(solution)/shard_map/reduce_sum | solution.py:278
  14.5 0.6 reshape.78.col_ref
  15.1 0.6 reshape.77.row_ref
  15.7 25.3 %shard_map.58 = (f32[8,16,128]{2,1,0:T(8,128)}, f32[32,32,128]{2,1,0:T(8,128)}) custom-call(f32[16,128]{1,0:T(8,128)} %reshape.77.row_ref, f32[32,128]{1,0:T(8,128)} %reshape.78.col_ref), custom_call_target="tpu_custom_call" | custom-call | tf_op jit(solution)/shard_map/pallas_call | solution.py:240
  41.0 0.9 reshape.79
  41.9 0.1 slice_reduce_fusion.1
  42.0 7.1 %fusion.2 = f32[1024,300]{1,0:T(8,128)} fusion(bf16[2048,300]{0,1:T(8,128)(2,1)S(1)} %copy-done, f32[1024,2048]{1,0:T(8,128)} %get-tuple-element.43, f32[1024]{0:T(1024)S(1)} %fusion.24, f32[1024]{0:T(1024)S(1)} %get-tuple-element.40), kind=kOutput, calls=%fused_computation.14 | convolution fusion | flops 1266679808 | bytes 10854400 | tf_op jit(solution)/shard_map/dot_general | solution.py:282
  49.2 0.3 reshape.80
  49.4 0.5 slice_reduce_fusion.3
  49.9 0.2 fusion.14
  50.1 5.9 %fusion = f32[2048,300]{1,0:T(8,128)S(1)} fusion(bf16[1024,300]{0,1:T(8,128)(2,1)S(1)} %copy-done.2, f32[1024,2048]{1,0:T(8,128)} %get-tuple-element.43, f32[2048]{0:T(1024)S(1)} %fusion.14, f32[2048]{0:T(1024)S(1)} %get-tuple-element.34), kind=kOutput, calls=%fused_computation.12 | convolution fusion | flops 1266679808 | bytes 11476992 | tf_op jit(solution)/shard_map/dot_general | solution.py:283
  56.1 2.2 fusion.32
  58.3 2.6 fusion.6
  60.9 0.2 copy.19
  61.1 0.5 reshape.81
  61.6 0.8 pad.14
  62.4 35.4 %shard_map.59 = f32[32,24,128]{2,1,0:T(8,128)} custom-call(f32[32,24,128]{2,1,0:T(8,128)} %bitcast.88), custom_call_target="tpu_custom_call" | custom-call | tf_op jit(solution)/shard_map/pallas_call | solution.py:150
  97.8 1.0 slice.53
  98.8 0.5 reshape.84
  99.3 0.9 pad.15.c_ref
  100.2 24.2 %shard_map.60 = f32[384,384]{1,0:T(8,128)} custom-call(f32[384,384]{1,0:T(8,128)} %pad.15.c_ref), custom_call_target="tpu_custom_call" | custom-call | tf_op jit(solution)/shard_map/pallas_call | solution.py:37
  124.3 7.2 %multiply_reduce_fusion = (f32[2048]{0:T(1024)S(1)}, f32[1024]{0:T(1024)S(1)}, f32[1024,2048]{1,0:T(8,128)}) fusion(bf16[2048,300]{0,1:T(8,128)(2,1)S(1)} %copy-done, bf16[1024,300]{0,1:T(8,128)(2,1)S(1)} %copy-done.2, f32[384,384]{1,0:T(8,128)} %shard_map.60), kind=kOutput, calls=%fused_computation.8 | convolution fusion | flops 1449206784 | bytes 10477568 | tf_op jit(solution)/shard_map/dot_general | solution.py:270
  131.5 5.2 %exponential_reduce_fusion = (f32[2048]{0:T(1024)S(1)}, f32[1024]{0:T(1024)S(1)}) fusion(f32[1024,2048]{1,0:T(8,128)} %get-tuple-element.44, f32[2048]{0:T(1024)S(1)} %get-tuple-element.25, f32[1024]{0:T(1024)S(1)} %get-tuple-element.26), kind=kLoop, calls=%fused_computation.2 | loop fusion | flops 10482688 | bytes 8413184 | tf_op jit(solution)/shard_map/reduce_sum | solution.py:278
  136.8 0.6 reshape.86.col_ref
  137.4 0.6 reshape.85.row_ref
  138.0 22.1 %shard_map.61 = (f32[8,16,128]{2,1,0:T(8,128)}, f32[32,32,128]{2,1,0:T(8,128)}) custom-call(f32[16,128]{1,0:T(8,128)} %reshape.85.row_ref, f32[32,128]{1,0:T(8,128)} %reshape.86.col_ref), custom_call_target="tpu_custom_call" | custom-call | tf_op jit(solution)/shard_map/pallas_call | solution.py:240
  160.1 1.3 reshape.88
  161.5 0.5 slice_reduce_fusion.2
  161.9 0.2 fusion.10
  162.1 7.2 %fusion.31 = (bf16[2048,300]{0,1:T(8,128)(2,1)}, f32[2048,300]{0,1:T(8,128)}) fusion(bf16[1024,300]{0,1:T(8,128)(2,1)S(1)} %copy-done.2, f32[1024,2048]{1,0:T(8,128)} %get-tuple-element.44, f32[2048]{0:T(1024)S(1)} %fusion.10, f32[2048]{0:T(1024)S(1)} %get-tuple-element.31), kind=kOutput, calls=%fused_computation.58 | convolution fusion | flops 1267294208 | bytes 12705792 | tf_op jit(solution)/shard_map/dot_general | solution.py:283
  169.5 5.1 %fusion.3 = f32[1024,300]{0,1:T(8,128)S(1)} fusion(bf16[2048,300]{0,1:T(8,128)(2,1)S(1)} %copy-done, f32[1024,2048]{1,0:T(8,128)} %get-tuple-element.44, f32[1024]{0:T(1024)S(1)} %fusion.20, f32[1024]{0:T(1024)S(1)} %get-tuple-element.37), kind=kOutput, calls=%fused_computation.15 | convolution fusion | flops 1266679808 | bytes 10854400 | tf_op jit(solution)/shard_map/dot_general | solution.py:282
  174.6 1.1 convolution_bitcast_fusion
  175.7 2.1 convolution_add_fusion
  177.8 1.0 copy.23
  178.8 1.5 reshape.89
  180.3 0.8 pad.16
  181.1 2.5 copy.24
  183.6 1.6 copy.25
  185.2 79.3 %shard_map.62 = (f32[32,24,128]{2,1,0:T(8,128)}, bf16[4,8,64,300]{3,2,1,0:T(8,128)(2,1)}, bf16[128,300]{1,0:T(8,128)(2,1)}) custom-call(f32[32,24,128]{2,1,0:T(8,128)} %bitcast.87, bf16[4,8,64,300]{3,2,1,0:T(8,128)(2,1)} %bitcast.85, f32[8,128,300]{2,1,0:T(8,128)} %bitcast.86), custom_call_target="tpu_custom_call" | custom-call | tf_op jit(solution)/shard_map/pallas_call | solution.py:166
  264.5 1.0 slice.59
  265.5 0.5 reshape.95
  266.0 0.9 pad.17.c_ref
  266.8 24.1 %shard_map.63 = f32[384,384]{1,0:T(8,128)} custom-call(f32[384,384]{1,0:T(8,128)} %pad.17.c_ref), custom_call_target="tpu_custom_call" | custom-call | tf_op jit(solution)/shard_map/pallas_call | solution.py:37
  290.9 1.8 slice.60
  292.8 2.5 copy.27
  295.2 1.6 copy.26
  (19 shorter events, 0.3 us)
Async XLA Ops:
  0.6 1.3 copy-start
  42.0 7.1 %copy-start.4 = (f32[32,32,128]{2,1,0:T(8,128)S(1)}, f32[32,32,128]{2,1,0:T(8,128)}, u32[]{:S(2)}) copy-start(f32[32,32,128]{2,1,0:T(8,128)} %get-tuple-element.11) | copy-start | bytes 1572868
  42.0 8.1 %copy-start.2 = (bf16[1024,300]{0,1:T(8,128)(2,1)S(1)}, bf16[1024,300]{0,1:T(8,128)(2,1)}, u32[]{:S(2)}) copy-start(bf16[1024,300]{0,1:T(8,128)(2,1)} %param.3) | copy-start | bytes 1843204
  50.1 8.2 %copy-start.3 = (f32[1024,300]{1,0:T(8,128)S(1)}, f32[1024,300]{1,0:T(8,128)}, u32[]{:S(2)}) copy-start(f32[1024,300]{1,0:T(8,128)} %fusion.2) | copy-start | bytes 3686404
  162.1 7.2 %copy-start.5 = (f32[8,16,128]{2,1,0:T(8,128)S(1)}, f32[8,16,128]{2,1,0:T(8,128)}, u32[]{:S(2)}) copy-start(f32[8,16,128]{2,1,0:T(8,128)} %get-tuple-element.12) | copy-start | bytes 196612
  169.5 6.2 %copy-start.1 = (f32[2048,300]{0,1:T(8,128)S(1)}, f32[2048,300]{0,1:T(8,128)}, u32[]{:S(2)}) copy-start(f32[2048,300]{0,1:T(8,128)} %get-tuple-element.46) | copy-start | bytes 7372804

commit v11 on v9

--- a/solution.py
+++ b/solution.py
@@ -114,7 +114,7 @@
         wait_all(my_z, n_z, on_z, lambda k: ot.at[my_y, my_z], lambda i: ot.at[my_y, i], s_3, r_3)
         start_all(my_y, n_y, on_y, lambda k: ot.at[my_y], lambda i: ot.at[i], s_4, r_4)
         wait_all(me_t, n_tgt, on_tgt, lambda k: xs.at[k], lambda i: gs.at[i], s_s, r_s)
-        os[...] = jnp.sum(gs[...], axis=0).astype(os.dtype)
+        os[...] = jnp.sum(gs[...].astype(jnp.float32), axis=0).astype(os.dtype)
         wait_all(my_y, n_y, on_y, lambda k: ot.at[my_y], lambda i: ot.at[i], s_4, r_4)
 
 
@@ -144,7 +144,7 @@
     piece = t_rows // n_src
     chunks = target_part.astype(jnp.bfloat16).reshape(n_y, n_z, piece, width)
     s_rows = source_part.shape[0]
-    pieces = source_part.reshape(n_tgt, s_rows // n_tgt, width)
+    pieces = source_part.astype(jnp.bfloat16).reshape(n_tgt, s_rows // n_tgt, width)
     out, target_sum, source_sum = pl.pallas_call(
         functools.partial(all_reduce_kernel, n_src, n_tgt, True),
         out_shape=(jax.ShapeDtypeStruct(flat.shape, jnp.float32),
@@ -154,7 +154,7 @@
         out_specs=(vmem, vmem, vmem),
         scratch_shapes=scratch
         + [pltpu.VMEM(chunks.shape, jnp.bfloat16), pltpu.VMEM((n_z, piece, width), jnp.bfloat16),
-           pltpu.VMEM((n_z, piece, width), jnp.bfloat16), pltpu.VMEM(pieces.shape, jnp.float32)]
+           pltpu.VMEM((n_z, piece, width), jnp.bfloat16), pltpu.VMEM(pieces.shape, jnp.bfloat16)]
         + sems
         + [pltpu.SemaphoreType.DMA((n,)) for n in (n_y, n_y, n_z, n_z, n_z, n_z, n_y, n_y, n_tgt, n_tgt)],
         compiler_params=pltpu.CompilerParams(collective_id=1, has_side_effects=True),

time: 269 us -> 268 us (level)
  matrix products: 67.5 us -> 64.4 us
    unnamed x19 -> x9, local copies, waits for them, and re-layouts: 4.57 us -> 6.39 us
where the time goes in v11:
time: 268 us; the launch traced here: 267 us
  Pallas kernels  161 us (60%)
  matrix products  64.4 us (24%)
  local copies, waits for them, and re-layouts  20.8 us (8%)
  other arithmetic  17.5 us (7%)
    pallas_call x1, Pallas kernels, all_reduce(): pl.pallas_call(functools.partial(all_reduce_kernel, n_src, n_tgt, True),...  78.3 us
    pallas_call x2, Pallas kernels, gather_stats(): pl.pallas_call(functools.partial(stats_gather_kernel, n_src, n_tgt), out_...  47.5 us
    pallas_call x1, Pallas kernels, all_reduce(): pl.pallas_call(functools.partial(all_reduce_kernel, n_src, n_tgt, False),...  35.4 us
    dot_general x2, matrix products, body(): lax.dot_general(mapped, target, (((1,), (1,)), ((), ())), preferred_eleme...  12.6 us
    dot_general x2, matrix products, body(): lax.dot_general(col_weights, source, (((0,), (0,)), ((), ())), preferred_...  12.2 us
    dot_general x16, matrix products, newton(): jnp.dot(current, gram_matrix, precision=highest)  11.8 us
    reduce_sum x2, other arithmetic, body(): col_part = jnp.sum(jnp.exp(scores - col_local[None, :]), axis=0)  10.6 us
    dot_general x2, matrix products, body(): jnp.dot(row_weights, target, preferred_element_type=jnp.float32)  10.1 us

profile of v11, /device:TPU:2, one launch (start us, length us, event | category | flops | bytes accessed | tf_op | source)
XLA Modules:
  0.0 266.9 jit_solution(15639073113360397799)
XLA Ops:
  0.6 1.3 copy-done
  1.9 7.3 %multiply_reduce_fusion.2 = (f32[2048]{0:T(1024)S(1)}, f32[1024]{0:T(1024)S(1)}, f32[1024,2048]{1,0:T(8,128)}) fusion(bf16[2048,300]{0,1:T(8,128)(2,1)S(1)} %copy-done, bf16[1024,300]{0,1:T(8,128)(2,1)} %param.7, f32[300,300]{1,0:T(8,128)} %param.9), kind=kOutput, calls=%fused_computation.16 | convolution fusion | flops 1449296768 | bytes 10604096 | tf_op jit(solution)/shard_map/dot_general | solution.py:252
  9.2 5.3 %exponential_reduce_fusion.2 = (f32[2048]{0:T(1024)S(1)}, f32[1024]{0:T(1024)S(1)}) fusion(f32[1024,2048]{1,0:T(8,128)} %get-tuple-element.81, f32[2048]{0:T(1024)S(1)} %get-tuple-element.59, f32[1024]{0:T(1024)S(1)} %get-tuple-element.60), kind=kLoop, calls=%fused_computation.12 | loop fusion | flops 10482688 | bytes 8413184 | tf_op jit(solution)/shard_map/reduce_sum | solution.py:260
  15.8 25.3 %shard_map.58 = (f32[8,16,128]{2,1,0:T(8,128)}, f32[32,32,128]{2,1,0:T(8,128)}) custom-call(f32[16,128]{1,0:T(8,128)} %reshape.77.row_ref, f32[32,128]{1,0:T(8,128)} %reshape.78.col_ref), custom_call_target="tpu_custom_call" | custom-call | tf_op jit(solution)/shard_map/pallas_call | solution.py:222
  41.2 1.3 reshape.80
  43.2 5.9 %fusion.4 = f32[2048,300]{1,0:T(8,128)S(1)} fusion(bf16[1024,300]{0,1:T(8,128)(2,1)S(1)} %copy-done.1, f32[1024,2048]{1,0:T(8,128)} %get-tuple-element.81, f32[2048]{0:T(1024)S(1)} %fusion.18, f32[2048]{0:T(1024)S(1)} %get-tuple-element.72), kind=kOutput, calls=%fused_computation.18 | convolution fusion | flops 1266679808 | bytes 11476992 | tf_op jit(solution)/shard_map/dot_general | solution.py:265
  49.0 2.2 fusion.43
  51.4 5.1 %fusion.6 = f32[1024,300]{1,0:T(8,128)S(1)} fusion(bf16[2048,300]{0,1:T(8,128)(2,1)S(1)} %copy-done, f32[1024,2048]{1,0:T(8,128)} %get-tuple-element.81, f32[1024]{0:T(1024)S(1)} %fusion.30, f32[1024]{0:T(1024)S(1)} %get-tuple-element.78), kind=kOutput, calls=%fused_computation.20 | convolution fusion | flops 1266679808 | bytes 10854400 | tf_op jit(solution)/shard_map/dot_general | solution.py:264
  56.5 2.6 fusion.10
  59.8 0.8 pad.7
  60.6 35.4 %shard_map.59 = f32[32,24,128]{2,1,0:T(8,128)} custom-call(f32[32,24,128]{2,1,0:T(8,128)} %bitcast.125), custom_call_target="tpu_custom_call" | custom-call | tf_op jit(solution)/shard_map/pallas_call | solution.py:132
  96.0 1.7 multiply_reduce_fusion.5
  98.4 1.0 slice_divide_fusion.1
  100.1 11.3 %while.20 = (s32[]{:T(128)}, f32[300,300]{0,1:T(8,128)S(1)}, s32[]{:T(128)}) while((s32[]{:T(128)}, f32[300,300]{0,1:T(8,128)S(1)}, s32[]{:T(128)}) %tuple.55), condition=%wide.region_10.11_spmd, body=%wide.region_9.10_spmd.sunk | while | flops 324270016 | bytes 2520045 | solution.py:25
  100.7 0.7 fusion.85
  102.1 0.7 fusion.85
  103.6 0.7 fusion.85
  105.0 0.7 fusion.85
  106.4 0.7 fusion.85
  107.8 0.7 fusion.85
  109.2 0.7 fusion.85
  110.6 0.7 fusion.85
  111.4 5.3 %multiply_reduce_fusion = (f32[2048]{0:T(1024)S(1)}, f32[1024]{0:T(1024)S(1)}, f32[1024,2048]{1,0:T(8,128)}) fusion(bf16[2048,300]{0,1:T(8,128)(2,1)S(1)} %copy-done, bf16[1024,300]{0,1:T(8,128)(2,1)S(1)} %copy-done.1, f32[300,300]{0,1:T(8,128)S(1)} %get-tuple-element.36), kind=kOutput, calls=%fused_computation.14 | convolution fusion | flops 1449296768 | bytes 10604096 | tf_op jit(solution)/shard_map/dot_general | solution.py:252
  116.7 5.3 %exponential_reduce_fusion = (f32[2048]{0:T(1024)S(1)}, f32[1024]{0:T(1024)S(1)}) fusion(f32[1024,2048]{1,0:T(8,128)} %get-tuple-element.82, f32[2048]{0:T(1024)S(1)} %get-tuple-element.55, f32[1024]{0:T(1024)S(1)} %get-tuple-element.56), kind=kLoop, calls=%fused_computation.8 | loop fusion | flops 10482688 | bytes 8413184 | tf_op jit(solution)/shard_map/reduce_sum | solution.py:260
  123.2 22.1 %shard_map.60 = (f32[8,16,128]{2,1,0:T(8,128)}, f32[32,32,128]{2,1,0:T(8,128)}) custom-call(f32[16,128]{1,0:T(8,128)} %reshape.84.row_ref, f32[32,128]{1,0:T(8,128)} %reshape.85.col_ref), custom_call_target="tpu_custom_call" | custom-call | tf_op jit(solution)/shard_map/pallas_call | solution.py:222
  145.3 0.9 reshape.86
  146.3 5.0 %fusion.40 = (bf16[1024,300]{0,1:T(8,128)(2,1)S(1)}, f32[1024,300]{0,1:T(8,128)S(1)}) fusion(bf16[2048,300]{0,1:T(8,128)(2,1)S(1)} %copy-done, f32[1024,2048]{1,0:T(8,128)} %get-tuple-element.82, f32[1024]{0:T(1024)S(1)} %fusion.26, f32[1024]{0:T(1024)S(1)} %get-tuple-element.75), kind=kOutput, calls=%fused_computation.69 | convolution fusion | flops 1266987008 | bytes 11468800 | tf_op jit(solution)/shard_map/dot_general | solution.py:264
  151.3 1.1 convolution_bitcast_fusion
  152.4 1.3 reshape.87
  154.4 6.4 %fusion.39 = (bf16[2048,300]{0,1:T(8,128)(2,1)}, f32[2048,300]{0,1:T(8,128)S(1)}) fusion(bf16[1024,300]{0,1:T(8,128)(2,1)S(1)} %copy-done.1, f32[1024,2048]{1,0:T(8,128)} %get-tuple-element.82, f32[2048]{0:T(1024)S(1)} %fusion.14, f32[2048]{0:T(1024)S(1)} %get-tuple-element.69), kind=kOutput, calls=%fused_computation.68 | convolution fusion | flops 1267294208 | bytes 12705792 | tf_op jit(solution)/shard_map/dot_general | solution.py:265
  160.8 2.1 convolution_add_fusion
  163.6 0.8 pad.8
  164.4 2.5 copy.26
  166.9 1.2 copy.27
  168.1 78.3 %shard_map.61 = (f32[32,24,128]{2,1,0:T(8,128)}, bf16[4,8,64,300]{3,2,1,0:T(8,128)(2,1)}, bf16[128,300]{1,0:T(8,128)(2,1)}) custom-call(f32[32,24,128]{2,1,0:T(8,128)} %bitcast.127, bf16[4,8,64,300]{3,2,1,0:T(8,128)(2,1)} %bitcast.121, bf16[8,128,300]{2,1,0:T(8,128)(2,1)} %bitcast.124), custom_call_target="tpu_custom_call" | custom-call | tf_op jit(solution)/shard_map/pallas_call | solution.py:148
  246.4 1.6 copy.29
  248.1 2.5 copy.30
  250.5 1.7 multiply_reduce_fusion.4
  252.9 1.0 slice_divide_fusion
  254.6 11.3 %while.21 = (s32[]{:T(128)}, f32[300,300]{0,1:T(8,128)S(1)}, s32[]{:T(128)}) while((s32[]{:T(128)}, f32[300,300]{0,1:T(8,128)S(1)}, s32[]{:T(128)}) %tuple.58), condition=%wide.region_21.22_spmd, body=%wide.region_20.21_spmd.sunk | while | flops 324270016 | bytes 2520045 | solution.py:25
  256.7 0.7 fusion.91
  258.1 0.7 fusion.91
  259.5 0.7 fusion.91
  260.9 0.7 fusion.91
  262.3 0.7 fusion.91
  263.7 0.7 fusion.91
  265.1 0.7 fusion.91
  265.9 1.0 copy.31
  (63 shorter events, 17.6 us)
Async XLA Ops:
  0.6 1.3 copy-start
  9.2 33.9 %copy-start.1 = (bf16[1024,300]{0,1:T(8,128)(2,1)S(1)}, bf16[1024,300]{0,1:T(8,128)(2,1)}, u32[]{:S(2)}) copy-start(bf16[1024,300]{0,1:T(8,128)(2,1)} %param.7) | copy-start | bytes 1843204
  43.2 8.1 %copy-start.2 = (f32[8,16,128]{2,1,0:T(8,128)S(1)}, f32[8,16,128]{2,1,0:T(8,128)}, u32[]{:S(2)}) copy-start(f32[8,16,128]{2,1,0:T(8,128)} %get-tuple-element.34) | copy-start | bytes 196612

commit v12 on v9

--- a/solution.py
+++ b/solution.py
@@ -25,6 +25,19 @@
     return lax.fori_loop(0, NEWTON_STEPS, newton, current)
 
 
+def polar_value(c):
+    highest = lax.Precision.HIGHEST
+    norm = jnp.sum(jnp.sum(c * c, axis=1, keepdims=True), axis=0, keepdims=True)
+    current = c / jnp.sqrt(norm + 1e-06)
+
+    def newton(step, current):
+        outer = lax.dot_general(current, current, (((1,), (1,)), ((), ())),
+                                precision=highest, preferred_element_type=jnp.float32)
+        return 1.5 * current - 0.5 * jnp.dot(outer, current, precision=highest,
+                                              preferred_element_type=jnp.float32)
+    return lax.fori_loop(0, NEWTON_STEPS, newton, current)
+
+
 def peer_barrier(n_src, n_tgt):
     me_s = lax.axis_index("src")
     me_t = lax.axis_index("tgt")
@@ -68,7 +81,7 @@
 
 def all_reduce_kernel(n_src, n_tgt, with_target, *refs):
     if with_target:
-        (xc, xt, xs, oc, ot, os, gather_src, gather_tgt, g1, g2, s1, gs,
+        (xc, xt, xs, oc, ot, os, op, gather_src, gather_tgt, g1, g2, s1, gs,
          s_a, r_a, s_b, r_b, s_c, r_c, s_1, r_1, s_2, r_2, s_3, r_3, s_4, r_4, s_s, r_s) = refs
     else:
         xc, oc, gather_src, gather_tgt, s_a, r_a, s_b, r_b, s_c, r_c = refs
@@ -113,6 +126,8 @@
     if with_target:
         wait_all(my_z, n_z, on_z, lambda k: ot.at[my_y, my_z], lambda i: ot.at[my_y, i], s_3, r_3)
         start_all(my_y, n_y, on_y, lambda k: ot.at[my_y], lambda i: ot.at[i], s_4, r_4)
+        width = op.shape[0]
+        op[...] = polar_value(oc[...].reshape(-1, width)[:width])
         wait_all(me_t, n_tgt, on_tgt, lambda k: xs.at[k], lambda i: gs.at[i], s_s, r_s)
         os[...] = jnp.sum(gs[...], axis=0).astype(os.dtype)
         wait_all(my_y, n_y, on_y, lambda k: ot.at[my_y], lambda i: ot.at[i], s_4, r_4)
@@ -122,6 +137,7 @@
     n_src = lax.axis_size("src")
     n_tgt = lax.axis_size("tgt")
     size = matrix.size
+    size_m = matrix.shape[0]
     lines = -(-size // 128)
     rows = -(-lines // (n_src * 8)) * 8
     flat = jnp.pad(matrix.reshape(-1), (0, n_src * rows * 128 - size)).reshape(n_src, rows, 128)
@@ -145,22 +161,26 @@
     chunks = target_part.astype(jnp.bfloat16).reshape(n_y, n_z, piece, width)
     s_rows = source_part.shape[0]
     pieces = source_part.reshape(n_tgt, s_rows // n_tgt, width)
-    out, target_sum, source_sum = pl.pallas_call(
+    side = -(-size_m // 128) * 128
+    step = -(-side // (n_src * 8)) * 8
+    block = jnp.pad(matrix, ((0, n_src * step - size_m), (0, side - size_m))).reshape(n_src, step, side)
+    _, target_sum, source_sum, polar = pl.pallas_call(
         functools.partial(all_reduce_kernel, n_src, n_tgt, True),
-        out_shape=(jax.ShapeDtypeStruct(flat.shape, jnp.float32),
+        out_shape=(jax.ShapeDtypeStruct(block.shape, jnp.float32),
                    jax.ShapeDtypeStruct(chunks.shape, jnp.bfloat16),
-                   jax.ShapeDtypeStruct(pieces.shape[1:], jnp.bfloat16)),
+                   jax.ShapeDtypeStruct(pieces.shape[1:], jnp.bfloat16),
+                   jax.ShapeDtypeStruct((side, side), jnp.float32)),
         in_specs=[vmem, vmem, vmem],
-        out_specs=(vmem, vmem, vmem),
-        scratch_shapes=scratch
+        out_specs=(vmem, vmem, vmem, vmem),
+        scratch_shapes=[pltpu.VMEM(block.shape, jnp.float32), pltpu.VMEM((n_tgt, step, side), jnp.float32)]
         + [pltpu.VMEM(chunks.shape, jnp.bfloat16), pltpu.VMEM((n_z, piece, width), jnp.bfloat16),
            pltpu.VMEM((n_z, piece, width), jnp.bfloat16), pltpu.VMEM(pieces.shape, jnp.float32)]
         + sems
         + [pltpu.SemaphoreType.DMA((n,)) for n in (n_y, n_y, n_z, n_z, n_z, n_z, n_y, n_y, n_tgt, n_tgt)],
         compiler_params=pltpu.CompilerParams(collective_id=1, has_side_effects=True),
-    )(flat, chunks, pieces)
+    )(block, chunks, pieces)
     target_sum = target_sum.reshape(t_rows, width)
-    return out.reshape(-1)[:size].reshape(matrix.shape), target_sum, source_sum
+    return polar[:size_m, :size_m], target_sum, source_sum
 
 
 def stats_gather_kernel(n_src, n_tgt, row_ref, col_ref, row_out, col_out,
@@ -268,10 +288,9 @@
         covariance = jnp.dot(source_f32.T, source_part, precision=highest)
         covariance = covariance + jnp.dot(target_part.T, target_f32, precision=highest)
         if iteration == ITERS - 1:
-            covariance, target_soft, source_soft = all_reduce(covariance, target_part, source_part)
+            current, target_soft, source_soft = all_reduce(covariance, target_part, source_part)
         else:
-            covariance = all_reduce(covariance)
-        current = polar_steps(covariance)
+            current = polar_steps(all_reduce(covariance))
     return (source_soft, target_soft, current)
 
 

time: 269 us -> 268 us (level)
  matrix products: 67.5 us -> 50.2 us
  Pallas kernels: 162 us -> 178 us
  local copies, waits for them, and re-layouts: 18.4 us -> 21.5 us
  other arithmetic: 17.5 us -> 14.8 us
    pallas_call x1, Pallas kernels: 79.2 us -> 95.6 us  [all_reduce(): pl.pallas_call(functools.partial(all_reduce_kernel, n_src, n_tgt, True),...]
    dot_general x2, matrix products: 13.2 us -> 5.82 us  [body(): lax.dot_general(col_weights, source, (((0,), (0,)), ((), ())), preferred_...]
    dot_general x16 -> x8, matrix products: 11.8 us -> 5.92 us  [newton(): jnp.dot(current, gram_matrix, precision=highest)]
    dot_general x16 -> x8, matrix products: 9.59 us -> 4.8 us  [newton(): gram_matrix = jnp.dot(current.T, current, precision=highest)]
    unnamed x19 -> x14, local copies, waits for them, and re-layouts: 4.57 us -> 5.43 us
where the time goes in v12:
time: 268 us; the launch traced here: 267 us
  Pallas kernels  178 us (66%)
  matrix products  50.2 us (19%)
  local copies, waits for them, and re-layouts  21.5 us (8%)
  other arithmetic  14.8 us (6%)
    pallas_call x1, Pallas kernels, all_reduce(): pl.pallas_call(functools.partial(all_reduce_kernel, n_src, n_tgt, True),...  95.6 us
    pallas_call x2, Pallas kernels, gather_stats(): pl.pallas_call(functools.partial(stats_gather_kernel, n_src, n_tgt), out_...  47.5 us
    pallas_call x1, Pallas kernels, all_reduce(): pl.pallas_call(functools.partial(all_reduce_kernel, n_src, n_tgt, False),...  35.5 us
    dot_general x2, matrix products, body(): lax.dot_general(mapped, target, (((1,), (1,)), ((), ())), preferred_eleme...  12.6 us
    dot_general x2, matrix products, body(): jnp.dot(row_weights, target, preferred_element_type=jnp.float32)  11.3 us
    reduce_sum x2, other arithmetic, body(): col_part = jnp.sum(jnp.exp(scores - col_local[None, :]), axis=0)  10.5 us
    dot_general x2, matrix products, body(): jnp.dot(target_part.T, target_f32, precision=highest)  5.99 us
    dot_general x8, matrix products, newton(): jnp.dot(current, gram_matrix, precision=highest)  5.92 us

profile of v12, /device:TPU:2, one launch (start us, length us, event | category | flops | bytes accessed | tf_op | source)
XLA Modules:
  0.0 266.9 jit_solution(9010019438082060554)
XLA Ops:
  0.6 1.3 copy-done
  1.9 7.3 %multiply_reduce_fusion.2 = (f32[2048]{0:T(1024)S(1)}, f32[1024]{0:T(1024)S(1)}, f32[1024,2048]{1,0:T(8,128)}) fusion(bf16[2048,300]{0,1:T(8,128)(2,1)S(1)} %copy-done, bf16[1024,300]{0,1:T(8,128)(2,1)} %param.5, f32[300,300]{1,0:T(8,128)} %param.7), kind=kOutput, calls=%fused_computation.13 | convolution fusion | flops 1449296768 | bytes 10604096 | tf_op jit(solution)/shard_map/dot_general | solution.py:272
  9.2 5.2 %exponential_reduce_fusion.2 = (f32[2048]{0:T(1024)S(1)}, f32[1024]{0:T(1024)S(1)}) fusion(f32[1024,2048]{1,0:T(8,128)} %get-tuple-element.62, f32[2048]{0:T(1024)S(1)} %get-tuple-element.44, f32[1024]{0:T(1024)S(1)} %get-tuple-element.45), kind=kLoop, calls=%fused_computation.9 | loop fusion | flops 10482688 | bytes 8413184 | tf_op jit(solution)/shard_map/reduce_sum | solution.py:280
  14.5 0.6 reshape.69.col_ref
  15.1 0.6 reshape.68.row_ref
  15.7 25.3 %shard_map.58 = (f32[8,16,128]{2,1,0:T(8,128)}, f32[32,32,128]{2,1,0:T(8,128)}) custom-call(f32[16,128]{1,0:T(8,128)} %reshape.68.row_ref, f32[32,128]{1,0:T(8,128)} %reshape.69.col_ref), custom_call_target="tpu_custom_call" | custom-call | tf_op jit(solution)/shard_map/pallas_call | solution.py:242
  41.1 0.9 reshape.70
  42.1 1.3 reshape.71
  44.1 5.8 %fusion.4 = f32[1024,300]{1,0:T(8,128)S(1)} fusion(bf16[2048,300]{0,1:T(8,128)(2,1)S(1)} %copy-done, f32[1024,2048]{1,0:T(8,128)} %get-tuple-element.62, f32[1024]{0:T(1024)S(1)} %fusion.28, f32[1024]{0:T(1024)S(1)} %get-tuple-element.59), kind=kOutput, calls=%fused_computation.17 | convolution fusion | flops 1266679808 | bytes 10854400 | tf_op jit(solution)/shard_map/dot_general | solution.py:284
  50.0 2.4 fusion.2
  52.4 2.2 fusion.39
  54.6 2.6 fusion.8
  57.9 0.8 pad.8
  58.7 35.5 %shard_map.59 = f32[32,24,128]{2,1,0:T(8,128)} custom-call(f32[32,24,128]{2,1,0:T(8,128)} %bitcast.111), custom_call_target="tpu_custom_call" | custom-call | tf_op jit(solution)/shard_map/pallas_call | solution.py:148
  94.2 1.7 multiply_reduce_fusion.4
  96.6 1.0 slice_divide_fusion
  98.3 11.3 %while.10 = (s32[]{:T(128)}, f32[300,300]{0,1:T(8,128)S(1)}, s32[]{:T(128)}) while((s32[]{:T(128)}, f32[300,300]{0,1:T(8,128)S(1)}, s32[]{:T(128)}) %tuple.40), condition=%wide.region_10.11_spmd, body=%wide.region_9.10_spmd.sunk | while | flops 324270016 | bytes 2520045 | solution.py:25
  98.3 0.6 fusion.70
  98.9 0.7 fusion.71
  100.3 0.7 fusion.71
  101.1 0.6 fusion.70
  101.7 0.7 fusion.71
  102.5 0.6 fusion.70
  103.1 0.7 fusion.71
  104.5 0.7 fusion.71
  105.4 0.6 fusion.70
  106.0 0.7 fusion.71
  106.8 0.6 fusion.70
  107.4 0.7 fusion.71
  108.8 0.7 fusion.71
  109.5 5.3 %multiply_reduce_fusion = (f32[2048]{0:T(1024)S(1)}, f32[1024]{0:T(1024)S(1)}, f32[1024,2048]{1,0:T(8,128)}) fusion(bf16[2048,300]{0,1:T(8,128)(2,1)S(1)} %copy-done, bf16[1024,300]{0,1:T(8,128)(2,1)S(1)} %copy-done.1, f32[300,300]{0,1:T(8,128)S(1)} %get-tuple-element.24), kind=kOutput, calls=%fused_computation.11 | convolution fusion | flops 1449296768 | bytes 10604096 | tf_op jit(solution)/shard_map/dot_general | solution.py:272
  114.8 5.3 %exponential_reduce_fusion = (f32[2048]{0:T(1024)S(1)}, f32[1024]{0:T(1024)S(1)}) fusion(f32[1024,2048]{1,0:T(8,128)} %get-tuple-element.63, f32[2048]{0:T(1024)S(1)} %get-tuple-element.40, f32[1024]{0:T(1024)S(1)} %get-tuple-element.41), kind=kLoop, calls=%fused_computation.5 | loop fusion | flops 10482688 | bytes 8413184 | tf_op jit(solution)/shard_map/reduce_sum | solution.py:280
  120.1 0.6 reshape.76.col_ref
  120.8 0.6 reshape.75.row_ref
  121.4 22.1 %shard_map.60 = (f32[8,16,128]{2,1,0:T(8,128)}, f32[32,32,128]{2,1,0:T(8,128)}) custom-call(f32[16,128]{1,0:T(8,128)} %reshape.75.row_ref, f32[32,128]{1,0:T(8,128)} %reshape.76.col_ref), custom_call_target="tpu_custom_call" | custom-call | tf_op jit(solution)/shard_map/pallas_call | solution.py:242
  143.5 0.9 reshape.77
  144.5 1.3 reshape.78
  146.5 5.5 %fusion.5 = f32[1024,300]{0,1:T(8,128)S(1)} fusion(bf16[2048,300]{0,1:T(8,128)(2,1)S(1)} %copy-done, f32[1024,2048]{1,0:T(8,128)} %get-tuple-element.63, f32[1024]{0:T(1024)S(1)} %fusion.24, f32[1024]{0:T(1024)S(1)} %get-tuple-element.56), kind=kOutput, calls=%fused_computation.18 | convolution fusion | flops 1266679808 | bytes 10854400 | tf_op jit(solution)/shard_map/dot_general | solution.py:284
  152.0 3.4 %fusion.37 = (bf16[2048,300]{0,1:T(8,128)(2,1)}, f32[2048,300]{0,1:T(8,128)}) fusion(bf16[1024,300]{0,1:T(8,128)(2,1)S(1)} %copy-done.1, f32[1024,2048]{1,0:T(8,128)S(1)} %bitcast.103, f32[2048]{0:T(1024)S(1)} %fusion.12, f32[2048]{0:T(1024)S(1)} %get-tuple-element.50), kind=kOutput, calls=%fused_computation.63 | convolution fusion | flops 1267294208 | bytes 12705792 | tf_op jit(solution)/shard_map/dot_general | solution.py:285
  155.4 2.5 copy.22
  157.9 1.1 convolution_bitcast_fusion
  159.0 3.8 %convolution_add_fusion = f32[300,300]{1,0:T(8,128)S(1)} fusion(f32[300,300]{1,0:T(8,128)S(1)} %convolution_bitcast_fusion, f32[2048,300]{0,1:T(8,128)} %get-tuple-element.65, bf16[2048,300]{0,1:T(8,128)(2,1)S(1)} %copy-done), kind=kOutput, calls=%fused_computation.23 | convolution fusion | flops 2211930112 | bytes 4406400 | tf_op jit(solution)/shard_map/dot_general | solution.py:289
  162.8 0.9 pad.9
  163.8 1.6 copy.23
  165.4 95.6 %shard_map.61 = (f32[32,16,384]{2,1,0:T(8,128)}, bf16[4,8,64,300]{3,2,1,0:T(8,128)(2,1)}, bf16[128,300]{1,0:T(8,128)(2,1)}, f32[384,384]{1,0:T(8,128)}) custom-call(f32[32,16,384]{2,1,0:T(8,128)} %bitcast.110, bf16[4,8,64,300]{3,2,1,0:T(8,128)(2,1)} %bitcast.106, f32[8,128,300]{2,1,0:T(8,128)} %bitcast.107), custom_call_target="tpu_custom_call" | custom-call | tf_op jit(solution)/shard_map/pallas_call | solution.py:167
  261.0 1.6 copy.24
  262.6 2.5 copy.25
  265.1 1.8 slice.39
  (40 shorter events, 5.0 us)
Async XLA Ops:
  0.6 1.3 copy-start
  43.4 6.5 %slice-start.2 = ((s8[8388608]{0:T(1024)(128)(4,1)}), s8[4194304]{0:T(1024)(128)(4,1)S(1)}, s32[]{:S(2)}) async-start(s8[8388608]{0:T(1024)(128)(4,1)} %bitcast.104), calls=%async_computation.2 | async-start | bytes 8388608
  44.1 5.9 %slice-start.3 = ((s8[8388608]{0:T(1024)(128)(4,1)}), s8[4194304]{0:T(1024)(128)(4,1)S(1)}, s32[]{:S(2)}) async-start(s8[8388608]{0:T(1024)(128)(4,1)} %bitcast.104), calls=%async_computation.3 | async-start | bytes 8388608
  44.1 5.9 %copy-start.1 = (bf16[1024,300]{0,1:T(8,128)(2,1)S(1)}, bf16[1024,300]{0,1:T(8,128)(2,1)}, u32[]{:S(2)}) copy-start(bf16[1024,300]{0,1:T(8,128)(2,1)} %param.5) | copy-start | bytes 1843204
  145.8 6.2 %slice-start = ((s8[8388608]{0:T(1024)(128)(4,1)}), s8[4194304]{0:T(1024)(128)(4,1)S(1)}, s32[]{:S(2)}) async-start(s8[8388608]{0:T(1024)(128)(4,1)} %bitcast.102), calls=%async_computation | async-start | bytes 8388608
  146.5 5.5 %slice-start.1 = ((s8[8388608]{0:T(1024)(128)(4,1)}), s8[4194304]{0:T(1024)(128)(4,1)S(1)}, s32[]{:S(2)}) async-start(s8[8388608]{0:T(1024)(128)(4,1)} %bitcast.102), calls=%async_computation.1 | async-start | bytes 8388608

commit v13 on v9

--- a/solution.py
+++ b/solution.py
@@ -265,8 +265,8 @@
         target_part = lax.dot_general(
             col_weights, source, (((0,), (0,)), ((), ())), preferred_element_type=jnp.float32
         )
-        covariance = jnp.dot(source_f32.T, source_part, precision=highest)
-        covariance = covariance + jnp.dot(target_part.T, target_f32, precision=highest)
+        covariance = jnp.dot(source_f32.T, source_part, precision=lax.Precision.HIGH)
+        covariance = covariance + jnp.dot(target_part.T, target_f32, precision=lax.Precision.HIGH)
         if iteration == ITERS - 1:
             covariance, target_soft, source_soft = all_reduce(covariance, target_part, source_part)
         else:

time: 269 us -> 267 us (level)
  no operation moved by 1% of the time
where the time goes in v13:
time: 267 us; the launch traced here: 266 us
  Pallas kernels  162 us (61%)
  matrix products  65 us (24%)
  local copies, waits for them, and re-layouts  18.4 us (7%)
  other arithmetic  17.5 us (7%)
    pallas_call x1, Pallas kernels, all_reduce(): pl.pallas_call(functools.partial(all_reduce_kernel, n_src, n_tgt, True),...  79.1 us
    pallas_call x2, Pallas kernels, gather_stats(): pl.pallas_call(functools.partial(stats_gather_kernel, n_src, n_tgt), out_...  47.4 us
    pallas_call x1, Pallas kernels, all_reduce(): pl.pallas_call(functools.partial(all_reduce_kernel, n_src, n_tgt, False),...  35.4 us
    dot_general x2, matrix products, body(): lax.dot_general(col_weights, source, (((0,), (0,)), ((), ())), preferred_...  13.2 us
    dot_general x2, matrix products, body(): lax.dot_general(mapped, target, (((1,), (1,)), ((), ())), preferred_eleme...  12.6 us
    dot_general x2, matrix products, body(): jnp.dot(row_weights, target, preferred_element_type=jnp.float32)  12.2 us
    dot_general x16, matrix products, newton(): jnp.dot(current, gram_matrix, precision=highest)  11.8 us
    reduce_sum x2, other arithmetic, body(): col_part = jnp.sum(jnp.exp(scores - col_local[None, :]), axis=0)  10.5 us

profile of v13, /device:TPU:2, one launch (start us, length us, event | category | flops | bytes accessed | tf_op | source)
XLA Modules:
  0.0 265.8 jit_solution(16041744108466396793)
XLA Ops:
  0.6 1.3 copy-done
  1.9 7.3 %multiply_reduce_fusion.2 = (f32[2048]{0:T(1024)S(1)}, f32[1024]{0:T(1024)S(1)}, f32[1024,2048]{1,0:T(8,128)}) fusion(bf16[2048,300]{0,1:T(8,128)(2,1)S(1)} %copy-done, bf16[1024,300]{0,1:T(8,128)(2,1)} %param.7, f32[300,300]{1,0:T(8,128)} %param.9), kind=kOutput, calls=%fused_computation.16 | convolution fusion | flops 1449296768 | bytes 10604096 | tf_op jit(solution)/shard_map/dot_general | solution.py:252
  9.2 5.2 %exponential_reduce_fusion.2 = (f32[2048]{0:T(1024)S(1)}, f32[1024]{0:T(1024)S(1)}) fusion(f32[1024,2048]{1,0:T(8,128)} %get-tuple-element.81, f32[2048]{0:T(1024)S(1)} %get-tuple-element.59, f32[1024]{0:T(1024)S(1)} %get-tuple-element.60), kind=kLoop, calls=%fused_computation.12 | loop fusion | flops 10482688 | bytes 8413184 | tf_op jit(solution)/shard_map/reduce_sum | solution.py:260
  15.7 25.3 %shard_map.58 = (f32[8,16,128]{2,1,0:T(8,128)}, f32[32,32,128]{2,1,0:T(8,128)}) custom-call(f32[16,128]{1,0:T(8,128)} %reshape.77.row_ref, f32[32,128]{1,0:T(8,128)} %reshape.78.col_ref), custom_call_target="tpu_custom_call" | custom-call | tf_op jit(solution)/shard_map/pallas_call | solution.py:222
  41.0 0.9 reshape.79
  42.0 7.1 %fusion.6 = f32[1024,300]{1,0:T(8,128)} fusion(bf16[2048,300]{0,1:T(8,128)(2,1)S(1)} %copy-done, f32[1024,2048]{1,0:T(8,128)} %get-tuple-element.81, f32[1024]{0:T(1024)S(1)} %fusion.30, f32[1024]{0:T(1024)S(1)} %get-tuple-element.78), kind=kOutput, calls=%fused_computation.20 | convolution fusion | flops 1266679808 | bytes 10854400 | tf_op jit(solution)/shard_map/dot_general | solution.py:264
  50.1 5.9 %fusion.4 = f32[2048,300]{1,0:T(8,128)S(1)} fusion(bf16[1024,300]{0,1:T(8,128)(2,1)S(1)} %copy-done.2, f32[1024,2048]{1,0:T(8,128)} %get-tuple-element.81, f32[2048]{0:T(1024)S(1)} %fusion.18, f32[2048]{0:T(1024)S(1)} %get-tuple-element.72), kind=kOutput, calls=%fused_computation.18 | convolution fusion | flops 1266679808 | bytes 11476992 | tf_op jit(solution)/shard_map/dot_general | solution.py:265
  56.1 1.5 fusion.42
  57.6 1.8 fusion.10
  60.1 0.8 pad.7
  60.8 35.4 %shard_map.59 = f32[32,24,128]{2,1,0:T(8,128)} custom-call(f32[32,24,128]{2,1,0:T(8,128)} %bitcast.126), custom_call_target="tpu_custom_call" | custom-call | tf_op jit(solution)/shard_map/pallas_call | solution.py:132
  96.3 1.7 multiply_reduce_fusion.5
  98.7 1.0 slice_divide_fusion.1
  100.4 11.3 %while.20 = (s32[]{:T(128)}, f32[300,300]{0,1:T(8,128)S(1)}, s32[]{:T(128)}) while((s32[]{:T(128)}, f32[300,300]{0,1:T(8,128)S(1)}, s32[]{:T(128)}) %tuple.54), condition=%wide.region_10.11_spmd, body=%wide.region_9.10_spmd.sunk | while | flops 324270016 | bytes 2520045 | solution.py:25
  101.0 0.7 fusion.84
  102.4 0.7 fusion.84
  103.8 0.7 fusion.84
  105.2 0.7 fusion.84
  106.7 0.7 fusion.84
  108.1 0.7 fusion.84
  109.5 0.7 fusion.84
  110.9 0.7 fusion.84
  111.6 5.3 %multiply_reduce_fusion = (f32[2048]{0:T(1024)S(1)}, f32[1024]{0:T(1024)S(1)}, f32[1024,2048]{1,0:T(8,128)}) fusion(bf16[2048,300]{0,1:T(8,128)(2,1)S(1)} %copy-done, bf16[1024,300]{0,1:T(8,128)(2,1)S(1)} %copy-done.2, f32[300,300]{0,1:T(8,128)S(1)} %get-tuple-element.36), kind=kOutput, calls=%fused_computation.14 | convolution fusion | flops 1449296768 | bytes 10604096 | tf_op jit(solution)/shard_map/dot_general | solution.py:252
  116.9 5.3 %exponential_reduce_fusion = (f32[2048]{0:T(1024)S(1)}, f32[1024]{0:T(1024)S(1)}) fusion(f32[1024,2048]{1,0:T(8,128)} %get-tuple-element.82, f32[2048]{0:T(1024)S(1)} %get-tuple-element.55, f32[1024]{0:T(1024)S(1)} %get-tuple-element.56), kind=kLoop, calls=%fused_computation.8 | loop fusion | flops 10482688 | bytes 8413184 | tf_op jit(solution)/shard_map/reduce_sum | solution.py:260
  123.5 22.1 %shard_map.60 = (f32[8,16,128]{2,1,0:T(8,128)}, f32[32,32,128]{2,1,0:T(8,128)}) custom-call(f32[16,128]{1,0:T(8,128)} %reshape.84.row_ref, f32[32,128]{1,0:T(8,128)} %reshape.85.col_ref), custom_call_target="tpu_custom_call" | custom-call | tf_op jit(solution)/shard_map/pallas_call | solution.py:222
  145.6 1.3 reshape.87
  147.6 7.2 %fusion.39 = (bf16[2048,300]{0,1:T(8,128)(2,1)}, f32[2048,300]{0,1:T(8,128)}) fusion(bf16[1024,300]{0,1:T(8,128)(2,1)S(1)} %copy-done.2, f32[1024,2048]{1,0:T(8,128)} %get-tuple-element.82, f32[2048]{0:T(1024)S(1)} %fusion.14, f32[2048]{0:T(1024)S(1)} %get-tuple-element.69), kind=kOutput, calls=%fused_computation.68 | convolution fusion | flops 1267294208 | bytes 12705792 | tf_op jit(solution)/shard_map/dot_general | solution.py:265
  155.0 5.1 %fusion.7 = f32[1024,300]{0,1:T(8,128)S(1)} fusion(bf16[2048,300]{0,1:T(8,128)(2,1)S(1)} %copy-done, f32[1024,2048]{1,0:T(8,128)} %get-tuple-element.82, f32[1024]{0:T(1024)S(1)} %fusion.26, f32[1024]{0:T(1024)S(1)} %get-tuple-element.75), kind=kOutput, calls=%fused_computation.21 | convolution fusion | flops 1266679808 | bytes 10854400 | tf_op jit(solution)/shard_map/dot_general | solution.py:264
  160.1 0.8 convolution_bitcast_fusion
  160.9 1.5 convolution_add_fusion
  163.1 0.8 pad.8
  163.8 2.5 copy.26
  166.4 1.6 copy.27
  168.0 79.1 %shard_map.61 = (f32[32,24,128]{2,1,0:T(8,128)}, bf16[4,8,64,300]{3,2,1,0:T(8,128)(2,1)}, bf16[128,300]{1,0:T(8,128)(2,1)}) custom-call(f32[32,24,128]{2,1,0:T(8,128)} %bitcast.125, bf16[4,8,64,300]{3,2,1,0:T(8,128)(2,1)} %bitcast.121, f32[8,128,300]{2,1,0:T(8,128)} %bitcast.122), custom_call_target="tpu_custom_call" | custom-call | tf_op jit(solution)/shard_map/pallas_call | solution.py:148
  247.2 1.7 multiply_reduce_fusion.4
  249.5 1.0 slice_divide_fusion
  251.2 11.3 %while.21 = (s32[]{:T(128)}, f32[300,300]{0,1:T(8,128)S(1)}, s32[]{:T(128)}) while((s32[]{:T(128)}, f32[300,300]{0,1:T(8,128)S(1)}, s32[]{:T(128)}) %tuple.57), condition=%wide.region_21.22_spmd, body=%wide.region_20.21_spmd.sunk | while | flops 324270016 | bytes 2520045 | solution.py:25
  251.9 0.7 fusion.90
  253.3 0.7 fusion.90
  254.7 0.7 fusion.90
  256.1 0.7 fusion.90
  257.5 0.7 fusion.90
  258.9 0.7 fusion.90
  260.4 0.7 fusion.90
  261.8 0.7 fusion.90
  262.5 1.0 copy.31
  263.5 1.5 copy.30
  265.0 0.7 copy.29
  (73 shorter events, 17.1 us)
Async XLA Ops:
  0.6 1.3 copy-start
  42.0 7.1 %copy-start.5 = (f32[32,32,128]{2,1,0:T(8,128)S(1)}, f32[32,32,128]{2,1,0:T(8,128)}, u32[]{:S(2)}) copy-start(f32[32,32,128]{2,1,0:T(8,128)} %get-tuple-element.35) | copy-start | bytes 1572868
  42.0 8.1 %copy-start.2 = (bf16[1024,300]{0,1:T(8,128)(2,1)S(1)}, bf16[1024,300]{0,1:T(8,128)(2,1)}, u32[]{:S(2)}) copy-start(bf16[1024,300]{0,1:T(8,128)(2,1)} %param.7) | copy-start | bytes 1843204
  50.1 7.4 %copy-start.3 = (f32[1024,300]{1,0:T(8,128)S(1)}, f32[1024,300]{1,0:T(8,128)}, u32[]{:S(2)}) copy-start(f32[1024,300]{1,0:T(8,128)} %fusion.6) | copy-start | bytes 3686404
  147.6 7.2 %copy-start.7 = (f32[8,16,128]{2,1,0:T(8,128)S(1)}, f32[8,16,128]{2,1,0:T(8,128)}, u32[]{:S(2)}) copy-start(f32[8,16,128]{2,1,0:T(8,128)} %get-tuple-element.37) | copy-start | bytes 196612
  155.0 6.0 %copy-start.1 = (f32[2048,300]{0,1:T(8,128)S(1)}, f32[2048,300]{0,1:T(8,128)}, u32[]{:S(2)}) copy-start(f32[2048,300]{0,1:T(8,128)} %get-tuple-element.84) | copy-start | bytes 7372804
  251.2 12.3 %copy-start.4 = (bf16[4,8,64,300]{3,2,1,0:T(8,128)(2,1)S(1)}, bf16[4,8,64,300]{3,2,1,0:T(8,128)(2,1)}, u32[]{:S(2)}) copy-start(bf16[4,8,64,300]{3,2,1,0:T(8,128)(2,1)} %get-tuple-element.40) | copy-start | bytes 3686404
  251.2 13.8 %copy-start.6 = (bf16[128,300]{1,0:T(8,128)(2,1)S(1)}, bf16[128,300]{1,0:T(8,128)(2,1)}, u32[]{:S(2)}) copy-start(bf16[128,300]{1,0:T(8,128)(2,1)} %get-tuple-element.50) | copy-start | bytes 230404

commit v14 on v13

--- a/solution.py
+++ b/solution.py
@@ -22,7 +22,7 @@
     def newton(step, current):
         gram_matrix = jnp.dot(current.T, current, precision=highest)
         return 1.5 * current - 0.5 * jnp.dot(current, gram_matrix, precision=highest)
-    return lax.fori_loop(0, NEWTON_STEPS, newton, current)
+    return lax.fori_loop(0, NEWTON_STEPS, newton, current, unroll=2)
 
 
 def peer_barrier(n_src, n_tgt):

time: 267 us -> 266 us (level)
  no operation moved by 1% of the time
where the time goes in v14:
time: 266 us; the launch traced here: 265 us
  Pallas kernels  162 us (61%)
  matrix products  64.7 us (24%)
  local copies, waits for them, and re-layouts  17.9 us (7%)
  other arithmetic  17.5 us (7%)
    pallas_call x1, Pallas kernels, all_reduce(): pl.pallas_call(functools.partial(all_reduce_kernel, n_src, n_tgt, True),...  78.9 us
    pallas_call x2, Pallas kernels, gather_stats(): pl.pallas_call(functools.partial(stats_gather_kernel, n_src, n_tgt), out_...  47.4 us
    pallas_call x1, Pallas kernels, all_reduce(): pl.pallas_call(functools.partial(all_reduce_kernel, n_src, n_tgt, False),...  35.4 us
    dot_general x2, matrix products, body(): lax.dot_general(col_weights, source, (((0,), (0,)), ((), ())), preferred_...  13.2 us
    dot_general x2, matrix products, body(): lax.dot_general(mapped, target, (((1,), (1,)), ((), ())), preferred_eleme...  12.6 us
    dot_general x2, matrix products, body(): jnp.dot(row_weights, target, preferred_element_type=jnp.float32)  12.2 us
    dot_general x16, matrix products, newton(): jnp.dot(current, gram_matrix, precision=highest)  11.6 us
    reduce_sum x2, other arithmetic, body(): col_part = jnp.sum(jnp.exp(scores - col_local[None, :]), axis=0)  10.5 us

profile of v14, /device:TPU:2, one launch (start us, length us, event | category | flops | bytes accessed | tf_op | source)
XLA Modules:
  0.0 264.5 jit_solution(17743201249523661752)
XLA Ops:
  0.6 1.3 copy-done
  1.9 7.3 %multiply_reduce_fusion.2 = (f32[2048]{0:T(1024)S(1)}, f32[1024]{0:T(1024)S(1)}, f32[1024,2048]{1,0:T(8,128)}) fusion(bf16[2048,300]{0,1:T(8,128)(2,1)S(1)} %copy-done, bf16[1024,300]{0,1:T(8,128)(2,1)} %param.7, f32[300,300]{1,0:T(8,128)} %param.9), kind=kOutput, calls=%fused_computation.20 | convolution fusion | flops 1449296768 | bytes 10604096 | tf_op jit(solution)/shard_map/dot_general | solution.py:252
  9.2 5.2 %exponential_reduce_fusion.2 = (f32[2048]{0:T(1024)S(1)}, f32[1024]{0:T(1024)S(1)}) fusion(f32[1024,2048]{1,0:T(8,128)} %get-tuple-element.81, f32[2048]{0:T(1024)S(1)} %get-tuple-element.59, f32[1024]{0:T(1024)S(1)} %get-tuple-element.60), kind=kLoop, calls=%fused_computation.16 | loop fusion | flops 10482688 | bytes 8413184 | tf_op jit(solution)/shard_map/reduce_sum | solution.py:260
  15.7 25.3 %shard_map.58 = (f32[8,16,128]{2,1,0:T(8,128)}, f32[32,32,128]{2,1,0:T(8,128)}) custom-call(f32[16,128]{1,0:T(8,128)} %reshape.77.row_ref, f32[32,128]{1,0:T(8,128)} %reshape.78.col_ref), custom_call_target="tpu_custom_call" | custom-call | tf_op jit(solution)/shard_map/pallas_call | solution.py:222
  41.0 0.9 reshape.79
  42.0 7.1 %fusion.8 = f32[1024,300]{1,0:T(8,128)} fusion(bf16[2048,300]{0,1:T(8,128)(2,1)S(1)} %copy-done, f32[1024,2048]{1,0:T(8,128)} %get-tuple-element.81, f32[1024]{0:T(1024)S(1)} %fusion.32, f32[1024]{0:T(1024)S(1)} %get-tuple-element.78), kind=kOutput, calls=%fused_computation.24 | convolution fusion | flops 1266679808 | bytes 10854400 | tf_op jit(solution)/shard_map/dot_general | solution.py:264
  50.1 5.9 %fusion.6 = f32[2048,300]{1,0:T(8,128)S(1)} fusion(bf16[1024,300]{0,1:T(8,128)(2,1)S(1)} %copy-done.2, f32[1024,2048]{1,0:T(8,128)} %get-tuple-element.81, f32[2048]{0:T(1024)S(1)} %fusion.20, f32[2048]{0:T(1024)S(1)} %get-tuple-element.72), kind=kOutput, calls=%fused_computation.22 | convolution fusion | flops 1266679808 | bytes 11476992 | tf_op jit(solution)/shard_map/dot_general | solution.py:265
  56.1 1.5 fusion.46
  57.6 1.8 fusion.12
  60.1 0.8 pad.7
  60.8 35.4 %shard_map.59 = f32[32,24,128]{2,1,0:T(8,128)} custom-call(f32[32,24,128]{2,1,0:T(8,128)} %bitcast.150), custom_call_target="tpu_custom_call" | custom-call | tf_op jit(solution)/shard_map/pallas_call | solution.py:132
  96.3 1.7 multiply_reduce_fusion.5
  98.7 1.0 slice_divide_fusion.1
  100.4 10.7 %while.20 = (s32[]{:T(128)}, f32[300,300]{0,1:T(8,128)S(1)}, s32[]{:T(128)}) while((s32[]{:T(128)}, f32[300,300]{0,1:T(8,128)S(1)}, s32[]{:T(128)}) %tuple.54), condition=%wide.region_10.11_spmd, body=%wide.region_9.10_spmd.sunk | while | flops 648540032 | bytes 3600045 | solution.py:25
  101.0 0.7 fusion.112
  102.3 0.7 fusion.114
  103.7 0.7 fusion.112
  105.0 0.7 fusion.114
  106.3 0.7 fusion.112
  107.7 0.7 fusion.114
  109.0 0.7 fusion.112
  110.4 0.7 fusion.114
  111.1 5.3 %multiply_reduce_fusion = (f32[2048]{0:T(1024)S(1)}, f32[1024]{0:T(1024)S(1)}, f32[1024,2048]{1,0:T(8,128)}) fusion(bf16[2048,300]{0,1:T(8,128)(2,1)S(1)} %copy-done, bf16[1024,300]{0,1:T(8,128)(2,1)S(1)} %copy-done.2, f32[300,300]{0,1:T(8,128)S(1)} %get-tuple-element.36), kind=kOutput, calls=%fused_computation.18 | convolution fusion | flops 1449296768 | bytes 10604096 | tf_op jit(solution)/shard_map/dot_general | solution.py:252
  116.4 5.3 %exponential_reduce_fusion = (f32[2048]{0:T(1024)S(1)}, f32[1024]{0:T(1024)S(1)}) fusion(f32[1024,2048]{1,0:T(8,128)} %get-tuple-element.82, f32[2048]{0:T(1024)S(1)} %get-tuple-element.55, f32[1024]{0:T(1024)S(1)} %get-tuple-element.56), kind=kLoop, calls=%fused_computation.12 | loop fusion | flops 10482688 | bytes 8413184 | tf_op jit(solution)/shard_map/reduce_sum | solution.py:260
  122.9 22.1 %shard_map.60 = (f32[8,16,128]{2,1,0:T(8,128)}, f32[32,32,128]{2,1,0:T(8,128)}) custom-call(f32[16,128]{1,0:T(8,128)} %reshape.84.row_ref, f32[32,128]{1,0:T(8,128)} %reshape.85.col_ref), custom_call_target="tpu_custom_call" | custom-call | tf_op jit(solution)/shard_map/pallas_call | solution.py:222
  145.1 1.3 reshape.87
  147.1 7.2 %fusion.41 = (bf16[2048,300]{0,1:T(8,128)(2,1)}, f32[2048,300]{0,1:T(8,128)}) fusion(bf16[1024,300]{0,1:T(8,128)(2,1)S(1)} %copy-done.2, f32[1024,2048]{1,0:T(8,128)} %get-tuple-element.82, f32[2048]{0:T(1024)S(1)} %fusion.16, f32[2048]{0:T(1024)S(1)} %get-tuple-element.69), kind=kOutput, calls=%fused_computation.72 | convolution fusion | flops 1267294208 | bytes 12705792 | tf_op jit(solution)/shard_map/dot_general | solution.py:265
  154.5 5.1 %fusion.9 = f32[1024,300]{0,1:T(8,128)S(1)} fusion(bf16[2048,300]{0,1:T(8,128)(2,1)S(1)} %copy-done, f32[1024,2048]{1,0:T(8,128)} %get-tuple-element.82, f32[1024]{0:T(1024)S(1)} %fusion.28, f32[1024]{0:T(1024)S(1)} %get-tuple-element.75), kind=kOutput, calls=%fused_computation.25 | convolution fusion | flops 1266679808 | bytes 10854400 | tf_op jit(solution)/shard_map/dot_general | solution.py:264
  159.6 0.8 convolution_bitcast_fusion
  160.4 1.5 convolution_add_fusion
  162.5 0.8 pad.8
  163.3 2.5 copy.34
  165.9 1.6 copy.35
  167.5 78.9 %shard_map.61 = (f32[32,24,128]{2,1,0:T(8,128)}, bf16[4,8,64,300]{3,2,1,0:T(8,128)(2,1)}, bf16[128,300]{1,0:T(8,128)(2,1)}) custom-call(f32[32,24,128]{2,1,0:T(8,128)} %bitcast.149, bf16[4,8,64,300]{3,2,1,0:T(8,128)(2,1)} %bitcast.145, f32[8,128,300]{2,1,0:T(8,128)} %bitcast.146), custom_call_target="tpu_custom_call" | custom-call | tf_op jit(solution)/shard_map/pallas_call | solution.py:148
  246.4 1.7 multiply_reduce_fusion.4
  248.8 1.0 slice_divide_fusion
  250.5 10.7 %while.21 = (s32[]{:T(128)}, f32[300,300]{0,1:T(8,128)S(1)}, s32[]{:T(128)}) while((s32[]{:T(128)}, f32[300,300]{0,1:T(8,128)S(1)}, s32[]{:T(128)}) %tuple.57), condition=%wide.region_21.22_spmd, body=%wide.region_20.21_spmd.sunk | while | flops 648540032 | bytes 3600045 | solution.py:25
  251.1 0.7 fusion.124
  252.5 0.7 fusion.126
  253.8 0.7 fusion.124
  255.1 0.7 fusion.126
  256.5 0.7 fusion.124
  257.8 0.7 fusion.126
  259.2 0.7 fusion.124
  260.5 0.7 fusion.126
  261.2 1.0 copy.39
  262.2 1.5 copy.38
  263.8 0.7 copy.37
  (57 shorter events, 16.6 us)
Async XLA Ops:
  0.6 1.3 copy-start
  42.0 7.1 %copy-start.5 = (f32[32,32,128]{2,1,0:T(8,128)S(1)}, f32[32,32,128]{2,1,0:T(8,128)}, u32[]{:S(2)}) copy-start(f32[32,32,128]{2,1,0:T(8,128)} %get-tuple-element.35) | copy-start | bytes 1572868
  42.0 8.1 %copy-start.2 = (bf16[1024,300]{0,1:T(8,128)(2,1)S(1)}, bf16[1024,300]{0,1:T(8,128)(2,1)}, u32[]{:S(2)}) copy-start(bf16[1024,300]{0,1:T(8,128)(2,1)} %param.7) | copy-start | bytes 1843204
  50.1 7.4 %copy-start.3 = (f32[1024,300]{1,0:T(8,128)S(1)}, f32[1024,300]{1,0:T(8,128)}, u32[]{:S(2)}) copy-start(f32[1024,300]{1,0:T(8,128)} %fusion.8) | copy-start | bytes 3686404
  147.1 7.2 %copy-start.7 = (f32[8,16,128]{2,1,0:T(8,128)S(1)}, f32[8,16,128]{2,1,0:T(8,128)}, u32[]{:S(2)}) copy-start(f32[8,16,128]{2,1,0:T(8,128)} %get-tuple-element.37) | copy-start | bytes 196612
  154.4 6.0 %copy-start.1 = (f32[2048,300]{0,1:T(8,128)S(1)}, f32[2048,300]{0,1:T(8,128)}, u32[]{:S(2)}) copy-start(f32[2048,300]{0,1:T(8,128)} %get-tuple-element.84) | copy-start | bytes 7372804
  250.5 11.7 %copy-start.4 = (bf16[4,8,64,300]{3,2,1,0:T(8,128)(2,1)S(1)}, bf16[4,8,64,300]{3,2,1,0:T(8,128)(2,1)}, u32[]{:S(2)}) copy-start(bf16[4,8,64,300]{3,2,1,0:T(8,128)(2,1)} %get-tuple-element.40) | copy-start | bytes 3686404
  250.5 13.3 %copy-start.6 = (bf16[128,300]{1,0:T(8,128)(2,1)S(1)}, bf16[128,300]{1,0:T(8,128)(2,1)}, u32[]{:S(2)}) copy-start(bf16[128,300]{1,0:T(8,128)(2,1)} %get-tuple-element.50) | copy-start | bytes 230404

commit v15 on v14

--- a/solution.py
+++ b/solution.py
@@ -265,8 +265,17 @@
         target_part = lax.dot_general(
             col_weights, source, (((0,), (0,)), ((), ())), preferred_element_type=jnp.float32
         )
-        covariance = jnp.dot(source_f32.T, source_part, precision=lax.Precision.HIGH)
-        covariance = covariance + jnp.dot(target_part.T, target_f32, precision=lax.Precision.HIGH)
+        source_hi = source_part.astype(jnp.bfloat16)
+        source_lo = (source_part - source_hi.astype(jnp.float32)).astype(jnp.bfloat16)
+        target_hi = target_part.astype(jnp.bfloat16)
+        target_lo = (target_part - target_hi.astype(jnp.float32)).astype(jnp.bfloat16)
+        down = (((0,), (0,)), ((), ()))
+        covariance = (
+            lax.dot_general(source, source_hi, down, preferred_element_type=jnp.float32)
+            + lax.dot_general(source, source_lo, down, preferred_element_type=jnp.float32)
+            + lax.dot_general(target_hi, target, down, preferred_element_type=jnp.float32)
+            + lax.dot_general(target_lo, target, down, preferred_element_type=jnp.float32)
+        )
         if iteration == ITERS - 1:
             covariance, target_soft, source_soft = all_reduce(covariance, target_part, source_part)
         else:

time: 266 us -> 263 us (0.989)
  matrix products: 64.7 us -> 60.3 us
  local copies, waits for them, and re-layouts: 17.9 us -> 21.6 us
    dot_general x2, matrix products: 13.2 us -> 9.09 us  [body(): lax.dot_general(col_weights, source, (((0,), (0,)), ((), ())), preferred_...]
    dot_general x2, matrix products: 12.2 us -> 9.49 us  [body(): jnp.dot(row_weights, target, preferred_element_type=jnp.float32)]
    dot_general x4 -> x8, matrix products: 5.57 us -> 7.72 us  [the longest x2 2.48 us: body(): lax.dot_general(target_hi, target, down, preferred_element_type=jnp.float32)]
where the time goes in v15:
time: 263 us; the launch traced here: 262 us
  Pallas kernels  162 us (62%)
  matrix products  60.3 us (23%)
  local copies, waits for them, and re-layouts  21.6 us (8%)
  other arithmetic  15.5 us (6%)
    pallas_call x1, Pallas kernels, all_reduce(): pl.pallas_call(functools.partial(all_reduce_kernel, n_src, n_tgt, True),...  79 us
    pallas_call x2, Pallas kernels, gather_stats(): pl.pallas_call(functools.partial(stats_gather_kernel, n_src, n_tgt), out_...  47.5 us
    pallas_call x1, Pallas kernels, all_reduce(): pl.pallas_call(functools.partial(all_reduce_kernel, n_src, n_tgt, False),...  35.4 us
    dot_general x2, matrix products, body(): lax.dot_general(mapped, target, (((1,), (1,)), ((), ())), preferred_eleme...  12.8 us
    dot_general x16, matrix products, newton(): jnp.dot(current, gram_matrix, precision=highest)  11.6 us
    reduce_sum x2, other arithmetic, body(): col_part = jnp.sum(jnp.exp(scores - col_local[None, :]), axis=0)  10.5 us
    dot_general x16, matrix products, newton(): gram_matrix = jnp.dot(current.T, current, precision=highest)  9.55 us
    dot_general x2, matrix products, body(): jnp.dot(row_weights, target, preferred_element_type=jnp.float32)  9.49 us

profile of v15, /device:TPU:2, one launch (start us, length us, event | category | flops | bytes accessed | tf_op | source)
XLA Modules:
  0.0 262.0 jit_solution(3758844594768444159)
XLA Ops:
  0.6 1.3 copy-done
  1.9 7.3 %multiply_reduce_fusion.2 = (f32[2048]{0:T(1024)S(1)}, f32[1024]{0:T(1024)S(1)}, f32[1024,2048]{1,0:T(8,128)}) fusion(bf16[2048,300]{0,1:T(8,128)(2,1)S(1)} %copy-done, bf16[1024,300]{0,1:T(8,128)(2,1)} %param.7, f32[300,300]{1,0:T(8,128)} %param.9), kind=kOutput, calls=%fused_computation.20 | convolution fusion | flops 1449296768 | bytes 10604096 | tf_op jit(solution)/shard_map/dot_general | solution.py:252
  9.2 5.2 %exponential_reduce_fusion.2 = (f32[2048]{0:T(1024)S(1)}, f32[1024]{0:T(1024)S(1)}) fusion(f32[1024,2048]{1,0:T(8,128)} %get-tuple-element.81, f32[2048]{0:T(1024)S(1)} %get-tuple-element.59, f32[1024]{0:T(1024)S(1)} %get-tuple-element.60), kind=kLoop, calls=%fused_computation.16 | loop fusion | flops 10482688 | bytes 8413184 | tf_op jit(solution)/shard_map/reduce_sum | solution.py:260
  15.8 25.3 %shard_map.58 = (f32[8,16,128]{2,1,0:T(8,128)}, f32[32,32,128]{2,1,0:T(8,128)}) custom-call(f32[16,128]{1,0:T(8,128)} %reshape.77.row_ref, f32[32,128]{1,0:T(8,128)} %reshape.78.col_ref), custom_call_target="tpu_custom_call" | custom-call | tf_op jit(solution)/shard_map/pallas_call | solution.py:222
  41.1 1.3 reshape.80
  43.1 4.5 %fusion.6 = f32[2048,300]{0,1:T(8,128)S(1)} fusion(bf16[1024,300]{0,1:T(8,128)(2,1)S(1)} %copy-done.1, f32[1024,2048]{1,0:T(8,128)} %get-tuple-element.81, f32[2048]{0:T(1024)S(1)} %fusion.36, f32[2048]{0:T(1024)S(1)} %get-tuple-element.72), kind=kOutput, calls=%fused_computation.22 | convolution fusion | flops 1266679808 | bytes 11476992 | tf_op jit(solution)/shard_map/dot_general | solution.py:265
  47.7 0.8 fusion.12
  48.5 0.8 fusion.21
  49.5 4.7 %fusion.8 = f32[1024,300]{0,1:T(8,128)S(1)} fusion(bf16[2048,300]{0,1:T(8,128)(2,1)S(1)} %copy-done, f32[1024,2048]{1,0:T(8,128)} %get-tuple-element.81, f32[1024]{0:T(1024)S(1)} %fusion.48, f32[1024]{0:T(1024)S(1)} %get-tuple-element.78), kind=kOutput, calls=%fused_computation.24 | convolution fusion | flops 1266679808 | bytes 10854400 | tf_op jit(solution)/shard_map/dot_general | solution.py:264
  55.9 0.8 pad.7
  56.7 35.4 %shard_map.59 = f32[32,24,128]{2,1,0:T(8,128)} custom-call(f32[32,24,128]{2,1,0:T(8,128)} %bitcast.157), custom_call_target="tpu_custom_call" | custom-call | tf_op jit(solution)/shard_map/pallas_call | solution.py:132
  92.2 1.7 multiply_reduce_fusion.5
  94.5 1.0 slice_divide_fusion.1
  96.2 10.7 %while.20 = (s32[]{:T(128)}, f32[300,300]{0,1:T(8,128)S(1)}, s32[]{:T(128)}) while((s32[]{:T(128)}, f32[300,300]{0,1:T(8,128)S(1)}, s32[]{:T(128)}) %tuple.54), condition=%wide.region_10.11_spmd, body=%wide.region_9.10_spmd.sunk | while | flops 648540032 | bytes 3600045 | solution.py:25
  96.8 0.7 fusion.129
  98.2 0.7 fusion.131
  99.5 0.7 fusion.129
  100.9 0.7 fusion.131
  102.2 0.7 fusion.129
  103.6 0.7 fusion.131
  104.9 0.7 fusion.129
  106.2 0.7 fusion.131
  107.0 5.5 %multiply_reduce_fusion = (f32[2048]{0:T(1024)S(1)}, f32[1024]{0:T(1024)S(1)}, f32[1024,2048]{1,0:T(8,128)}) fusion(bf16[2048,300]{0,1:T(8,128)(2,1)S(1)} %copy-done, bf16[1024,300]{0,1:T(8,128)(2,1)S(1)} %copy-done.1, f32[300,300]{0,1:T(8,128)S(1)} %get-tuple-element.36), kind=kOutput, calls=%fused_computation.18 | convolution fusion | flops 1449296768 | bytes 10604096 | tf_op jit(solution)/shard_map/dot_general | solution.py:252
  112.5 5.3 %exponential_reduce_fusion = (f32[2048]{0:T(1024)S(1)}, f32[1024]{0:T(1024)S(1)}) fusion(f32[1024,2048]{1,0:T(8,128)} %get-tuple-element.82, f32[2048]{0:T(1024)S(1)} %get-tuple-element.55, f32[1024]{0:T(1024)S(1)} %get-tuple-element.56), kind=kLoop, calls=%fused_computation.12 | loop fusion | flops 10482688 | bytes 8413184 | tf_op jit(solution)/shard_map/reduce_sum | solution.py:260
  119.0 22.2 %shard_map.60 = (f32[8,16,128]{2,1,0:T(8,128)}, f32[32,32,128]{2,1,0:T(8,128)}) custom-call(f32[16,128]{1,0:T(8,128)} %reshape.84.row_ref, f32[32,128]{1,0:T(8,128)} %reshape.85.col_ref), custom_call_target="tpu_custom_call" | custom-call | tf_op jit(solution)/shard_map/pallas_call | solution.py:222
  141.2 1.3 reshape.87
  143.2 4.5 %fusion.57 = (bf16[2048,300]{0,1:T(8,128)(2,1)S(1)}, f32[2048,300]{0,1:T(8,128)S(1)}) fusion(bf16[1024,300]{0,1:T(8,128)(2,1)S(1)} %copy-done.1, f32[1024,2048]{1,0:T(8,128)} %get-tuple-element.82, f32[2048]{0:T(1024)S(1)} %fusion.32, f32[2048]{0:T(1024)S(1)} %get-tuple-element.69), kind=kOutput, calls=%fused_computation.91 | convolution fusion | flops 1267294208 | bytes 12705792 | tf_op jit(solution)/shard_map/dot_general | solution.py:265
  147.7 1.6 fusion.13
  149.4 1.7 fusion.62
  151.2 4.7 %fusion.9 = f32[1024,300]{0,1:T(8,128)S(1)} fusion(bf16[2048,300]{0,1:T(8,128)(2,1)S(1)} %copy-done, f32[1024,2048]{1,0:T(8,128)} %get-tuple-element.82, f32[1024]{0:T(1024)S(1)} %fusion.44, f32[1024]{0:T(1024)S(1)} %get-tuple-element.75), kind=kOutput, calls=%fused_computation.25 | convolution fusion | flops 1266679808 | bytes 10854400 | tf_op jit(solution)/shard_map/dot_general | solution.py:264
  157.1 1.3 fusion.19
  158.4 1.2 copy.37
  160.1 0.8 pad.8
  160.8 2.5 copy.38
  163.4 1.6 copy.39
  165.0 79.0 %shard_map.61 = (f32[32,24,128]{2,1,0:T(8,128)}, bf16[4,8,64,300]{3,2,1,0:T(8,128)(2,1)}, bf16[128,300]{1,0:T(8,128)(2,1)}) custom-call(f32[32,24,128]{2,1,0:T(8,128)} %bitcast.156, bf16[4,8,64,300]{3,2,1,0:T(8,128)(2,1)} %bitcast.152, f32[8,128,300]{2,1,0:T(8,128)} %bitcast.153), custom_call_target="tpu_custom_call" | custom-call | tf_op jit(solution)/shard_map/pallas_call | solution.py:148
  244.0 1.7 copy.41
  245.7 2.5 copy.42
  250.2 10.8 %while.21 = (s32[]{:T(128)}, f32[300,300]{0,1:T(8,128)S(1)}, s32[]{:T(128)}) while((s32[]{:T(128)}, f32[300,300]{0,1:T(8,128)S(1)}, s32[]{:T(128)}) %tuple.57), condition=%wide.region_21.22_spmd, body=%wide.region_20.21_spmd.sunk | while | flops 648540032 | bytes 3600045 | solution.py:25
  250.8 0.7 fusion.141
  252.2 0.7 fusion.143
  253.5 0.7 fusion.141
  254.9 0.7 fusion.143
  256.2 0.7 fusion.141
  257.6 0.7 fusion.143
  258.9 0.7 fusion.141
  260.3 0.7 fusion.143
  261.0 1.0 copy.43
  (61 shorter events, 19.0 us)
Async XLA Ops:
  0.6 1.3 copy-start
  14.5 28.6 %copy-start.1 = (bf16[1024,300]{0,1:T(8,128)(2,1)S(1)}, bf16[1024,300]{0,1:T(8,128)(2,1)}, u32[]{:S(2)}) copy-start(bf16[1024,300]{0,1:T(8,128)(2,1)} %param.7) | copy-start | bytes 1843204
  48.5 0.8 copy-start.7
  147.7 1.6 copy-start.2
  149.3 1.7 copy-start.6
  155.9 1.0 copy-start.3
  155.9 1.2 copy-start.5
  244.0 4.2 %copy-start.4 = (f32[32,24,128]{2,1,0:T(8,128)S(1)}, f32[32,24,128]{2,1,0:T(8,128)}, u32[]{:S(2)}) copy-start(f32[32,24,128]{2,1,0:T(8,128)} %get-tuple-element.41) | copy-start | bytes 1179652
